TPU v7x, 512 devices: a whole 4x4x16 slice. The times are simulated.
512 devices in a mesh: neuron: 128 (over z, y, core), trial: 4 (over x).
Axes of the slice: x: 4, y: 4, z: 16, core: 2. Of those that a mesh axis runs over, the one named last changes fastest.
Arguments:
- tensor: bfloat16 [8, 16384, 1024], P('trial', 'neuron'), may hold values from -1000 to 1000
- time_init: float32 [32, 1024], replicated, may hold values from -6 to 6
- trial_init: float32 [32, 8], P(None, 'trial'), may hold values from -6 to 6
Outputs:
- neuron_factor: float32 [32, 16384], P(None, 'neuron')
- time_factor: float32 [32, 1024], P(None, ('neuron', 'trial'))
- trial_factor: float32 [32, 8], P(None, 'trial')
All inputs are finite; a program needn't handle non-finite values.
Results may differ from a plain program's by a relative error of at most 0.011.
Values may be sent and summed in bfloat16 or wider, within the bound.
No kernel may reach another device: no remote copies, remote signals or barrier semaphores. Data moves between devices by JAX's collectives and lax.ppermute only.
A program may use at most 64 MiB of HBM per device.

v0:
```python
import jax
import jax.numpy as jnp
from jax import lax
from jax.sharding import PartitionSpec as P

SWEEPS = 2


ridge_share = 0.1
tiny_eps = 1e-06


def gram_of(matrix):
    return lax.dot_general(
        matrix,
        matrix,
        (((1,), (1,)), ((), ())),
        precision=lax.Precision.HIGHEST,
        preferred_element_type=jnp.float32,
    )


def damped_solve(gram_mat, right_hand):
    order_size = gram_mat.shape[0]
    identity_mat = jnp.eye(order_size, dtype=jnp.float32)
    damped = gram_mat + ridge_share * (jnp.trace(gram_mat) / order_size) * identity_mat
    cholesky_low = jnp.linalg.cholesky(damped)
    return jax.scipy.linalg.cho_solve((cholesky_low, True), right_hand)


def per_device(tensor, time_init, trial_init):
    timepoints = tensor.shape[2]
    component_count = time_init.shape[0]
    neuron_count = tensor.shape[1] * lax.axis_size("neuron")
    devices = lax.axis_size("neuron") * lax.axis_size("trial")
    share_width = timepoints // devices
    position = lax.axis_index(("neuron", "trial"))

    def trial_gram_of(trial_cols):
        return gram_of(lax.all_gather(trial_cols, "trial", axis=1, tiled=True))

    trial_now = trial_init
    trial_gram = trial_gram_of(trial_now)
    time_gram = gram_of(time_init)
    time_rounded = time_init.astype(jnp.bfloat16)
    time_out = lax.dynamic_slice_in_dim(time_init, position * share_width, share_width, 1)
    neuron_now = jnp.zeros((component_count, tensor.shape[1]), jnp.float32)
    for sweep_index in range(SWEEPS):
        projected = jnp.einsum(
            "rj,kij->kri", time_rounded, tensor, preferred_element_type=jnp.float32
        )
        local_terms = jnp.sum(trial_now.T[:, :, None] * projected, axis=0)
        neuron_terms = lax.psum(local_terms, "trial")
        neuron_raw = damped_solve(trial_gram * time_gram, neuron_terms)
        squares = lax.psum(jnp.sum(neuron_raw * neuron_raw, axis=1), "neuron")
        scaling = 1.0 / jnp.sqrt(squares / neuron_count + tiny_eps)
        neuron_now = neuron_raw * scaling[:, None]
        neuron_gram, trial_terms = lax.psum(
            (gram_of(neuron_now), jnp.sum(neuron_now[None] * projected, axis=2).T), "neuron"
        )
        trial_now = damped_solve(neuron_gram * time_gram, trial_terms)
        trial_gram = trial_gram_of(trial_now)
        weights = (neuron_now[None] * trial_now.T[:, :, None]).astype(jnp.bfloat16)
        time_local = jnp.einsum("kri,kij->rj", weights, tensor, preferred_element_type=jnp.float32)
        time_system = neuron_gram * trial_gram
        time_terms = lax.psum(time_local, ("neuron", "trial"))
        time_raw = damped_solve(time_system, time_terms)
        time_now = time_raw / jnp.sqrt(
            jnp.mean(time_raw * time_raw, axis=1, keepdims=True) + tiny_eps
        )
        time_gram = gram_of(time_now)
        time_rounded = time_now.astype(jnp.bfloat16)
        time_out = lax.dynamic_slice_in_dim(time_now, position * share_width, share_width, 1)
    return (neuron_now, time_out, trial_now)


def solution(mesh):
    placed = (P("trial", "neuron", None), P(), P(None, "trial"))
    return jax.shard_map(
        per_device,
        mesh=mesh,
        in_specs=placed,
        out_specs=(P(None, "neuron"), P(None, ("neuron", "trial")), P(None, "trial")),
        check_vma=False,
    )
```

profile of v0, /device:TPU:1, one launch (start us, length us, event | category | flops | bytes accessed | tf_op | source)
XLA Modules:
  0.0 2487.0 jit_solution(9856906988820335533)
XLA Ops:
  7.2 1.3 fusion.51
  8.5 8.7 all-gather
  17.2 0.8 select_reduce_fusion.8
  18.8 2.9 cholesky.104
  21.7 0.6 compare_reduce_fusion.5
  22.4 0.7 fusion.5
  23.0 2.4 custom-call.20
  25.5 0.3 multiply_reduce_fusion.5
  25.8 11.0 psum.70
  36.8 0.2 fusion.38
  37.0 0.3 multiply_reduce_fusion.7
  37.3 259.1 %psum.71 = f32[32]{0:T(128)S(1)} all-reduce(f32[32]{0:T(128)S(1)} %get-tuple-element.29), channel_id=1, replica_groups=mesh['neuron'=128,'trial'=4] {'neuron'}, use_global_device_ids=true, to_apply=%region_6.9 | all-reduce | flops 32 | bytes 256 | tf_op jit(solution)/shard_map/psum | solution.py:55
  296.4 0.2 fusion.52
  296.6 0.1 multiply_reduce_fusion.4
  296.7 485.7 %all-reduce.1 = (f32[32,2]{0,1:T(2,128)S(1)}, f32[32,32]{0,1:T(8,128)S(1)}) all-reduce(f32[32,2]{0,1:T(2,128)S(1)} %bitcast.141, f32[32,32]{0,1:T(8,128)S(1)} %fusion.52), channel_id=1, replica_groups=mesh['neuron'=128,'trial'=4] {'neuron'}, use_global_device_ids=true, to_apply=%region_10.13 | all-reduce | flops 1088 | bytes 8704 | tf_op jit(solution)/shard_map/psum | solution.py:58
  782.4 0.6 select_reduce_fusion.7
  783.8 2.9 cholesky.115
  786.7 0.6 compare_reduce_fusion.4
  787.3 0.7 fusion.6
  788.0 2.4 custom-call.21
  790.4 0.2 fusion.33
  790.7 0.2 fusion.31
  790.9 0.9 convolution_bitcast_fusion.1
  791.9 6.2 all-gather.1
  798.1 0.8 select_reduce_fusion.6
  799.7 2.9 cholesky.126
  802.6 0.6 compare_reduce_fusion.3
  803.3 0.7 fusion.7
  803.9 2.4 custom-call.22
  806.4 440.6 %all-reduce.5.cloned.1.call-done = f32[32,1024]{1,0:T(8,128)} async-done(((f32[32,1024]{1,0:T(8,128)}), f32[32,1024]{1,0:T(8,128)}) %all-reduce.5.cloned.1.call-update) | async-done | bytes 131088 | tf_op jit(solution)/shard_map/psum | solution.py:66
  1246.9 1.2 fusion.28
  1248.2 0.4 multiply_reduce_fusion.1
  1248.5 0.3 multiply_reduce_fusion.3
  1248.8 1.0 select_reduce_fusion.5
  1250.5 2.9 cholesky.137
  1253.5 0.6 compare_reduce_fusion.2
  1254.1 0.7 fusion.8
  1254.8 2.4 custom-call.23
  1257.2 12.2 psum.75
  1269.4 0.2 fusion.23
  1269.6 0.3 multiply_reduce_fusion.6
  1269.8 249.2 %psum.76 = f32[32]{0:T(128)S(1)} all-reduce(f32[32]{0:T(128)S(1)} %get-tuple-element.37), channel_id=1, replica_groups=mesh['neuron'=128,'trial'=4] {'neuron'}, use_global_device_ids=true, to_apply=%region_18.23 | all-reduce | flops 32 | bytes 256 | tf_op jit(solution)/shard_map/psum | solution.py:55
  1519.1 0.1 fusion.53
  1519.2 0.1 multiply_reduce_fusion.2
  1519.3 485.9 %all-reduce = (f32[32,2]{0,1:T(2,128)S(1)}, f32[32,32]{0,1:T(8,128)S(1)}) all-reduce(f32[32,2]{0,1:T(2,128)S(1)} %bitcast.142, f32[32,32]{0,1:T(8,128)S(1)} %fusion.53), channel_id=1, replica_groups=mesh['neuron'=128,'trial'=4] {'neuron'}, use_global_device_ids=true, to_apply=%region_22.27 | all-reduce | flops 1088 | bytes 8704 | tf_op jit(solution)/shard_map/psum | solution.py:58
  2005.2 0.6 select_reduce_fusion.4
  2006.6 2.9 cholesky.148
  2009.5 0.6 compare_reduce_fusion.1
  2010.2 0.7 fusion.9
  2010.8 2.4 custom-call.24
  2013.3 0.2 fusion.18
  2013.5 0.2 fusion.16
  2013.7 5.3 all-gather.2
  2019.0 0.8 select_reduce_fusion.3
  2020.5 2.9 cholesky.159
  2023.5 0.6 compare_reduce_fusion
  2024.1 0.9 convolution_bitcast_fusion
  2025.0 0.7 fusion.10
  2025.7 2.4 custom-call.25
  2028.1 449.7 %all-reduce.7.cloned.1.call-done = f32[32,1024]{1,0:T(8,128)} async-done(((f32[32,1024]{1,0:T(8,128)}), f32[32,1024]{1,0:T(8,128)}) %all-reduce.7.cloned.1.call-update) | async-done | bytes 131088 | tf_op jit(solution)/shard_map/psum | solution.py:66
  2477.9 1.2 fusion.13
  2479.1 0.4 multiply_reduce_fusion
  2479.5 0.1 dynamic-slice_divide_fusion
  2479.6 0.6 copy.39
  (44 shorter events, 1.1 us)
Async XLA Ops:
  7.2 18.3 copy-start
  7.2 1239.8 %all-reduce.5.cloned.1.call-start = ((), (), s32[]{:S(2)}) async-start(), calls=%async_computation | async-start | bytes 262144 | tf_op jit(solution)/shard_map/psum | solution.py:66
  7.2 1.3 copy-start.4
  8.5 16.9 copy-start.1
  791.8 1686.1 %all-reduce.7.cloned.1.call-start = ((), (), s32[]{:S(2)}) async-start(), calls=%async_computation.1 | async-start | bytes 262144 | tf_op jit(solution)/shard_map/psum | solution.py:66
  1519.1 505.0 %copy-start.2 = (f32[32,128]{1,0:T(8,128)}, f32[32,128]{1,0:T(8,128)S(1)}, u32[]{:S(2)}) copy-start(f32[32,128]{1,0:T(8,128)S(1)} %broadcast_multiply_fusion) | copy-start | bytes 49156
  2013.7 10.4 copy-start.3
Sparse Core Ops, SparseCore 0:
  791.9 454.9 all-reduce.4
  2025.2 452.6 all-reduce.6
where the time goes:
time: 2490 us
  blocking collectives  1520 us (61%)
  waiting for transfers between devices  890 us (36%)
  other arithmetic  41.8 us (2%)
    psum x2, blocking collectives, per_device(): lax.psum((gram_of(neuron_now), jnp.sum(neuron_now[None] * projected, axis...  972 us
    psum x2, waiting for transfers between devices, per_device(): time_terms = lax.psum(time_local, ('neuron', 'trial'))  890 us
    psum x2, blocking collectives, per_device(): squares = lax.psum(jnp.sum(neuron_raw * neuron_raw, axis=1), 'neuron')  508 us
  transfers between devices with their start and end apart: 2, of which 2 were waited for; matrix products, arithmetic and copies ran while one was open for 0% of the time, Pallas kernels for 0%

commit v1 on v0

v1 whole, which is shorter than its diff:
```python
import jax
import jax.numpy as jnp
from jax import lax
from jax.sharding import PartitionSpec as P

SWEEPS = 2


ridge_share = 0.1
tiny_eps = 1e-06
EXACT = lax.Precision.HIGHEST


def gram_of(matrix):
    return lax.dot_general(
        matrix,
        matrix,
        (((1,), (1,)), ((), ())),
        precision=EXACT,
        preferred_element_type=jnp.float32,
    )


def damped_solve(gram_mat, right_hand):
    order_size = gram_mat.shape[0]
    identity_mat = jnp.eye(order_size, dtype=jnp.float32)
    damped = gram_mat + ridge_share * (jnp.trace(gram_mat) / order_size) * identity_mat
    cholesky_low = jnp.linalg.cholesky(damped)
    return jax.scipy.linalg.cho_solve((cholesky_low, True), right_hand)


def to_rows(*pieces):
    flat = jnp.concatenate([piece.reshape(-1) for piece in pieces])
    spare = -flat.shape[0] % 128
    return jnp.pad(flat, (0, spare)).reshape(-1, 128)


def from_rows(rows, *shapes):
    flat = rows.reshape(rows.shape[0], -1)
    taken, start = [], 0
    for shape in shapes:
        size = 1
        for extent in shape:
            size *= extent
        taken.append(flat[:, start : start + size].reshape((rows.shape[0],) + shape))
        start += size
    return taken


def share_all(rows, axis):
    members = lax.axis_size(axis)
    return lax.all_to_all(jnp.broadcast_to(rows[None], (members,) + rows.shape), axis, 0, 0)


def per_device(tensor, time_init, trial_init):
    own_trials, own_neurons, timepoints = tensor.shape
    components = time_init.shape[0]
    blocks, planes = lax.axis_size("neuron"), lax.axis_size("trial")
    neuron_count = own_neurons * blocks
    trial_count = own_trials * planes
    width = timepoints // blocks
    plane = lax.axis_index("trial")
    gram_rows = components // planes

    time_now = time_init
    trial_now = None
    for sweep_index in range(SWEEPS):
        time_gram = gram_of(time_now)
        projected = jnp.einsum(
            "rj,kij->kri",
            time_now.astype(jnp.bfloat16),
            tensor,
            preferred_element_type=jnp.float32,
        )
        if trial_now is None:
            own_trial = trial_init
        else:
            own_trial = lax.dynamic_slice_in_dim(trial_now, plane * own_trials, own_trials, 1)
        local_terms = jnp.sum(own_trial.T[:, :, None] * projected, axis=0)
        if trial_now is None:
            shared = share_all(
                jnp.concatenate([local_terms, to_rows(trial_init)], axis=0), "trial"
            )
            neuron_terms = jnp.sum(shared[:, :components], axis=0)
            (columns,) = from_rows(shared[:, components:], (components, own_trials))
            trial_now = columns.transpose(1, 0, 2).reshape(components, trial_count)
        else:
            neuron_terms = jnp.sum(share_all(local_terms, "trial"), axis=0)
        raw = damped_solve(gram_of(trial_now) * time_gram, neuron_terms)

        own_rows = lax.dynamic_slice_in_dim(raw, plane * gram_rows, gram_rows, 0)
        gram_part = lax.dot_general(
            own_rows, raw, (((1,), (1,)), ((), ())),
            precision=EXACT, preferred_element_type=jnp.float32,
        )
        terms_part = jnp.sum(raw[None] * projected, axis=2)
        partial = jnp.einsum(
            "ri,kij->krj", raw.astype(jnp.bfloat16), tensor, preferred_element_type=jnp.float32
        )
        chunks = partial.reshape(own_trials * components, width, blocks)
        chunks = chunks.transpose(2, 1, 0).reshape(blocks, -1, 128)
        small = to_rows(gram_part, terms_part)
        small_hi = small.astype(jnp.bfloat16)
        small_lo = (small - small_hi.astype(jnp.float32)).astype(jnp.bfloat16)
        small = jnp.concatenate([small_hi, small_lo], axis=0)
        sent = jnp.concatenate(
            [
                chunks.astype(jnp.bfloat16),
                jnp.broadcast_to(small[None], (blocks,) + small.shape),
            ],
            axis=1,
        )
        got = lax.all_to_all(sent, "neuron", 0, 0).astype(jnp.float32)
        summed = jnp.sum(got, axis=0)
        chunk_rows = chunks.shape[1]
        small_rows = small_hi.shape[0]
        merged = jnp.concatenate(
            [
                summed[:chunk_rows],
                summed[chunk_rows : chunk_rows + small_rows] + summed[chunk_rows + small_rows :],
            ],
            axis=0,
        )
        shared = share_all(merged, "trial")
        columns, gram_all, terms_all = from_rows(
            shared,
            (width, own_trials, components),
            (gram_rows, components),
            (own_trials, components),
        )
        raw_gram = gram_all.reshape(components, components)
        scaling = 1.0 / jnp.sqrt(jnp.diagonal(raw_gram) / neuron_count + tiny_eps)
        neuron_now = raw * scaling[:, None]
        neuron_gram = scaling[:, None] * raw_gram * scaling[None, :]
        trial_terms = terms_all.reshape(trial_count, components).T * scaling[:, None]
        trial_now = damped_solve(neuron_gram * time_gram, trial_terms)
        trial_gram = gram_of(trial_now)
        weighted = columns * trial_now.T.reshape(planes, 1, own_trials, components)
        time_terms = jnp.sum(weighted, axis=(0, 2)).T * scaling[:, None]
        time_part = damped_solve(neuron_gram * trial_gram, time_terms)
        gathered = share_all(to_rows(time_part.T), "neuron")
        (gathered,) = from_rows(gathered, (width, components))
        time_raw = gathered.transpose(2, 1, 0).reshape(components, timepoints)
        time_now = time_raw / jnp.sqrt(
            jnp.mean(time_raw * time_raw, axis=1, keepdims=True) + tiny_eps
        )
    position = lax.axis_index(("neuron", "trial"))
    share_width = timepoints // (blocks * planes)
    time_out = lax.dynamic_slice_in_dim(time_now, position * share_width, share_width, 1)
    trial_out = lax.dynamic_slice_in_dim(trial_now, plane * own_trials, own_trials, 1)
    return (neuron_now, time_out, trial_out)


def solution(mesh):
    placed = (P("trial", "neuron", None), P(), P(None, "trial"))
    return jax.shard_map(
        per_device,
        mesh=mesh,
        in_specs=placed,
        out_specs=(P(None, "neuron"), P(None, ("neuron", "trial")), P(None, "trial")),
        check_vma=False,
    )
```

time: 2490 us -> 237 us (0.10)
  blocking collectives: 1520 us -> 97 us
  waiting for transfers between devices: 890 us -> 40.5 us
  starting transfers between devices: 0.08 us -> 32.1 us
    psum x6 -> x0, blocking collectives: 1500 us -> none  [the longest x2 972 us: per_device(): lax.psum((gram_of(neuron_now), jnp.sum(neuron_now[None] * projected, axis...]
    psum x2 -> x0, waiting for transfers between devices: 890 us -> none  [per_device(): time_terms = lax.psum(time_local, ('neuron', 'trial'))]
    all_to_all x0 -> x3, blocking collectives: none -> 97 us  [the longest x2 90.5 us: per_device(): got = lax.all_to_all(sent, 'neuron', 0, 0).astype(jnp.float32)]
    all_to_all x0 -> x5, waiting for transfers between devices: none -> 40.5 us  [share_all(): lax.all_to_all(jnp.broadcast_to(rows[None], (members,) + rows.shape), axi...]
    all_to_all x0 -> x5, starting transfers between devices: none -> 32.1 us  [share_all(): lax.all_to_all(jnp.broadcast_to(rows[None], (members,) + rows.shape), axi...]
  transfers between devices with their start and end apart: 2 -> 5, of which waited for: 2 -> 5; matrix products, arithmetic and copies ran while one was open for 0% -> 2% of each run, Pallas kernels for 0% -> 0%
where the time goes in v1:
time: 237 us; the launch traced here: 236 us
  blocking collectives  97 us (41%)
  other arithmetic  43.7 us (18%)
  waiting for transfers between devices  40.5 us (17%)
  starting transfers between devices  32.1 us (14%)
  local copies, waits for them, and re-layouts  10.3 us (4%)
  matrix products  7.62 us (3%)
  between operations  5.06 us (2%)
    all_to_all x2, blocking collectives, per_device(): got = lax.all_to_all(sent, 'neuron', 0, 0).astype(jnp.float32)  90.5 us
    all_to_all x5, waiting for transfers between devices, share_all(): lax.all_to_all(jnp.broadcast_to(rows[None], (members,) + rows.shape), axi...  40.5 us
    all_to_all x5, starting transfers between devices, share_all(): lax.all_to_all(jnp.broadcast_to(rows[None], (members,) + rows.shape), axi...  32.1 us
    another operation x18, other arithmetic, damped_solve(): cholesky_low = jnp.linalg.cholesky(damped)  21.6 us
    another operation x12, other arithmetic, damped_solve(): return jax.scipy.linalg.cho_solve((cholesky_low, True), right_hand)  18.5 us
    all_to_all x1, blocking collectives, share_all(): lax.all_to_all(jnp.broadcast_to(rows[None], (members,) + rows.shape), axi...  6.56 us
  transfers between devices with their start and end apart: 5, of which 5 were waited for; matrix products, arithmetic and copies ran while one was open for 2% of the time, Pallas kernels for 0%

profile of v1, /device:TPU:1, one launch (start us, length us, event | category | flops | bytes accessed | tf_op | source)
XLA Modules:
  0.0 236.4 jit_solution(9240566224281867585)
XLA Ops:
  0.6 0.8 copy.245
  1.7 0.6 copy-done.2
  2.3 1.2 multiply_reduce_fusion.5
  3.5 0.6 broadcast_in_dim.36
  4.1 4.8 %all-to-all-start = ((f32[4,33,128]{2,1,0:T(8,128)}), f32[4,33,128]{2,1,0:T(8,128)S(1)}, u32[]{:S(2)}, u32[]{:S(2)}) async-start(f32[4,33,128]{2,1,0:T(8,128)} %broadcast_in_dim.36), calls=%async_computation | async-start | bytes 163840 | tf_op jit(solution)/shard_map/all_to_all | solution.py:52
  9.0 0.3 fusion.81
  9.2 4.3 %all-to-all-done = f32[4,33,128]{2,1,0:T(8,128)S(1)} async-done(((f32[4,33,128]{2,1,0:T(8,128)}), f32[4,33,128]{2,1,0:T(8,128)S(1)}, u32[]{:S(2)}, u32[]{:S(2)}) %all-to-all-start) | async-done | bytes 67616 | tf_op jit(solution)/shard_map/all_to_all | solution.py:52
  13.7 0.8 select_reduce_fusion.8
  15.3 2.9 %cholesky.104 = f32[32,32]{1,0:T(8,128)S(1)} custom-call(f32[32,32]{1,0:T(8,128)S(1)} %fusion.41), custom_call_target="Cholesky" | custom-call | tf_op jit(solution)/shard_map/jit(cholesky)/cholesky | solution.py:28
  18.2 0.6 compare_reduce_fusion.5
  18.9 0.7 fusion.8
  19.5 2.4 %custom-call.20 = f32[1,32,32]{1,2,0:T(8,128)S(1)} custom-call(f32[1,32,32]{2,1,0:T(8,128)S(1)} %fusion.8), custom_call_target="InvertDiagBlocksLowerTriangular" | custom-call | tf_op jit(solution)/shard_map/jit(_cho_solve)/triangular_solve | solution.py:29
  22.0 0.2 fusion.39
  22.8 0.2 convolution_convert_fusion.1
  23.3 0.2 pad_maximum_fusion
  23.5 51.6 %all_to_all.40 = bf16[128,10,128]{2,1,0:T(8,128)(2,1)S(1)} all-to-all(bf16[128,10,128]{2,1,0:T(8,128)(2,1)S(1)} %pad_maximum_fusion), channel_id=1, replica_groups=mesh['neuron'=128,'trial'=4] {'neuron'}, dimensions={0} | all-to-all | bytes 655360 | tf_op jit(solution)/shard_map/all_to_all | solution.py:113
  75.2 0.6 broadcast_in_dim.39
  75.9 3.3 %all-to-all-start.2 = ((f32[4,7,128]{2,1,0:T(8,128)}), f32[4,7,128]{2,1,0:T(8,128)S(1)}, u32[]{:S(2)}, u32[]{:S(2)}) async-start(f32[4,7,128]{2,1,0:T(8,128)} %broadcast_in_dim.39), calls=%async_computation.2 | async-start | bytes 32768 | tf_op jit(solution)/shard_map/all_to_all | solution.py:52
  79.1 4.2 %all-to-all-done.2 = f32[4,7,128]{2,1,0:T(8,128)S(1)} async-done(((f32[4,7,128]{2,1,0:T(8,128)}), f32[4,7,128]{2,1,0:T(8,128)S(1)}, u32[]{:S(2)}, u32[]{:S(2)}) %all-to-all-start.2) | async-done | bytes 14368 | tf_op jit(solution)/shard_map/all_to_all | solution.py:52
  83.5 0.7 gather_fusion
  84.3 0.7 select_reduce_fusion.7
  85.8 2.9 %cholesky.115 = f32[32,32]{1,0:T(8,128)S(1)} custom-call(f32[32,32]{1,0:T(8,128)S(1)} %fusion.36), custom_call_target="Cholesky" | custom-call | tf_op jit(solution)/shard_map/jit(cholesky)/cholesky | solution.py:28
  88.7 0.6 compare_reduce_fusion.4
  89.4 0.7 fusion.9
  90.0 2.4 %custom-call.21 = f32[1,32,32]{1,2,0:T(8,128)S(1)} custom-call(f32[1,32,32]{2,1,0:T(8,128)S(1)} %fusion.9), custom_call_target="InvertDiagBlocksLowerTriangular" | custom-call | tf_op jit(solution)/shard_map/jit(_cho_solve)/triangular_solve | solution.py:29
  92.7 0.8 select_reduce_fusion.6
  94.4 2.9 %cholesky.126 = f32[32,32]{1,0:T(8,128)S(1)} custom-call(f32[32,32]{1,0:T(8,128)S(1)} %fusion.31), custom_call_target="Cholesky" | custom-call | tf_op jit(solution)/shard_map/jit(cholesky)/cholesky | solution.py:28
  97.3 0.6 compare_reduce_fusion.3
  98.0 0.7 fusion.10
  98.7 2.4 %custom-call.22 = f32[1,32,32]{1,2,0:T(8,128)S(1)} custom-call(f32[1,32,32]{2,1,0:T(8,128)S(1)} %fusion.10), custom_call_target="InvertDiagBlocksLowerTriangular" | custom-call | tf_op jit(solution)/shard_map/jit(_cho_solve)/triangular_solve | solution.py:29
  101.7 0.7 broadcast_in_dim.41
  102.4 10.4 %all-to-all-start.3 = ((f32[128,2,128]{2,1,0:T(2,128)}), f32[128,2,128]{2,1,0:T(2,128)S(1)}, u32[]{:S(2)}, u32[]{:S(2)}) async-start(f32[128,2,128]{2,1,0:T(2,128)} %broadcast_in_dim.41), calls=%async_computation.3 | async-start | bytes 262144 | tf_op jit(solution)/shard_map/all_to_all | solution.py:52
  112.8 16.0 %all-to-all-done.3 = f32[128,2,128]{2,1,0:T(2,128)S(1)} async-done(((f32[128,2,128]{2,1,0:T(2,128)}), f32[128,2,128]{2,1,0:T(2,128)S(1)}, u32[]{:S(2)}, u32[]{:S(2)}) %all-to-all-start.3) | async-done | bytes 131104 | tf_op jit(solution)/shard_map/all_to_all | solution.py:52
  129.0 0.9 select_reduce_fusion.5
  130.7 2.9 %cholesky.137 = f32[32,32]{1,0:T(8,128)S(1)} custom-call(f32[32,32]{1,0:T(8,128)S(1)} %fusion.27), custom_call_target="Cholesky" | custom-call | tf_op jit(solution)/shard_map/jit(cholesky)/cholesky | solution.py:28
  133.7 0.6 compare_reduce_fusion.2
  134.3 0.3 multiply_reduce_fusion.3
  134.6 0.7 broadcast_in_dim.42
  135.2 3.3 %all-to-all-start.4 = ((f32[4,32,128]{2,1,0:T(8,128)}), f32[4,32,128]{2,1,0:T(8,128)S(1)}, u32[]{:S(2)}, u32[]{:S(2)}) async-start(f32[4,32,128]{2,1,0:T(8,128)} %broadcast_in_dim.42), calls=%async_computation.4 | async-start | bytes 131072 | tf_op jit(solution)/shard_map/all_to_all | solution.py:52
  138.5 0.7 fusion.11
  139.2 2.4 %custom-call.23 = f32[1,32,32]{1,2,0:T(8,128)S(1)} custom-call(f32[1,32,32]{2,1,0:T(8,128)S(1)} %fusion.11), custom_call_target="InvertDiagBlocksLowerTriangular" | custom-call | tf_op jit(solution)/shard_map/jit(_cho_solve)/triangular_solve | solution.py:29
  141.6 1.3 all-to-all-done.4
  143.0 0.2 fusion.25
  143.8 0.2 convolution_convert_fusion
  144.2 0.2 pad_maximum_fusion.1
  144.4 38.8 %all_to_all.41 = bf16[128,10,128]{2,1,0:T(8,128)(2,1)S(1)} all-to-all(bf16[128,10,128]{2,1,0:T(8,128)(2,1)S(1)} %pad_maximum_fusion.1), channel_id=1, replica_groups=mesh['neuron'=128,'trial'=4] {'neuron'}, dimensions={0} | all-to-all | bytes 655360 | tf_op jit(solution)/shard_map/all_to_all | solution.py:113
  183.4 6.6 %all_to_all.42 = f32[4,7,128]{2,1,0:T(8,128)S(1)} all-to-all(f32[4,7,128]{2,1,0:T(8,128)S(1)} %broadcast_in_dim.44), channel_id=1, replica_groups=mesh['neuron'=128,'trial'=4] {'trial'}, dimensions={0} | all-to-all | bytes 28672 | tf_op jit(solution)/shard_map/all_to_all | solution.py:52
  190.0 0.7 gather_fusion.1
  190.9 0.7 select_reduce_fusion.4
  192.4 2.9 %cholesky.148 = f32[32,32]{1,0:T(8,128)S(1)} custom-call(f32[32,32]{1,0:T(8,128)S(1)} %fusion.22), custom_call_target="Cholesky" | custom-call | tf_op jit(solution)/shard_map/jit(cholesky)/cholesky | solution.py:28
  195.4 0.6 compare_reduce_fusion.1
  196.0 0.7 fusion.12
  196.7 2.4 %custom-call.24 = f32[1,32,32]{1,2,0:T(8,128)S(1)} custom-call(f32[1,32,32]{2,1,0:T(8,128)S(1)} %fusion.12), custom_call_target="InvertDiagBlocksLowerTriangular" | custom-call | tf_op jit(solution)/shard_map/jit(_cho_solve)/triangular_solve | solution.py:29
  199.4 0.8 select_reduce_fusion.3
  201.0 2.9 %cholesky.159 = f32[32,32]{1,0:T(8,128)S(1)} custom-call(f32[32,32]{1,0:T(8,128)S(1)} %fusion.17), custom_call_target="Cholesky" | custom-call | tf_op jit(solution)/shard_map/jit(cholesky)/cholesky | solution.py:28
  203.9 0.6 compare_reduce_fusion
  204.6 0.7 fusion.13
  205.2 2.4 %custom-call.25 = f32[1,32,32]{1,2,0:T(8,128)S(1)} custom-call(f32[1,32,32]{2,1,0:T(8,128)S(1)} %fusion.13), custom_call_target="InvertDiagBlocksLowerTriangular" | custom-call | tf_op jit(solution)/shard_map/jit(_cho_solve)/triangular_solve | solution.py:29
  208.3 0.7 broadcast_in_dim.46
  209.0 10.4 %all-to-all-start.7 = ((f32[128,2,128]{2,1,0:T(2,128)}), f32[128,2,128]{2,1,0:T(2,128)S(1)}, u32[]{:S(2)}, u32[]{:S(2)}) async-start(f32[128,2,128]{2,1,0:T(2,128)} %broadcast_in_dim.46), calls=%async_computation.7 | async-start | bytes 262144 | tf_op jit(solution)/shard_map/all_to_all | solution.py:52
  219.4 0.6 constant_dynamic-slice_fusion
  220.0 0.7 broadcast_multiply_fusion
  220.6 14.7 %all-to-all-done.7 = f32[128,2,128]{2,1,0:T(2,128)S(1)} async-done(((f32[128,2,128]{2,1,0:T(2,128)}), f32[128,2,128]{2,1,0:T(2,128)S(1)}, u32[]{:S(2)}, u32[]{:S(2)}) %all-to-all-start.7) | async-done | bytes 131104 | tf_op jit(solution)/shard_map/all_to_all | solution.py:52
  235.7 0.6 copy.276
  (114 shorter events, 6.0 us)
Async XLA Ops:
  0.6 1.1 copy-start
  1.6 0.7 copy-start.2
  3.5 5.5 %copy-start.1 = (f32[32,1024]{1,0:T(8,128)S(1)}, f32[32,1024]{1,0:T(8,128)}, u32[]{:S(2)}) copy-start(f32[32,1024]{1,0:T(8,128)} %param.9) | copy-start | bytes 393220
  4.1 9.4 %all-to-all-start = ((f32[4,33,128]{2,1,0:T(8,128)}), f32[4,33,128]{2,1,0:T(8,128)S(1)}, u32[]{:S(2)}, u32[]{:S(2)}) async-start(f32[4,33,128]{2,1,0:T(8,128)} %broadcast_in_dim.36), calls=%async_computation | async-start | bytes 163840 | tf_op jit(solution)/shard_map/all_to_all | solution.py:52
  75.9 7.4 %all-to-all-start.2 = ((f32[4,7,128]{2,1,0:T(8,128)}), f32[4,7,128]{2,1,0:T(8,128)S(1)}, u32[]{:S(2)}, u32[]{:S(2)}) async-start(f32[4,7,128]{2,1,0:T(8,128)} %broadcast_in_dim.39), calls=%async_computation.2 | async-start | bytes 32768 | tf_op jit(solution)/shard_map/all_to_all | solution.py:52
  102.4 26.4 %all-to-all-start.3 = ((f32[128,2,128]{2,1,0:T(2,128)}), f32[128,2,128]{2,1,0:T(2,128)S(1)}, u32[]{:S(2)}, u32[]{:S(2)}) async-start(f32[128,2,128]{2,1,0:T(2,128)} %broadcast_in_dim.41), calls=%async_computation.3 | async-start | bytes 262144 | tf_op jit(solution)/shard_map/all_to_all | solution.py:52
  135.2 7.7 %all-to-all-start.4 = ((f32[4,32,128]{2,1,0:T(8,128)}), f32[4,32,128]{2,1,0:T(8,128)S(1)}, u32[]{:S(2)}, u32[]{:S(2)}) async-start(f32[4,32,128]{2,1,0:T(8,128)} %broadcast_in_dim.42), calls=%async_computation.4 | async-start | bytes 131072 | tf_op jit(solution)/shard_map/all_to_all | solution.py:52
  209.0 26.4 %all-to-all-start.7 = ((f32[128,2,128]{2,1,0:T(2,128)}), f32[128,2,128]{2,1,0:T(2,128)S(1)}, u32[]{:S(2)}, u32[]{:S(2)}) async-start(f32[128,2,128]{2,1,0:T(2,128)} %broadcast_in_dim.46), calls=%async_computation.7 | async-start | bytes 262144 | tf_op jit(solution)/shard_map/all_to_all | solution.py:52

commit v2 on v0

v2 whole, which is shorter than its diff:
```python
import jax
import jax.numpy as jnp
from jax import lax
from jax.experimental import pallas as pl
from jax.sharding import Mesh, PartitionSpec as P

SWEEPS = 2


ridge_share = 0.1
tiny_eps = 1e-06
EXACT = lax.Precision.HIGHEST
LANES = 128


def gram_of(matrix):
    return lax.dot_general(
        matrix,
        matrix,
        (((1,), (1,)), ((), ())),
        precision=EXACT,
        preferred_element_type=jnp.float32,
    )


def product(left, right):
    return lax.dot_general(
        left,
        right,
        (((1,), (0,)), ((), ())),
        precision=EXACT,
        preferred_element_type=jnp.float32,
    )


def damped_inverse(system):
    size = system.shape[0]
    rows = lax.broadcasted_iota(jnp.int32, (size, size), 0)
    cols = lax.broadcasted_iota(jnp.int32, (size, size), 1)
    eye = (rows == cols).astype(jnp.float32)
    trace = jnp.sum(jnp.sum(system * eye, axis=1, keepdims=True), axis=0, keepdims=True)
    damped = system + ridge_share * (trace / size) * eye
    both = jnp.concatenate([damped, eye], axis=1)
    row = lax.broadcasted_iota(jnp.int32, (size, 1), 0)
    for step in range(size):
        pivot_row = both[step : step + 1, :] / both[step : step + 1, step : step + 1]
        cleared = both - both[:, step : step + 1] * pivot_row
        both = jnp.where(row == step, pivot_row, cleared)
    return both[:, size:]


def inverse_body(left_ref, right_ref, out_ref):
    out_ref[...] = damped_inverse(left_ref[...] * right_ref[...])


def inverse_of(left, right):
    return pl.pallas_call(
        inverse_body, out_shape=jax.ShapeDtypeStruct(left.shape, jnp.float32)
    )(left, right)


def share_all(rows, axis):
    members = lax.axis_size(axis)
    return lax.all_to_all(jnp.broadcast_to(rows[None], (members,) + rows.shape), axis, 0, 0)


def per_device(tensor, time_init, trial_init):
    own_trials, own_neurons, timepoints = tensor.shape
    components = time_init.shape[0]
    planes = lax.axis_size("x")
    blocks = lax.axis_size(("y", "core"))
    neuron_count = own_neurons * blocks * lax.axis_size("z")
    trial_count = own_trials * planes
    width = timepoints // blocks
    plane = lax.axis_index("x")
    q_rows = own_trials * components

    time_now = time_init
    trial_now = None
    trial_gram = None
    for sweep_index in range(SWEEPS):
        time_gram = gram_of(time_now)
        projected = jnp.einsum(
            "rj,kij->kri",
            time_now.astype(jnp.bfloat16),
            tensor,
            preferred_element_type=jnp.float32,
        ).reshape(q_rows, own_neurons)
        if trial_now is None:
            padded = jnp.pad(trial_init, ((0, 0), (0, own_neurons - own_trials)))
            shared = share_all(jnp.concatenate([projected, padded], axis=0), "x")
            trial_now = jnp.concatenate(
                [shared[member, q_rows:, :own_trials] for member in range(planes)], axis=1
            )
            trial_gram = gram_of(trial_now)
            shared = shared[:, :q_rows]
        else:
            shared = share_all(projected, "x")
        projected = shared.reshape(trial_count, components, own_neurons)
        neuron_terms = jnp.sum(trial_now.T[:, :, None] * projected, axis=0)
        raw = product(inverse_of(trial_gram, time_gram), neuron_terms)

        raw_gram = gram_of(raw)
        terms = jnp.sum(raw[None] * projected, axis=2).T
        partial = jnp.einsum(
            "ri,kij->krj", raw.astype(jnp.bfloat16), tensor, preferred_element_type=jnp.float32
        ).reshape(q_rows, blocks, width)
        small = jnp.concatenate(
            [
                raw_gram,
                terms,
                jnp.zeros((components, width - components - trial_count), jnp.float32),
            ],
            axis=1,
        )
        sent = jnp.concatenate(
            [partial.transpose(1, 0, 2), jnp.broadcast_to(small[None], (blocks,) + small.shape)],
            axis=1,
        )
        summed = jnp.sum(lax.all_to_all(sent, ("y", "core"), 0, 0), axis=0)
        rounded = lax.reduce_precision(summed, 8, 7)
        rest = summed[q_rows:] - rounded[q_rows:]
        halves = jnp.concatenate([rounded, rest], axis=0).astype(jnp.bfloat16)
        got = share_all(halves, "z").astype(jnp.float32)
        summed = jnp.sum(got, axis=0)
        columns = summed[:q_rows].reshape(own_trials, components, width)
        small = summed[q_rows : q_rows + components] + summed[q_rows + components :]
        raw_gram = small[:, :components]
        terms = small[:, components : components + trial_count]
        scaling = 1.0 / jnp.sqrt(jnp.diagonal(raw_gram) / neuron_count + tiny_eps)
        neuron_now = raw * scaling[:, None]
        neuron_gram = scaling[:, None] * raw_gram * scaling[None, :]
        trial_now = product(inverse_of(neuron_gram, time_gram), terms * scaling[:, None])
        trial_gram = gram_of(trial_now)
        own_trial = lax.dynamic_slice_in_dim(trial_now, plane * own_trials, own_trials, 1)
        weighted = jnp.sum(own_trial.T[:, :, None] * columns, axis=0) * scaling[:, None]
        gathered = share_all(weighted, ("y", "core", "x"))
        time_inverse = inverse_of(neuron_gram, trial_gram)
        gathered = jnp.sum(gathered.reshape(blocks, planes, components, width), axis=1)
        time_terms = gathered.transpose(1, 0, 2).reshape(components, timepoints)
        time_raw = product(time_inverse, time_terms)
        time_now = time_raw / jnp.sqrt(
            jnp.mean(time_raw * time_raw, axis=1, keepdims=True) + tiny_eps
        )
    position = lax.axis_index(("z", "y", "core", "x"))
    share_width = timepoints // lax.axis_size(("z", "y", "core", "x"))
    time_out = lax.dynamic_slice_in_dim(time_now, position * share_width, share_width, 1)
    trial_out = lax.dynamic_slice_in_dim(trial_now, plane * own_trials, own_trials, 1)
    return (neuron_now, time_out, trial_out)


def solution(mesh):
    neuron, trial = mesh.shape["neuron"], mesh.shape["trial"]
    layers = max(neuron // 8, 1)
    fine = Mesh(
        mesh.devices.reshape(layers, neuron // layers // 2, 2, trial), ("z", "y", "core", "x")
    )
    rows = ("z", "y", "core")
    return jax.shard_map(
        per_device,
        mesh=fine,
        in_specs=(P("x", rows, None), P(), P(None, "x")),
        out_specs=(P(None, rows), P(None, rows + ("x",)), P(None, "x")),
        check_vma=False,
    )
```

time: 2490 us -> 193 us (0.08)
  blocking collectives: 1520 us -> 57.8 us
  waiting for transfers between devices: 890 us -> 39.7 us
  starting transfers between devices: 0.08 us -> 42.8 us
  other arithmetic: 41.8 us -> 3.41 us
  Pallas kernels: 0 us -> 25 us
    psum x6 -> x0, blocking collectives: 1500 us -> none  [the longest x2 972 us: per_device(): lax.psum((gram_of(neuron_now), jnp.sum(neuron_now[None] * projected, axis...]
    psum x2 -> x0, waiting for transfers between devices: 890 us -> none  [per_device(): time_terms = lax.psum(time_local, ('neuron', 'trial'))]
    all_to_all x0 -> x3, blocking collectives: none -> 57.8 us  [the longest x1 28.9 us: share_all(): lax.all_to_all(jnp.broadcast_to(rows[None], (members,) + rows.shape), axi...]
    all_to_all x0 -> x5, starting transfers between devices: none -> 42.8 us  [share_all(): lax.all_to_all(jnp.broadcast_to(rows[None], (members,) + rows.shape), axi...]
    another operation x30 -> x4, other arithmetic: 40.1 us -> 0.03 us  [the longest x18 21.6 us: damped_solve(): cholesky_low = jnp.linalg.cholesky(damped)]
    all_to_all x0 -> x5, waiting for transfers between devices: none -> 39.7 us  [share_all(): lax.all_to_all(jnp.broadcast_to(rows[None], (members,) + rows.shape), axi...]
    pallas_call x0 -> x6, Pallas kernels: none -> 25 us  [inverse_of(): pl.pallas_call(inverse_body, out_shape=jax.ShapeDtypeStruct(left.shape, j...]
  transfers between devices with their start and end apart: 2 -> 5, of which waited for: 2 -> 4; matrix products, arithmetic and copies ran while one was open for 0% -> 2% of each run, Pallas kernels for 0% -> 7%
where the time goes in v2:
time: 193 us; the launch traced here: 190 us
  blocking collectives  57.8 us (30%)
  starting transfers between devices  42.8 us (22%)
  waiting for transfers between devices  39.7 us (21%)
  Pallas kernels  25 us (13%)
  local copies, waits for them, and re-layouts  10.6 us (5%)
  matrix products  10.1 us (5%)
  other arithmetic  3.41 us (2%)
    all_to_all x5, starting transfers between devices, share_all(): lax.all_to_all(jnp.broadcast_to(rows[None], (members,) + rows.shape), axi...  42.8 us
    all_to_all x5, waiting for transfers between devices, share_all(): lax.all_to_all(jnp.broadcast_to(rows[None], (members,) + rows.shape), axi...  39.7 us
    all_to_all x1, blocking collectives, share_all(): lax.all_to_all(jnp.broadcast_to(rows[None], (members,) + rows.shape), axi...  28.9 us
    all_to_all x2, blocking collectives, per_device(): summed = jnp.sum(lax.all_to_all(sent, ('y', 'core'), 0, 0), axis=0)  28.8 us
    pallas_call x6, Pallas kernels, inverse_of(): pl.pallas_call(inverse_body, out_shape=jax.ShapeDtypeStruct(left.shape, j...  25 us
    dot_general x7, matrix products, gram_of(): lax.dot_general(matrix, matrix, (((1,), (1,)), ((), ())), precision=EXACT...  4.56 us
    broadcast_in_dim x6, local copies, waits for them, and re-layouts, share_all(): jnp.broadcast_to(rows[None], (members,) + rows.shape)  4.05 us
  transfers between devices with their start and end apart: 5, of which 4 were waited for; matrix products, arithmetic and copies ran while one was open for 2% of the time, Pallas kernels for 7%

profile of v2, /device:TPU:1, one launch (start us, length us, event | category | flops | bytes accessed | tf_op | source)
XLA Modules:
  0.0 190.4 jit_solution(16411053317080081721)
XLA Ops:
  0.6 0.8 copy.39
  1.5 0.2 copy-done
  1.7 1.1 fusion.10
  2.9 0.7 broadcast_in_dim.24
  3.6 5.0 %all-to-all-start = ((f32[4,96,128]{2,1,0:T(8,128)}), f32[4,96,128]{2,1,0:T(8,128)S(1)}, u32[]{:S(2)}, u32[]{:S(2)}) async-start(f32[4,96,128]{2,1,0:T(8,128)} %broadcast_in_dim.24), calls=%async_computation | async-start | bytes 393216 | tf_op jit(solution)/shard_map/all_to_all | solution.py:64
  8.5 0.1 pad.18.clone
  8.6 0.9 fusion.31.right_ref
  9.5 4.2 %all-to-all-done = f32[4,96,128]{2,1,0:T(8,128)S(1)} async-done(((f32[4,96,128]{2,1,0:T(8,128)}), f32[4,96,128]{2,1,0:T(8,128)S(1)}, u32[]{:S(2)}, u32[]{:S(2)}) %all-to-all-start) | async-done | bytes 196640 | tf_op jit(solution)/shard_map/all_to_all | solution.py:64
  13.7 0.1 copy.28
  14.0 0.8 fusion.28.left_ref
  14.9 0.1 multiply_reduce_fusion.3
  15.0 4.2 %shard_map.58 = f32[32,32]{1,0:T(8,128)} custom-call(f32[32,32]{1,0:T(8,128)} %fusion.28.left_ref, f32[32,32]{1,0:T(8,128)} %fusion.31.right_ref), custom_call_target="tpu_custom_call" | custom-call | tf_op jit(solution)/shard_map/pallas_call | solution.py:57
  19.2 0.8 fusion.32
  20.0 0.2 fusion.33
  20.2 0.2 fusion.21
  20.4 0.1 fusion.7
  20.6 0.1 copy.33
  20.8 0.1 maximum_maximum_fusion
  20.9 16.9 %all_to_all.40 = f32[8,96,128]{2,1,0:T(8,128)S(1)} all-to-all(f32[8,96,128]{2,1,0:T(8,128)S(1)} %pad_maximum_fusion), channel_id=1, replica_groups=mesh['z'=16,'y'=4,'core'=2,'x'=4] {'y','core'}, dimensions={0} | all-to-all | bytes 786432 | tf_op jit(solution)/shard_map/all_to_all | solution.py:120
  37.9 0.9 broadcast_in_dim.26
  38.8 12.4 %all-to-all-start.2 = ((bf16[16,128,128]{2,1,0:T(8,128)(2,1)}), bf16[16,128,128]{2,1,0:T(8,128)(2,1)S(1)}, u32[]{:S(2)}, u32[]{:S(2)}) async-start(bf16[16,128,128]{2,1,0:T(8,128)(2,1)} %broadcast_in_dim.26), calls=%async_computation.2 | async-start | bytes 1048576 | tf_op jit(solution)/shard_map/all_to_all | solution.py:64
  51.3 23.1 %all-to-all-done.2 = bf16[16,128,128]{2,1,0:T(8,128)(2,1)S(1)} async-done(((bf16[16,128,128]{2,1,0:T(8,128)(2,1)}), bf16[16,128,128]{2,1,0:T(8,128)(2,1)S(1)}, u32[]{:S(2)}, u32[]{:S(2)}) %all-to-all-start.2) | async-done | bytes 524320 | tf_op jit(solution)/shard_map/all_to_all | solution.py:64
  74.4 0.6 copy-done.2
  75.0 0.7 gather_fusion
  75.8 0.7 multiply_multiply_fusion.1.left_ref
  76.5 4.2 %shard_map.59 = f32[32,32]{1,0:T(8,128)} custom-call(f32[32,32]{1,0:T(8,128)} %multiply_multiply_fusion.1.left_ref, f32[32,32]{1,0:T(8,128)} %fusion.31.right_ref), custom_call_target="tpu_custom_call" | custom-call | tf_op jit(solution)/shard_map/pallas_call | solution.py:57
  80.6 1.0 fusion.17
  81.8 0.9 broadcast_in_dim.27
  82.6 10.5 %all-to-all-start.3 = ((f32[32,32,128]{2,1,0:T(8,128)}), f32[32,32,128]{2,1,0:T(8,128)S(1)}, u32[]{:S(2)}, u32[]{:S(2)}) async-start(f32[32,32,128]{2,1,0:T(8,128)} %broadcast_in_dim.27), calls=%async_computation.3 | async-start | bytes 1048576 | tf_op jit(solution)/shard_map/all_to_all | solution.py:64
  93.2 0.8 fusion.34.right_ref.left_ref
  94.0 4.2 %shard_map.60 = f32[32,32]{1,0:T(8,128)} custom-call(f32[32,32]{1,0:T(8,128)} %multiply_multiply_fusion.1.left_ref, f32[32,32]{1,0:T(8,128)} %fusion.34.right_ref.left_ref), custom_call_target="tpu_custom_call" | custom-call | tf_op jit(solution)/shard_map/pallas_call | solution.py:57
  98.2 6.5 %all-to-all-done.3 = f32[32,32,128]{2,1,0:T(8,128)S(1)} async-done(((f32[32,32,128]{2,1,0:T(8,128)}), f32[32,32,128]{2,1,0:T(8,128)S(1)}, u32[]{:S(2)}, u32[]{:S(2)}) %all-to-all-start.3) | async-done | bytes 524320 | tf_op jit(solution)/shard_map/all_to_all | solution.py:64
  104.7 0.4 multiply_reduce_fusion.2
  105.1 0.3 fusion.8
  105.4 0.7 broadcast_in_dim.29
  106.1 3.3 %all-to-all-start.4 = ((f32[4,64,128]{2,1,0:T(8,128)}), f32[4,64,128]{2,1,0:T(8,128)S(1)}, u32[]{:S(2)}, u32[]{:S(2)}) async-start(f32[4,64,128]{2,1,0:T(8,128)} %broadcast_in_dim.29), calls=%async_computation.4 | async-start | bytes 262144 | tf_op jit(solution)/shard_map/all_to_all | solution.py:64
  109.4 0.9 fusion.14.right_ref
  110.3 4.2 %shard_map.61 = f32[32,32]{1,0:T(8,128)} custom-call(f32[32,32]{1,0:T(8,128)} %fusion.34.right_ref.left_ref, f32[32,32]{1,0:T(8,128)} %fusion.14.right_ref), custom_call_target="tpu_custom_call" | custom-call | tf_op jit(solution)/shard_map/pallas_call | solution.py:57
  114.5 0.1 multiply_reduce_fusion.1
  114.6 0.6 copy-done.6
  115.2 0.1 fusion.35
  115.3 0.2 fusion.19
  115.6 0.1 fusion.36
  115.9 0.1 fusion.6
  116.1 0.1 copy.36
  116.1 0.1 maximum_maximum_fusion.1
  116.3 11.9 %all_to_all.41 = f32[8,96,128]{2,1,0:T(8,128)S(1)} all-to-all(f32[8,96,128]{2,1,0:T(8,128)S(1)} %pad_maximum_fusion.1), channel_id=1, replica_groups=mesh['z'=16,'y'=4,'core'=2,'x'=4] {'y','core'}, dimensions={0} | all-to-all | bytes 786432 | tf_op jit(solution)/shard_map/all_to_all | solution.py:120
  128.3 0.1 broadcast_in_dim.31
  128.4 28.9 %all_to_all.42 = bf16[16,128,128]{2,1,0:T(8,128)(2,1)S(1)} all-to-all(bf16[16,128,128]{2,1,0:T(8,128)(2,1)S(1)} %broadcast_in_dim.31), channel_id=1, replica_groups=mesh['z'=16,'y'=4,'core'=2,'x'=4] {'z'}, dimensions={0} | all-to-all | bytes 1048576 | tf_op jit(solution)/shard_map/all_to_all | solution.py:64
  157.4 0.6 copy-done.3
  158.0 0.7 gather_fusion.1
  158.7 0.7 multiply_multiply_fusion.left_ref
  159.4 4.2 %shard_map.62 = f32[32,32]{1,0:T(8,128)} custom-call(f32[32,32]{1,0:T(8,128)} %multiply_multiply_fusion.left_ref, f32[32,32]{1,0:T(8,128)} %fusion.14.right_ref), custom_call_target="tpu_custom_call" | custom-call | tf_op jit(solution)/shard_map/pallas_call | solution.py:57
  163.6 1.0 fusion.15
  164.6 0.7 broadcast_multiply_fusion
  165.3 0.8 broadcast_in_dim.32
  166.2 11.6 %all-to-all-start.7 = ((f32[32,32,128]{2,1,0:T(8,128)}), f32[32,32,128]{2,1,0:T(8,128)S(1)}, u32[]{:S(2)}, u32[]{:S(2)}) async-start(f32[32,32,128]{2,1,0:T(8,128)} %broadcast_in_dim.32), calls=%async_computation.7 | async-start | bytes 1048576 | tf_op jit(solution)/shard_map/all_to_all | solution.py:64
  177.8 0.8 fusion.37.right_ref
  178.7 4.2 %shard_map.63 = f32[32,32]{1,0:T(8,128)} custom-call(f32[32,32]{1,0:T(8,128)} %multiply_multiply_fusion.left_ref, f32[32,32]{1,0:T(8,128)} %fusion.37.right_ref), custom_call_target="tpu_custom_call" | custom-call | tf_op jit(solution)/shard_map/pallas_call | solution.py:57
  182.8 0.6 constant_dynamic-slice_fusion
  183.4 5.8 %all-to-all-done.7 = f32[32,32,128]{2,1,0:T(8,128)S(1)} async-done(((f32[32,32,128]{2,1,0:T(8,128)}), f32[32,32,128]{2,1,0:T(8,128)S(1)}, u32[]{:S(2)}, u32[]{:S(2)}) %all-to-all-start.7) | async-done | bytes 524320 | tf_op jit(solution)/shard_map/all_to_all | solution.py:64
  189.3 0.4 multiply_reduce_fusion
  189.7 0.1 dynamic-slice_divide_fusion
  189.8 0.6 copy.38
  (59 shorter events, 1.4 us)
Async XLA Ops:
  0.6 1.1 copy-start
  3.6 5.0 %copy-start.1 = (f32[32,1024]{1,0:T(8,128)S(1)}, f32[32,1024]{1,0:T(8,128)}, u32[]{:S(2)}) copy-start(f32[32,1024]{1,0:T(8,128)} %param.4) | copy-start | bytes 393220
  3.6 10.1 %all-to-all-start = ((f32[4,96,128]{2,1,0:T(8,128)}), f32[4,96,128]{2,1,0:T(8,128)S(1)}, u32[]{:S(2)}, u32[]{:S(2)}) async-start(f32[4,96,128]{2,1,0:T(8,128)} %broadcast_in_dim.24), calls=%async_computation | async-start | bytes 393216 | tf_op jit(solution)/shard_map/all_to_all | solution.py:64
  38.8 35.5 %all-to-all-start.2 = ((bf16[16,128,128]{2,1,0:T(8,128)(2,1)}), bf16[16,128,128]{2,1,0:T(8,128)(2,1)S(1)}, u32[]{:S(2)}, u32[]{:S(2)}) async-start(bf16[16,128,128]{2,1,0:T(8,128)(2,1)} %broadcast_in_dim.26), calls=%async_computation.2 | async-start | bytes 1048576 | tf_op jit(solution)/shard_map/all_to_all | solution.py:64
  74.4 0.6 copy-start.2
  80.6 1.0 slice-start
  82.6 22.0 %all-to-all-start.3 = ((f32[32,32,128]{2,1,0:T(8,128)}), f32[32,32,128]{2,1,0:T(8,128)S(1)}, u32[]{:S(2)}, u32[]{:S(2)}) async-start(f32[32,32,128]{2,1,0:T(8,128)} %broadcast_in_dim.27), calls=%async_computation.3 | async-start | bytes 1048576 | tf_op jit(solution)/shard_map/all_to_all | solution.py:64
  98.2 6.6 %copy-start.5 = (f32[32,32]{1,0:T(8,128)S(1)}, f32[32,32]{1,0:T(8,128)}, u32[]{:S(2)}) copy-start(f32[32,32]{1,0:T(8,128)} %shard_map.60) | copy-start | bytes 12292
  106.1 8.4 %all-to-all-start.4 = ((f32[4,64,128]{2,1,0:T(8,128)}), f32[4,64,128]{2,1,0:T(8,128)S(1)}, u32[]{:S(2)}, u32[]{:S(2)}) async-start(f32[4,64,128]{2,1,0:T(8,128)} %broadcast_in_dim.29), calls=%async_computation.4 | async-start | bytes 262144 | tf_op jit(solution)/shard_map/all_to_all | solution.py:64
  114.5 0.7 copy-start.6
  157.4 0.6 copy-start.3
  163.6 1.0 slice-start.1
  166.2 23.1 %all-to-all-start.7 = ((f32[32,32,128]{2,1,0:T(8,128)}), f32[32,32,128]{2,1,0:T(8,128)S(1)}, u32[]{:S(2)}, u32[]{:S(2)}) async-start(f32[32,32,128]{2,1,0:T(8,128)} %broadcast_in_dim.32), calls=%async_computation.7 | async-start | bytes 1048576 | tf_op jit(solution)/shard_map/all_to_all | solution.py:64
  183.4 5.9 %copy-start.4 = (f32[32,32]{1,0:T(8,128)S(1)}, f32[32,32]{1,0:T(8,128)}, u32[]{:S(2)}) copy-start(f32[32,32]{1,0:T(8,128)} %shard_map.63) | copy-start | bytes 12292

commit v3 on v0

v3 whole, which is shorter than its diff:
```python
import jax
import jax.numpy as jnp
from jax import lax
from jax.experimental import pallas as pl
from jax.experimental.pallas import tpu as pltpu
from jax.sharding import Mesh, PartitionSpec as P

SWEEPS = 2


ridge_share = 0.1
tiny_eps = 1e-06
EXACT = lax.Precision.HIGHEST
PART = 8
WIRE = jnp.bfloat16


def gram_of(matrix):
    return lax.dot_general(
        matrix,
        matrix,
        (((1,), (1,)), ((), ())),
        precision=EXACT,
        preferred_element_type=jnp.float32,
    )


def product(left, right):
    return lax.dot_general(
        left,
        right,
        (((1,), (0,)), ((), ())),
        precision=EXACT,
        preferred_element_type=jnp.float32,
    )


def eye_of(size):
    rows = lax.broadcasted_iota(jnp.int32, (size, size), 0)
    cols = lax.broadcasted_iota(jnp.int32, (size, size), 1)
    return (rows == cols).astype(jnp.float32)


def damped_inverse(system):
    size = system.shape[0]
    eye = eye_of(size)
    trace = jnp.sum(jnp.sum(system * eye, axis=1, keepdims=True), axis=0, keepdims=True)
    share = size / trace
    both = jnp.concatenate([system * share + ridge_share * eye, eye], axis=1)
    row = lax.broadcasted_iota(jnp.int32, both.shape, 0)
    for step in range(0, size, 2):
        first = jnp.broadcast_to(both[:, step : step + 1], both.shape)
        second = jnp.broadcast_to(both[:, step + 1 : step + 2], both.shape)
        upper, lower = both[step : step + 1], both[step + 1 : step + 2]
        p00, p01 = first[step : step + 1], second[step : step + 1]
        p10, p11 = first[step + 1 : step + 2], second[step + 1 : step + 2]
        over = 1.0 / (p00 * p11 - p01 * p10)
        new_upper = (p11 * upper - p01 * lower) * over
        new_lower = (p00 * lower - p10 * upper) * over
        cleared = both - first * new_upper - second * new_lower
        both = jnp.where(row == step, new_upper, jnp.where(row == step + 1, new_lower, cleared))
    return both[:, size:] * share


def pack_small(gram, terms):
    size = gram.shape[0]
    pieces = []
    for start in range(0, size, PART):
        pieces.append(gram[start : start + PART, start:])
    for start in range(0, size, PART):
        pieces.append(terms[start : start + PART])
    used = sum(piece.shape[1] for piece in pieces)
    pieces.append(jnp.zeros((PART, 128 - used), jnp.float32))
    return jnp.concatenate(pieces, axis=1)


def unpack_small(tile, size, count):
    rows, place = [], 0
    for start in range(0, size, PART):
        piece = tile[:, place : place + size - start]
        place += size - start
        if start:
            piece = jnp.concatenate([jnp.zeros((PART, start), jnp.float32), piece], axis=1)
        rows.append(piece)
    upper = jnp.concatenate(rows, axis=0)
    terms = []
    for start in range(0, size, PART):
        terms.append(tile[:, place : place + count])
        place += count
    row_part = lax.broadcasted_iota(jnp.int32, (size, size), 0) // PART
    col_part = lax.broadcasted_iota(jnp.int32, (size, size), 1) // PART
    return jnp.where(col_part >= row_part, upper, upper.T), jnp.concatenate(terms, axis=0)


def call(body, outs, *args, smem=()):
    specs = [
        pl.BlockSpec(memory_space=pltpu.SMEM if place in smem else pltpu.VMEM)
        for place in range(len(args))
    ]
    return pl.pallas_call(
        body,
        out_shape=outs,
        in_specs=specs,
        out_specs=jax.tree.map(lambda out: pl.BlockSpec(memory_space=pltpu.VMEM), outs),
    )(*args)


def put_projected(time_now, tensor_ref, sent_ref):
    rounded = time_now.astype(jnp.bfloat16)
    size = time_now.shape[0]
    for trial in range(tensor_ref.shape[0]):
        projected = lax.dot_general(
            rounded,
            tensor_ref[trial],
            (((1,), (1,)), ((), ())),
            preferred_element_type=jnp.float32,
        )
        for member in range(sent_ref.shape[0]):
            sent_ref[member, trial * size : (trial + 1) * size, :] = projected


def project_body(time_ref, trial_ref, tensor_ref, sent_ref):
    put_projected(time_ref[...], tensor_ref, sent_ref)
    size, count = trial_ref.shape
    lanes = sent_ref.shape[2]
    tile = jnp.concatenate([trial_ref[...], jnp.zeros((size, lanes - count), jnp.float32)], axis=1)
    for member in range(sent_ref.shape[0]):
        sent_ref[member, tensor_ref.shape[0] * size :, :] = tile


def put_neuron(trial_now, inverse, shared_ref, tensor_ref, raw_ref, sent_ref):
    size, trial_count = trial_now.shape
    own_trials = tensor_ref.shape[0]
    terms = []
    projected = []
    for trial in range(trial_count):
        start = trial % own_trials * size
        projected.append(shared_ref[trial // own_trials, start : start + size, :])
    neuron_terms = trial_now[:, 0:1] * projected[0]
    for trial in range(1, trial_count):
        neuron_terms = neuron_terms + trial_now[:, trial : trial + 1] * projected[trial]
    raw = product(inverse, neuron_terms)
    raw_ref[...] = raw
    lane = lax.broadcasted_iota(jnp.int32, (size, trial_count), 1)
    terms = jnp.zeros((size, trial_count), jnp.float32)
    for trial in range(trial_count):
        one = jnp.sum(raw * projected[trial], axis=1, keepdims=True)
        terms = jnp.where(lane == trial, one, terms)
    small = pack_small(gram_of(raw), terms)
    blocks, rows, width = sent_ref.shape
    rounded = raw.astype(jnp.bfloat16)
    for trial in range(own_trials):
        partial = jnp.dot(rounded, tensor_ref[trial], preferred_element_type=jnp.float32)
        for block in range(blocks):
            sent_ref[block, trial * size : (trial + 1) * size, :] = partial[
                :, block * width : (block + 1) * width
            ]
    for block in range(blocks):
        sent_ref[block, own_trials * size :, :] = small


def first_neuron_body(shared_ref, gram_ref, tensor_ref, raw_ref, sent_ref):
    own_trials = tensor_ref.shape[0]
    size = raw_ref.shape[0]
    columns = [
        shared_ref[member, own_trials * size :, :own_trials]
        for member in range(shared_ref.shape[0])
    ]
    trial_now = jnp.concatenate(columns, axis=1)
    inverse = damped_inverse(gram_of(trial_now) * gram_ref[...])
    put_neuron(trial_now, inverse, shared_ref, tensor_ref, raw_ref, sent_ref)


def neuron_body(shared_ref, trial_ref, inverse_ref, tensor_ref, raw_ref, sent_ref):
    put_neuron(trial_ref[...], inverse_ref[...], shared_ref, tensor_ref, raw_ref, sent_ref)


def reduce_body(got_ref, sent_ref):
    total = got_ref[0]
    for member in range(1, got_ref.shape[0]):
        total = total + got_ref[member]
    rounded = total.astype(WIRE)
    main = total.shape[0] - PART
    small = total[main:]
    high = small.astype(WIRE).astype(jnp.float32)
    halves = jnp.concatenate([high, small - high], axis=0).astype(WIRE)
    for member in range(sent_ref.shape[0]):
        sent_ref[member, :main, :] = rounded[:main]
        sent_ref[member, main:, :] = halves


def finish_body(neuron_count, plane_ref, got_ref, gram_ref, raw_ref, *outs):
    neuron_ref, neuron_gram_ref, trial_ref, trial_gram_ref, own_ref, sent_ref = outs
    size = raw_ref.shape[0]
    trial_count = trial_ref.shape[1]
    own_trials = own_ref.shape[1]
    total = got_ref[0].astype(jnp.float32)
    for member in range(1, got_ref.shape[0]):
        total = total + got_ref[member].astype(jnp.float32)
    main = own_trials * size
    small = total[main : main + PART] + total[main + PART :]
    raw_gram, terms = unpack_small(small, size, trial_count)
    diagonal = raw_gram * eye_of(size)
    down = 1.0 / jnp.sqrt(jnp.sum(diagonal, axis=1, keepdims=True) / neuron_count + tiny_eps)
    across = 1.0 / jnp.sqrt(jnp.sum(diagonal, axis=0, keepdims=True) / neuron_count + tiny_eps)
    neuron_ref[...] = raw_ref[...] * down
    neuron_gram = down * raw_gram * across
    neuron_gram_ref[...] = neuron_gram
    trial_now = product(damped_inverse(neuron_gram * gram_ref[...]), terms * down)
    trial_ref[...] = trial_now
    trial_gram_ref[...] = gram_of(trial_now)
    lane = lax.broadcasted_iota(jnp.int32, trial_now.shape, 1)
    weighted = None
    for trial in range(own_trials):
        mine = lane == plane_ref[0] * own_trials + trial
        column = jnp.sum(jnp.where(mine, trial_now, 0.0), axis=1, keepdims=True)
        own_ref[:, trial : trial + 1] = column
        part = column * total[trial * size : (trial + 1) * size]
        weighted = part if weighted is None else weighted + part
    weighted = weighted * down
    for member in range(sent_ref.shape[0]):
        sent_ref[member] = weighted


def inverse_body(left_ref, right_ref, out_ref):
    out_ref[...] = damped_inverse(left_ref[...] * right_ref[...])


def time_of(planes, got_ref, inverse_ref):
    pieces = []
    for block in range(got_ref.shape[0] // planes):
        piece = got_ref[block * planes]
        for plane in range(1, planes):
            piece = piece + got_ref[block * planes + plane]
        pieces.append(piece)
    raw = product(inverse_ref[...], jnp.concatenate(pieces, axis=1))
    mean = jnp.sum(raw * raw, axis=1, keepdims=True) / raw.shape[1]
    return raw / jnp.sqrt(mean + tiny_eps)


def next_body(planes, got_ref, inverse_ref, tensor_ref, time_ref, sent_ref):
    time_now = time_of(planes, got_ref, inverse_ref)
    time_ref[...] = time_now
    put_projected(time_now, tensor_ref, sent_ref)


def gram_body(time_ref, gram_ref):
    gram_ref[...] = gram_of(time_ref[...])


def next_inverse_body(time_ref, trial_gram_ref, gram_ref, inverse_ref):
    gram = gram_of(time_ref[...])
    gram_ref[...] = gram
    inverse_ref[...] = damped_inverse(gram * trial_gram_ref[...])


def last_body(planes, got_ref, inverse_ref, time_ref):
    time_ref[...] = time_of(planes, got_ref, inverse_ref)


def per_device(tensor, time_init, trial_init):
    own_trials, own_neurons, timepoints = tensor.shape
    components = time_init.shape[0]
    planes = lax.axis_size("x")
    short = ("y", "core")
    blocks = lax.axis_size(short)
    layers = lax.axis_size("z")
    neuron_count = own_neurons * blocks * layers
    trial_count = own_trials * planes
    width = timepoints // blocks
    main = own_trials * components
    plane = lax.axis_index("x").astype(jnp.int32).reshape(1)

    def shape(*dims, kind=jnp.float32):
        return jax.ShapeDtypeStruct(dims, kind)

    square = shape(components, components)
    neuron_outs = (shape(components, own_neurons), shape(blocks, main + PART, width))
    shared = call(
        project_body,
        shape(planes, main + components, own_neurons),
        time_init,
        trial_init,
        tensor,
    )
    shared = lax.all_to_all(shared, "x", 0, 0)
    time_gram = call(gram_body, square, time_init)
    raw, sent = call(first_neuron_body, neuron_outs, shared, time_gram, tensor)
    for sweep_index in range(SWEEPS):
        got = lax.all_to_all(sent, short, 0, 0)
        sent = call(reduce_body, shape(layers, main + 2 * PART, width, kind=WIRE), got)
        got = lax.all_to_all(sent, "z", 0, 0)
        neuron_now, neuron_gram, trial_now, trial_gram, own_trial, sent = call(
            lambda *refs: finish_body(neuron_count, *refs),
            (
                shape(components, own_neurons),
                square,
                shape(components, trial_count),
                square,
                shape(components, own_trials),
                shape(blocks * planes, components, width),
            ),
            plane,
            got,
            time_gram,
            raw,
            smem=(0,),
        )
        got = lax.all_to_all(sent, short + ("x",), 0, 0)
        inverse = call(inverse_body, square, neuron_gram, trial_gram)
        if sweep_index == SWEEPS - 1:
            time_now = call(
                lambda *refs: last_body(planes, *refs),
                shape(components, timepoints),
                got,
                inverse,
            )
            break
        time_now, shared = call(
            lambda *refs: next_body(planes, *refs),
            (shape(components, timepoints), shape(planes, main, own_neurons)),
            got,
            inverse,
            tensor,
        )
        shared = lax.all_to_all(shared, "x", 0, 0)
        time_gram, inverse = call(next_inverse_body, (square, square), time_now, trial_gram)
        raw, sent = call(neuron_body, neuron_outs, shared, trial_now, inverse, tensor)
    position = lax.axis_index(("z", "y", "core", "x"))
    share_width = timepoints // (layers * blocks * planes)
    time_out = lax.dynamic_slice_in_dim(time_now, position * share_width, share_width, 1)
    return (neuron_now, time_out, own_trial)


def solution(mesh):
    neuron, trial = mesh.shape["neuron"], mesh.shape["trial"]
    layers = max(neuron // 8, 1)
    fine = Mesh(
        mesh.devices.reshape(layers, neuron // layers // 2, 2, trial), ("z", "y", "core", "x")
    )
    rows = ("z", "y", "core")
    return jax.shard_map(
        per_device,
        mesh=fine,
        in_specs=(P("x", rows, None), P(), P(None, "x")),
        out_specs=(P(None, rows), P(None, rows + ("x",)), P(None, "x")),
        check_vma=False,
    )
```

time: 2490 us -> 173 us (0.07)
  blocking collectives: 1520 us -> 51.9 us
  waiting for transfers between devices: 890 us -> 35.7 us
  other arithmetic: 41.8 us -> 0 us
  starting transfers between devices: 0.08 us -> 39.5 us
  Pallas kernels: 0 us -> 36 us
    psum x6 -> x0, blocking collectives: 1500 us -> none  [the longest x2 972 us: per_device(): lax.psum((gram_of(neuron_now), jnp.sum(neuron_now[None] * projected, axis...]
    psum x2 -> x0, waiting for transfers between devices: 890 us -> none  [per_device(): time_terms = lax.psum(time_local, ('neuron', 'trial'))]
    all_to_all x0 -> x3, blocking collectives: none -> 51.9 us  [the longest x2 30.7 us: per_device(): got = lax.all_to_all(sent, short, 0, 0)]
    another operation x30 -> x0, other arithmetic: 40.1 us -> none  [the longest x18 21.6 us: damped_solve(): cholesky_low = jnp.linalg.cholesky(damped)]
    all_to_all x0 -> x5, starting transfers between devices: none -> 39.5 us  [the longest x2 20.3 us: per_device(): got = lax.all_to_all(sent, short + ('x',), 0, 0)]
    pallas_call x0 -> x13, Pallas kernels: none -> 36 us  [call(): pl.pallas_call(body, out_shape=outs, in_specs=specs, out_specs=jax.tree.m...]
    all_to_all x0 -> x5, waiting for transfers between devices: none -> 35.7 us  [the longest x2 15.6 us: per_device(): got = lax.all_to_all(sent, short + ('x',), 0, 0)]
  transfers between devices with their start and end apart: 2 -> 5, of which waited for: 2 -> 5; matrix products, arithmetic and copies ran while one was open for 0% -> 0% of each run, Pallas kernels for 0% -> 7%
where the time goes in v3:
time: 173 us; the launch traced here: 172 us
  blocking collectives  51.9 us (30%)
  starting transfers between devices  39.5 us (23%)
  Pallas kernels  36 us (21%)
  waiting for transfers between devices  35.7 us (21%)
  local copies, waits for them, and re-layouts  7.76 us (4%)
    pallas_call x13, Pallas kernels, call(): pl.pallas_call(body, out_shape=outs, in_specs=specs, out_specs=jax.tree.m...  36 us
    all_to_all x2, blocking collectives, per_device(): got = lax.all_to_all(sent, short, 0, 0)  30.7 us
    all_to_all x1, blocking collectives, per_device(): got = lax.all_to_all(sent, 'z', 0, 0)  21.1 us
    all_to_all x2, starting transfers between devices, per_device(): got = lax.all_to_all(sent, short + ('x',), 0, 0)  20.3 us
    all_to_all x2, waiting for transfers between devices, per_device(): got = lax.all_to_all(sent, short + ('x',), 0, 0)  15.6 us
    all_to_all x1, waiting for transfers between devices, per_device(): got = lax.all_to_all(sent, 'z', 0, 0)  15.3 us
    all_to_all x1, starting transfers between devices, per_device(): got = lax.all_to_all(sent, 'z', 0, 0)  11.1 us
    all_to_all x2, starting transfers between devices, per_device(): shared = lax.all_to_all(shared, 'x', 0, 0)  8.15 us
  transfers between devices with their start and end apart: 5, of which 5 were waited for; matrix products, arithmetic and copies ran while one was open for 0% of the time, Pallas kernels for 7%

profile of v3, /device:TPU:1, one launch (start us, length us, event | category | flops | bytes accessed | tf_op | source)
XLA Modules:
  0.0 171.6 jit_solution(13990030095222446999)
XLA Ops:
  0.6 1.4 copy.6.trial_ref
  2.0 2.1 %shard_map.58 = f32[4,96,128]{2,1,0:T(8,128)} custom-call(f32[32,1024]{1,0:T(8,128)} %time_ref.3, f32[32,2]{1,0:T(8,128)} %copy.6.trial_ref, bf16[2,128,1024]{2,1,0:T(8,128)(2,1)} %tensor_ref.5), custom_call_target="tpu_custom_call" | custom-call | tf_op jit(solution)/shard_map/pallas_call | solution.py:100
  4.1 4.8 %all-to-all-start = ((f32[4,96,128]{2,1,0:T(8,128)}), f32[4,96,128]{2,1,0:T(8,128)S(1)}, u32[]{:S(2)}, u32[]{:S(2)}) async-start(f32[4,96,128]{2,1,0:T(8,128)} %shard_map.58), calls=%async_computation | async-start | bytes 393216 | tf_op jit(solution)/shard_map/all_to_all | solution.py:286
  8.9 1.8 %shard_map.59.gram_ref.refs_2_ = f32[32,32]{1,0:T(8,128)} custom-call(f32[32,1024]{1,0:T(8,128)} %time_ref.3), custom_call_target="tpu_custom_call" | custom-call | tf_op jit(solution)/shard_map/pallas_call | solution.py:100
  10.7 3.4 %all-to-all-done.shared_ref = f32[4,96,128]{2,1,0:T(8,128)S(1)} async-done(((f32[4,96,128]{2,1,0:T(8,128)}), f32[4,96,128]{2,1,0:T(8,128)S(1)}, u32[]{:S(2)}, u32[]{:S(2)}) %all-to-all-start) | async-done | bytes 196640 | tf_op jit(solution)/shard_map/all_to_all | solution.py:286
  14.1 0.0 copy-start.3
  14.1 0.7 copy-done.3
  14.8 4.2 %shard_map.60 = (f32[32,128]{1,0:T(8,128)}, f32[8,72,128]{2,1,0:T(8,128)}) custom-call(f32[4,96,128]{2,1,0:T(8,128)} %copy-done.3, f32[32,32]{1,0:T(8,128)} %shard_map.59.gram_ref.refs_2_, bf16[2,128,1024]{2,1,0:T(8,128)(2,1)} %tensor_ref.5), custom_call_target="tpu_custom_call" | custom-call | tf_op jit(solution)/shard_map/pallas_call | solution.py:100
  18.9 17.8 %all_to_all.40.got_ref = f32[8,72,128]{2,1,0:T(8,128)} all-to-all(f32[8,72,128]{2,1,0:T(8,128)} %get-tuple-element.20), channel_id=1, replica_groups=mesh['z'=16,'y'=4,'core'=2,'x'=4] {'y','core'}, dimensions={0} | all-to-all | bytes 589824 | tf_op jit(solution)/shard_map/all_to_all | solution.py:290
  36.8 1.7 %shard_map.61 = bf16[16,80,128]{2,1,0:T(8,128)(2,1)} custom-call(f32[8,72,128]{2,1,0:T(8,128)} %all_to_all.40.got_ref), custom_call_target="tpu_custom_call" | custom-call | tf_op jit(solution)/shard_map/pallas_call | solution.py:100
  38.5 11.1 %all-to-all-start.2 = ((bf16[16,80,128]{2,1,0:T(8,128)(2,1)}), bf16[16,80,128]{2,1,0:T(8,128)(2,1)S(1)}, u32[]{:S(2)}, u32[]{:S(2)}) async-start(bf16[16,80,128]{2,1,0:T(8,128)(2,1)} %shard_map.61), calls=%async_computation.2 | async-start | bytes 655360 | tf_op jit(solution)/shard_map/all_to_all | solution.py:292
  49.6 15.3 %all-to-all-done.2.refs_1_ = bf16[16,80,128]{2,1,0:T(8,128)(2,1)S(1)} async-done(((bf16[16,80,128]{2,1,0:T(8,128)(2,1)}), bf16[16,80,128]{2,1,0:T(8,128)(2,1)S(1)}, u32[]{:S(2)}, u32[]{:S(2)}) %all-to-all-start.2) | async-done | bytes 327712 | tf_op jit(solution)/shard_map/all_to_all | solution.py:292
  64.9 0.0 copy-start.2
  64.9 0.7 copy-done.2
  65.6 4.1 %shard_map.62 = (f32[32,128]{1,0:T(8,128)}, f32[32,32]{1,0:T(8,128)}, f32[32,8]{1,0:T(8,128)}, f32[32,32]{1,0:T(8,128)}, f32[32,2]{1,0:T(8,128)}, /*index=5*/f32[32,32,128]{2,1,0:T(8,128)}) custom-call(s32[1]{0:T(128)} %bitcast.refs_0_, bf16[16,80,128]{2,1,0:T(8,128)(2,1)} %copy-done.2, f32[32,32]{1,0:T(8,128)} %shard_map.59.gram_ref.refs_2_, ...), custom_call_target="tpu_custom_call" | custom-call | tf_op jit(solution)/shard_map/pallas_call | solution.py:100
  69.6 10.2 %all-to-all-start.3 = ((f32[32,32,128]{2,1,0:T(8,128)}), f32[32,32,128]{2,1,0:T(8,128)S(1)}, u32[]{:S(2)}, u32[]{:S(2)}) async-start(f32[32,32,128]{2,1,0:T(8,128)} %get-tuple-element.22), calls=%async_computation.3 | async-start | bytes 1048576 | tf_op jit(solution)/shard_map/all_to_all | solution.py:309
  79.8 3.0 %shard_map.63.refs_1_ = f32[32,32]{1,0:T(8,128)} custom-call(f32[32,32]{1,0:T(8,128)} %get-tuple-element.23.left_ref, f32[32,32]{1,0:T(8,128)} %get-tuple-element.24.right_ref.trial_gram_ref), custom_call_target="tpu_custom_call" | custom-call | tf_op jit(solution)/shard_map/pallas_call | solution.py:100
  82.8 8.5 %all-to-all-done.3.refs_0_ = f32[32,32,128]{2,1,0:T(8,128)S(1)} async-done(((f32[32,32,128]{2,1,0:T(8,128)}), f32[32,32,128]{2,1,0:T(8,128)S(1)}, u32[]{:S(2)}, u32[]{:S(2)}) %all-to-all-start.3) | async-done | bytes 524320 | tf_op jit(solution)/shard_map/all_to_all | solution.py:309
  91.3 0.0 copy-start.1
  91.3 0.8 copy-done.1
  92.1 2.5 %shard_map.64 = (f32[32,1024]{1,0:T(8,128)}, f32[4,64,128]{2,1,0:T(8,128)}) custom-call(f32[32,32,128]{2,1,0:T(8,128)} %copy-done.1, f32[32,32]{1,0:T(8,128)} %shard_map.63.refs_1_, bf16[2,128,1024]{2,1,0:T(8,128)(2,1)} %tensor_ref.5), custom_call_target="tpu_custom_call" | custom-call | tf_op jit(solution)/shard_map/pallas_call | solution.py:100
  94.6 3.3 %all-to-all-start.4 = ((f32[4,64,128]{2,1,0:T(8,128)}), f32[4,64,128]{2,1,0:T(8,128)S(1)}, u32[]{:S(2)}, u32[]{:S(2)}) async-start(f32[4,64,128]{2,1,0:T(8,128)} %get-tuple-element.25), calls=%async_computation.4 | async-start | bytes 262144 | tf_op jit(solution)/shard_map/all_to_all | solution.py:326
  97.9 3.4 %shard_map.65 = (f32[32,32]{1,0:T(8,128)}, f32[32,32]{1,0:T(8,128)}) custom-call(f32[32,1024]{1,0:T(8,128)} %get-tuple-element.27.time_ref, f32[32,32]{1,0:T(8,128)} %get-tuple-element.24.right_ref.trial_gram_ref), custom_call_target="tpu_custom_call" | custom-call | tf_op jit(solution)/shard_map/pallas_call | solution.py:100
  101.4 1.4 all-to-all-done.4.shared_ref
  102.7 0.0 copy-start.4
  102.7 0.6 copy-done.4
  103.4 2.4 %shard_map.66 = (f32[32,128]{1,0:T(8,128)}, f32[8,72,128]{2,1,0:T(8,128)}) custom-call(f32[4,64,128]{2,1,0:T(8,128)} %copy-done.4, f32[32,8]{1,0:T(8,128)} %get-tuple-element.26.trial_ref, f32[32,32]{1,0:T(8,128)} %get-tuple-element.28.inverse_ref, bf16[2,128,1024]{2,1,0:T(8,128)(2,1)} %tensor_ref.5), custom_call_target="tpu_custom_call" | custom-call | tf_op jit(solution)/shard_map/pallas_call | solution.py:100
  105.8 12.9 %all_to_all.41.got_ref = f32[8,72,128]{2,1,0:T(8,128)} all-to-all(f32[8,72,128]{2,1,0:T(8,128)} %get-tuple-element.29), channel_id=1, replica_groups=mesh['z'=16,'y'=4,'core'=2,'x'=4] {'y','core'}, dimensions={0} | all-to-all | bytes 589824 | tf_op jit(solution)/shard_map/all_to_all | solution.py:290
  118.7 1.7 %shard_map.67 = bf16[16,80,128]{2,1,0:T(8,128)(2,1)} custom-call(f32[8,72,128]{2,1,0:T(8,128)} %all_to_all.41.got_ref), custom_call_target="tpu_custom_call" | custom-call | tf_op jit(solution)/shard_map/pallas_call | solution.py:100
  120.4 21.1 %all_to_all.42.refs_1_ = bf16[16,80,128]{2,1,0:T(8,128)(2,1)} all-to-all(bf16[16,80,128]{2,1,0:T(8,128)(2,1)} %shard_map.67), channel_id=1, replica_groups=mesh['z'=16,'y'=4,'core'=2,'x'=4] {'z'}, dimensions={0} | all-to-all | bytes 655360 | tf_op jit(solution)/shard_map/all_to_all | solution.py:292
  141.5 4.0 %shard_map.68 = (f32[32,128]{1,0:T(8,128)}, f32[32,32]{1,0:T(8,128)}, f32[32,8]{1,0:T(8,128)}, f32[32,32]{1,0:T(8,128)}, f32[32,2]{1,0:T(8,128)}, /*index=5*/f32[32,32,128]{2,1,0:T(8,128)}) custom-call(s32[1]{0:T(128)} %bitcast.refs_0_, bf16[16,80,128]{2,1,0:T(8,128)(2,1)} %all_to_all.42.refs_1_, f32[32,32]{1,0:T(8,128)} %get-tuple-element.30.refs_2_, ...), custom_call_target="tpu_custom_call" | custom-call | tf_op jit(solution)/shard_map/pallas_call | solution.py:100
  145.6 10.2 %all-to-all-start.7 = ((f32[32,32,128]{2,1,0:T(8,128)}), f32[32,32,128]{2,1,0:T(8,128)S(1)}, u32[]{:S(2)}, u32[]{:S(2)}) async-start(f32[32,32,128]{2,1,0:T(8,128)} %get-tuple-element.33), calls=%async_computation.7 | async-start | bytes 1048576 | tf_op jit(solution)/shard_map/all_to_all | solution.py:309
  155.8 0.0 copy-start.5
  155.8 0.7 copy-done.5
  156.5 0.6 copy.8
  157.1 3.0 %shard_map.69.refs_1_ = f32[32,32]{1,0:T(8,128)} custom-call(f32[32,32]{1,0:T(8,128)} %get-tuple-element.34.left_ref, f32[32,32]{1,0:T(8,128)} %get-tuple-element.35.right_ref), custom_call_target="tpu_custom_call" | custom-call | tf_op jit(solution)/shard_map/pallas_call | solution.py:100
  160.1 7.1 %all-to-all-done.7.refs_0_ = f32[32,32,128]{2,1,0:T(8,128)S(1)} async-done(((f32[32,32,128]{2,1,0:T(8,128)}), f32[32,32,128]{2,1,0:T(8,128)S(1)}, u32[]{:S(2)}, u32[]{:S(2)}) %all-to-all-start.7) | async-done | bytes 524320 | tf_op jit(solution)/shard_map/all_to_all | solution.py:309
  167.3 0.0 copy-start
  167.3 0.8 copy-done
  168.1 2.1 %shard_map.70 = f32[32,1024]{1,0:T(8,128)} custom-call(f32[32,32,128]{2,1,0:T(8,128)} %copy-done, f32[32,32]{1,0:T(8,128)} %shard_map.69.refs_1_), custom_call_target="tpu_custom_call" | custom-call | tf_op jit(solution)/shard_map/pallas_call | solution.py:100
  170.1 0.8 constant_dynamic-slice_fusion
  170.9 0.6 copy.7
Async XLA Ops:
  4.1 10.0 %all-to-all-start = ((f32[4,96,128]{2,1,0:T(8,128)}), f32[4,96,128]{2,1,0:T(8,128)S(1)}, u32[]{:S(2)}, u32[]{:S(2)}) async-start(f32[4,96,128]{2,1,0:T(8,128)} %shard_map.58), calls=%async_computation | async-start | bytes 393216 | tf_op jit(solution)/shard_map/all_to_all | solution.py:286
  14.1 0.7 copy-start.3
  38.5 26.4 %all-to-all-start.2 = ((bf16[16,80,128]{2,1,0:T(8,128)(2,1)}), bf16[16,80,128]{2,1,0:T(8,128)(2,1)S(1)}, u32[]{:S(2)}, u32[]{:S(2)}) async-start(bf16[16,80,128]{2,1,0:T(8,128)(2,1)} %shard_map.61), calls=%async_computation.2 | async-start | bytes 655360 | tf_op jit(solution)/shard_map/all_to_all | solution.py:292
  64.9 0.7 copy-start.2
  69.6 21.7 %all-to-all-start.3 = ((f32[32,32,128]{2,1,0:T(8,128)}), f32[32,32,128]{2,1,0:T(8,128)S(1)}, u32[]{:S(2)}, u32[]{:S(2)}) async-start(f32[32,32,128]{2,1,0:T(8,128)} %get-tuple-element.22), calls=%async_computation.3 | async-start | bytes 1048576 | tf_op jit(solution)/shard_map/all_to_all | solution.py:309
  91.3 0.8 copy-start.1
  94.6 8.1 %all-to-all-start.4 = ((f32[4,64,128]{2,1,0:T(8,128)}), f32[4,64,128]{2,1,0:T(8,128)S(1)}, u32[]{:S(2)}, u32[]{:S(2)}) async-start(f32[4,64,128]{2,1,0:T(8,128)} %get-tuple-element.25), calls=%async_computation.4 | async-start | bytes 262144 | tf_op jit(solution)/shard_map/all_to_all | solution.py:326
  102.7 0.6 copy-start.4
  145.6 21.7 %all-to-all-start.7 = ((f32[32,32,128]{2,1,0:T(8,128)}), f32[32,32,128]{2,1,0:T(8,128)S(1)}, u32[]{:S(2)}, u32[]{:S(2)}) async-start(f32[32,32,128]{2,1,0:T(8,128)} %get-tuple-element.33), calls=%async_computation.7 | async-start | bytes 1048576 | tf_op jit(solution)/shard_map/all_to_all | solution.py:309
  155.8 0.7 copy-start.5
  167.3 0.8 copy-start

commit v4 on v3

--- a/solution.py
+++ b/solution.py
@@ -33,6 +33,21 @@
         precision=EXACT,
         preferred_element_type=jnp.float32,
     )
+
+
+def rows_product(left, right):
+    return lax.dot_general(
+        left,
+        right,
+        (((1,), (1,)), ((), ())),
+        precision=EXACT,
+        preferred_element_type=jnp.float32,
+    )
+
+
+def split(values):
+    high = values.astype(WIRE).astype(jnp.float32)
+    return jnp.concatenate([high, values - high], axis=0).astype(WIRE)
 
 
 def eye_of(size):
@@ -92,17 +107,28 @@
     return jnp.where(col_part >= row_part, upper, upper.T), jnp.concatenate(terms, axis=0)
 
 
-def call(body, outs, *args, smem=()):
+def call(body, outs, *args, smem=(), slow=()):
+    single = not isinstance(outs, tuple)
+    listed = (outs,) if single else outs
     specs = [
         pl.BlockSpec(memory_space=pltpu.SMEM if place in smem else pltpu.VMEM)
         for place in range(len(args))
     ]
-    return pl.pallas_call(
+    args = [
+        arg if place in smem else pltpu.with_memory_space_constraint(arg, pltpu.VMEM)
+        for place, arg in enumerate(args)
+    ]
+    shapes = tuple(
+        out if place in slow else pltpu.VMEM(out.shape, out.dtype)
+        for place, out in enumerate(listed)
+    )
+    result = pl.pallas_call(
         body,
-        out_shape=outs,
+        out_shape=shapes,
         in_specs=specs,
-        out_specs=jax.tree.map(lambda out: pl.BlockSpec(memory_space=pltpu.VMEM), outs),
+        out_specs=tuple(pl.BlockSpec(memory_space=pltpu.VMEM) for _ in listed),
     )(*args)
+    return result[0] if single else result
 
 
 def put_projected(time_now, tensor_ref, sent_ref):
@@ -121,11 +147,12 @@
 
 def project_body(time_ref, trial_ref, tensor_ref, sent_ref):
     put_projected(time_ref[...], tensor_ref, sent_ref)
-    size, count = trial_ref.shape
+    count, size = trial_ref.shape
     lanes = sent_ref.shape[2]
-    tile = jnp.concatenate([trial_ref[...], jnp.zeros((size, lanes - count), jnp.float32)], axis=1)
+    tile = jnp.concatenate([trial_ref[...], jnp.zeros((PART - count, size), jnp.float32)], axis=0)
+    tile = jnp.concatenate([tile, jnp.zeros((PART, lanes - size), jnp.float32)], axis=1)
     for member in range(sent_ref.shape[0]):
-        sent_ref[member, tensor_ref.shape[0] * size :, :] = tile
+        sent_ref[member, count * size :, :] = tile
 
 
 def put_neuron(trial_now, inverse, shared_ref, tensor_ref, raw_ref, sent_ref):
@@ -146,11 +173,12 @@
     for trial in range(trial_count):
         one = jnp.sum(raw * projected[trial], axis=1, keepdims=True)
         terms = jnp.where(lane == trial, one, terms)
-    small = pack_small(gram_of(raw), terms)
+    small = split(pack_small(gram_of(raw), terms))
     blocks, rows, width = sent_ref.shape
     rounded = raw.astype(jnp.bfloat16)
     for trial in range(own_trials):
         partial = jnp.dot(rounded, tensor_ref[trial], preferred_element_type=jnp.float32)
+        partial = partial.astype(WIRE)
         for block in range(blocks):
             sent_ref[block, trial * size : (trial + 1) * size, :] = partial[
                 :, block * width : (block + 1) * width
@@ -162,11 +190,12 @@
 def first_neuron_body(shared_ref, gram_ref, tensor_ref, raw_ref, sent_ref):
     own_trials = tensor_ref.shape[0]
     size = raw_ref.shape[0]
-    columns = [
-        shared_ref[member, own_trials * size :, :own_trials]
+    main = own_trials * size
+    lines = [
+        shared_ref[member, main : main + own_trials, :size]
         for member in range(shared_ref.shape[0])
     ]
-    trial_now = jnp.concatenate(columns, axis=1)
+    trial_now = rows_product(eye_of(size), jnp.concatenate(lines, axis=0))
     inverse = damped_inverse(gram_of(trial_now) * gram_ref[...])
     put_neuron(trial_now, inverse, shared_ref, tensor_ref, raw_ref, sent_ref)
 
@@ -176,16 +205,14 @@
 
 
 def reduce_body(got_ref, sent_ref):
-    total = got_ref[0]
+    total = got_ref[0].astype(jnp.float32)
     for member in range(1, got_ref.shape[0]):
-        total = total + got_ref[member]
-    rounded = total.astype(WIRE)
-    main = total.shape[0] - PART
-    small = total[main:]
-    high = small.astype(WIRE).astype(jnp.float32)
-    halves = jnp.concatenate([high, small - high], axis=0).astype(WIRE)
+        total = total + got_ref[member].astype(jnp.float32)
+    main = total.shape[0] - 2 * PART
+    rounded = total[:main].astype(WIRE)
+    halves = split(total[main : main + PART] + total[main + PART :])
     for member in range(sent_ref.shape[0]):
-        sent_ref[member, :main, :] = rounded[:main]
+        sent_ref[member, :main, :] = rounded
         sent_ref[member, main:, :] = halves
 
 
@@ -193,7 +220,7 @@
     neuron_ref, neuron_gram_ref, trial_ref, trial_gram_ref, own_ref, sent_ref = outs
     size = raw_ref.shape[0]
     trial_count = trial_ref.shape[1]
-    own_trials = own_ref.shape[1]
+    own_trials = own_ref.shape[0]
     total = got_ref[0].astype(jnp.float32)
     for member in range(1, got_ref.shape[0]):
         total = total + got_ref[member].astype(jnp.float32)
@@ -210,11 +237,14 @@
     trial_ref[...] = trial_now
     trial_gram_ref[...] = gram_of(trial_now)
     lane = lax.broadcasted_iota(jnp.int32, trial_now.shape, 1)
+    row = lax.broadcasted_iota(jnp.int32, (own_trials, trial_count), 0)
+    column = lax.broadcasted_iota(jnp.int32, (own_trials, trial_count), 1)
+    chosen = (column == plane_ref[0] * own_trials + row).astype(jnp.float32)
+    own_ref[...] = rows_product(chosen, trial_now)
     weighted = None
     for trial in range(own_trials):
         mine = lane == plane_ref[0] * own_trials + trial
         column = jnp.sum(jnp.where(mine, trial_now, 0.0), axis=1, keepdims=True)
-        own_ref[:, trial : trial + 1] = column
         part = column * total[trial * size : (trial + 1) * size]
         weighted = part if weighted is None else weighted + part
     weighted = weighted * down
@@ -254,8 +284,13 @@
     inverse_ref[...] = damped_inverse(gram * trial_gram_ref[...])
 
 
-def last_body(planes, got_ref, inverse_ref, time_ref):
-    time_ref[...] = time_of(planes, got_ref, inverse_ref)
+def last_body(planes, place_ref, got_ref, inverse_ref, time_ref):
+    time_now = time_of(planes, got_ref, inverse_ref)
+    count = time_ref.shape[0]
+    row = lax.broadcasted_iota(jnp.int32, (count, time_now.shape[1]), 0)
+    column = lax.broadcasted_iota(jnp.int32, (count, time_now.shape[1]), 1)
+    chosen = (column == place_ref[0] * count + row).astype(jnp.float32)
+    time_ref[...] = rows_product(chosen, time_now)
 
 
 def per_device(tensor, time_init, trial_init):
@@ -275,12 +310,15 @@
         return jax.ShapeDtypeStruct(dims, kind)
 
     square = shape(components, components)
-    neuron_outs = (shape(components, own_neurons), shape(blocks, main + PART, width))
+    neuron_outs = (
+        shape(components, own_neurons),
+        shape(blocks, main + 2 * PART, width, kind=WIRE),
+    )
     shared = call(
         project_body,
-        shape(planes, main + components, own_neurons),
+        shape(planes, main + PART, own_neurons),
         time_init,
-        trial_init,
+        trial_init.T,
         tensor,
     )
     shared = lax.all_to_all(shared, "x", 0, 0)
@@ -297,7 +335,7 @@
                 square,
                 shape(components, trial_count),
                 square,
-                shape(components, own_trials),
+                shape(own_trials, components),
                 shape(blocks * planes, components, width),
             ),
             plane,
@@ -305,15 +343,20 @@
             time_gram,
             raw,
             smem=(0,),
+            slow=(0, 4) if sweep_index == SWEEPS - 1 else (),
         )
         got = lax.all_to_all(sent, short + ("x",), 0, 0)
         inverse = call(inverse_body, square, neuron_gram, trial_gram)
         if sweep_index == SWEEPS - 1:
-            time_now = call(
+            place = lax.axis_index(("z", "y", "core", "x")).astype(jnp.int32).reshape(1)
+            time_out = call(
                 lambda *refs: last_body(planes, *refs),
-                shape(components, timepoints),
+                shape(timepoints // (layers * blocks * planes), components),
+                place,
                 got,
                 inverse,
+                smem=(0,),
+                slow=(0,),
             )
             break
         time_now, shared = call(
@@ -326,10 +369,7 @@
         shared = lax.all_to_all(shared, "x", 0, 0)
         time_gram, inverse = call(next_inverse_body, (square, square), time_now, trial_gram)
         raw, sent = call(neuron_body, neuron_outs, shared, trial_now, inverse, tensor)
-    position = lax.axis_index(("z", "y", "core", "x"))
-    share_width = timepoints // (layers * blocks * planes)
-    time_out = lax.dynamic_slice_in_dim(time_now, position * share_width, share_width, 1)
-    return (neuron_now, time_out, own_trial)
+    return (neuron_now, time_out.T, own_trial.T)
 
 
 def solution(mesh):

time: 173 us -> 151 us (0.87)
  Pallas kernels: 36 us -> 18.8 us
  blocking collectives: 51.9 us -> 44.9 us
  waiting for transfers between devices: 35.7 us -> 42.2 us
  local copies, waits for them, and re-layouts: 7.76 us -> 2.62 us
    pallas_call x13, Pallas kernels: 36 us -> 18.8 us  [call(): pl.pallas_call(body, out_shape=shapes, in_specs=specs, out_specs=tuple((p...]
    all_to_all x2, blocking collectives: 30.7 us -> 24.1 us  [per_device(): got = lax.all_to_all(sent, short, 0, 0)]
    unnamed x15 -> x8, local copies, waits for them, and re-layouts: 6.97 us -> 2.62 us
    all_to_all x2, waiting for transfers between devices: 15.6 us -> 19.7 us  [per_device(): got = lax.all_to_all(sent, short + ('x',), 0, 0)]
    all_to_all x2, waiting for transfers between devices: 4.77 us -> 7.55 us  [per_device(): shared = lax.all_to_all(shared, 'x', 0, 0)]
  transfers between devices with their start and end apart: 5 -> 5, of which waited for: 5 -> 5; matrix products, arithmetic and copies ran while one was open for 0% -> 0% of each run, Pallas kernels for 7% -> 4%
where the time goes in v4:
time: 151 us; the launch traced here: 150 us
  blocking collectives  44.9 us (30%)
  waiting for transfers between devices  42.2 us (28%)
  starting transfers between devices  41 us (27%)
  Pallas kernels  18.8 us (12%)
  local copies, waits for them, and re-layouts  2.62 us (2%)
    all_to_all x2, blocking collectives, per_device(): got = lax.all_to_all(sent, short, 0, 0)  24.1 us
    all_to_all x1, blocking collectives, per_device(): got = lax.all_to_all(sent, 'z', 0, 0)  20.8 us
    all_to_all x2, starting transfers between devices, per_device(): got = lax.all_to_all(sent, short + ('x',), 0, 0)  20.5 us
    all_to_all x2, waiting for transfers between devices, per_device(): got = lax.all_to_all(sent, short + ('x',), 0, 0)  19.7 us
    pallas_call x13, Pallas kernels, call(): pl.pallas_call(body, out_shape=shapes, in_specs=specs, out_specs=tuple((p...  18.8 us
    all_to_all x1, waiting for transfers between devices, per_device(): got = lax.all_to_all(sent, 'z', 0, 0)  15 us
    all_to_all x1, starting transfers between devices, per_device(): got = lax.all_to_all(sent, 'z', 0, 0)  12.4 us
    all_to_all x2, starting transfers between devices, per_device(): shared = lax.all_to_all(shared, 'x', 0, 0)  8.15 us
  transfers between devices with their start and end apart: 5, of which 5 were waited for; matrix products, arithmetic and copies ran while one was open for 0% of the time, Pallas kernels for 4%

profile of v4, /device:TPU:1, one launch (start us, length us, event | category | flops | bytes accessed | tf_op | source)
XLA Modules:
  0.0 150.3 jit_solution(1696636875613829017)
XLA Ops:
  0.6 0.0 copy-start.3
  0.6 0.7 copy-done.3
  1.3 0.0 copy-start
  1.3 1.0 copy-done
  2.4 0.0 copy-start.2
  2.4 0.9 copy-done.2
  3.3 0.0 copy-start.1
  3.3 0.9 shard_map.58
  4.2 4.8 %all-to-all-start = ((f32[4,72,128]{2,1,0:T(8,128)}), f32[4,72,128]{2,1,0:T(8,128)S(1)}, u32[]{:S(2)}, u32[]{:S(2)}) async-start(f32[4,72,128]{2,1,0:T(8,128)} %shard_map.58), calls=%async_computation | async-start | bytes 294912 | tf_op jit(solution)/shard_map/all_to_all | solution.py:324
  9.0 0.2 shard_map.59.gram_ref.refs_2_
  9.3 4.7 %all-to-all-done.shared_ref = f32[4,72,128]{2,1,0:T(8,128)S(1)} async-done(((f32[4,72,128]{2,1,0:T(8,128)}), f32[4,72,128]{2,1,0:T(8,128)S(1)}, u32[]{:S(2)}, u32[]{:S(2)}) %all-to-all-start) | async-done | bytes 147488 | tf_op jit(solution)/shard_map/all_to_all | solution.py:324
  13.9 0.0 copy-done.1
  13.9 2.4 %shard_map.60 = (f32[32,128]{1,0:T(8,128)S(1)}, bf16[8,80,128]{2,1,0:T(8,128)(2,1)S(1)}) custom-call(f32[4,72,128]{2,1,0:T(8,128)S(1)} %all-to-all-done.shared_ref, f32[32,32]{1,0:T(8,128)S(1)} %shard_map.59.gram_ref.refs_2_, bf16[2,128,1024]{2,1,0:T(8,128)(2,1)S(1)} %copy-done.1), custom_call_target="tpu_custom_call" | custom-call | tf_op jit(solution)/shard_map/pallas_call | solution.py:125
  16.4 14.4 %all_to_all.40.got_ref = bf16[8,80,128]{2,1,0:T(8,128)(2,1)S(1)} all-to-all(bf16[8,80,128]{2,1,0:T(8,128)(2,1)S(1)} %get-tuple-element.20), channel_id=1, replica_groups=mesh['z'=16,'y'=4,'core'=2,'x'=4] {'y','core'}, dimensions={0} | all-to-all | bytes 327680 | tf_op jit(solution)/shard_map/all_to_all | solution.py:328
  30.8 0.8 shard_map.61
  31.5 12.4 %all-to-all-start.2 = ((bf16[16,80,128]{2,1,0:T(8,128)(2,1)}), bf16[16,80,128]{2,1,0:T(8,128)(2,1)S(1)}, u32[]{:S(2)}, u32[]{:S(2)}) async-start(bf16[16,80,128]{2,1,0:T(8,128)(2,1)} %shard_map.61), calls=%async_computation.2 | async-start | bytes 655360 | tf_op jit(solution)/shard_map/all_to_all | solution.py:330
  44.0 15.0 %all-to-all-done.2.refs_1_ = bf16[16,80,128]{2,1,0:T(8,128)(2,1)S(1)} async-done(((bf16[16,80,128]{2,1,0:T(8,128)(2,1)}), bf16[16,80,128]{2,1,0:T(8,128)(2,1)S(1)}, u32[]{:S(2)}, u32[]{:S(2)}) %all-to-all-start.2) | async-done | bytes 327712 | tf_op jit(solution)/shard_map/all_to_all | solution.py:330
  59.0 3.1 %shard_map.62 = (f32[32,128]{1,0:T(8,128)}, f32[32,32]{1,0:T(8,128)S(1)}, f32[32,8]{1,0:T(8,128)S(1)}, f32[32,32]{1,0:T(8,128)S(1)}, f32[2,32]{1,0:T(2,128)}, /*index=5*/f32[32,32,128]{2,1,0:T(8,128)}) custom-call(s32[1]{0:T(128)} %bitcast.refs_0_, bf16[16,80,128]{2,1,0:T(8,128)(2,1)S(1)} %all-to-all-done.2.refs_1_, ...), custom_call_target="tpu_custom_call" | custom-call | tf_op jit(solution)/shard_map/pallas_call | solution.py:125
  62.1 10.2 %all-to-all-start.3 = ((f32[32,32,128]{2,1,0:T(8,128)}), f32[32,32,128]{2,1,0:T(8,128)S(1)}, u32[]{:S(2)}, u32[]{:S(2)}) async-start(f32[32,32,128]{2,1,0:T(8,128)} %get-tuple-element.22), calls=%async_computation.3 | async-start | bytes 1048576 | tf_op jit(solution)/shard_map/all_to_all | solution.py:348
  72.3 1.7 %shard_map.63.refs_1_ = f32[32,32]{1,0:T(8,128)S(1)} custom-call(f32[32,32]{1,0:T(8,128)S(1)} %get-tuple-element.23.left_ref, f32[32,32]{1,0:T(8,128)S(1)} %get-tuple-element.24.right_ref.trial_gram_ref), custom_call_target="tpu_custom_call" | custom-call | tf_op jit(solution)/shard_map/pallas_call | solution.py:125
  74.0 9.8 %all-to-all-done.3.refs_0_ = f32[32,32,128]{2,1,0:T(8,128)S(1)} async-done(((f32[32,32,128]{2,1,0:T(8,128)}), f32[32,32,128]{2,1,0:T(8,128)S(1)}, u32[]{:S(2)}, u32[]{:S(2)}) %all-to-all-start.3) | async-done | bytes 524320 | tf_op jit(solution)/shard_map/all_to_all | solution.py:348
  83.8 1.3 shard_map.64
  85.1 3.3 %all-to-all-start.4 = ((f32[4,64,128]{2,1,0:T(8,128)}), f32[4,64,128]{2,1,0:T(8,128)S(1)}, u32[]{:S(2)}, u32[]{:S(2)}) async-start(f32[4,64,128]{2,1,0:T(8,128)} %get-tuple-element.25), calls=%async_computation.4 | async-start | bytes 262144 | tf_op jit(solution)/shard_map/all_to_all | solution.py:369
  88.4 1.9 %shard_map.65 = (f32[32,32]{1,0:T(8,128)S(1)}, f32[32,32]{1,0:T(8,128)S(1)}) custom-call(f32[32,1024]{1,0:T(8,128)S(1)} %get-tuple-element.27.time_ref, f32[32,32]{1,0:T(8,128)S(1)} %get-tuple-element.24.right_ref.trial_gram_ref), custom_call_target="tpu_custom_call" | custom-call | tf_op jit(solution)/shard_map/pallas_call | solution.py:125
  90.3 2.9 %all-to-all-done.4.shared_ref = f32[4,64,128]{2,1,0:T(8,128)S(1)} async-done(((f32[4,64,128]{2,1,0:T(8,128)}), f32[4,64,128]{2,1,0:T(8,128)S(1)}, u32[]{:S(2)}, u32[]{:S(2)}) %all-to-all-start.4) | async-done | bytes 131104 | tf_op jit(solution)/shard_map/all_to_all | solution.py:369
  93.2 0.5 shard_map.66
  93.7 9.7 %all_to_all.41.got_ref = bf16[8,80,128]{2,1,0:T(8,128)(2,1)S(1)} all-to-all(bf16[8,80,128]{2,1,0:T(8,128)(2,1)S(1)} %get-tuple-element.29), channel_id=1, replica_groups=mesh['z'=16,'y'=4,'core'=2,'x'=4] {'y','core'}, dimensions={0} | all-to-all | bytes 327680 | tf_op jit(solution)/shard_map/all_to_all | solution.py:328
  103.5 20.8 %all_to_all.42.refs_1_ = bf16[16,80,128]{2,1,0:T(8,128)(2,1)S(1)} all-to-all(bf16[16,80,128]{2,1,0:T(8,128)(2,1)S(1)} %shard_map.67), channel_id=1, replica_groups=mesh['z'=16,'y'=4,'core'=2,'x'=4] {'z'}, dimensions={0} | all-to-all | bytes 655360 | tf_op jit(solution)/shard_map/all_to_all | solution.py:330
  124.3 3.0 %shard_map.68 = (f32[32,128]{1,0:T(8,128)}, f32[32,32]{1,0:T(8,128)S(1)}, f32[32,8]{1,0:T(8,128)}, f32[32,32]{1,0:T(8,128)S(1)}, f32[2,32]{1,0:T(2,128)}, /*index=5*/f32[32,32,128]{2,1,0:T(8,128)}) custom-call(s32[1]{0:T(128)} %bitcast.refs_0_, bf16[16,80,128]{2,1,0:T(8,128)(2,1)S(1)} %all_to_all.42.refs_1_, f32[32,32]{1,0:T(8,128)S(1)} %get-tuple-element.30.refs_2_, ...), custom_call_target="tpu_custom_call" | custom-call | tf_op jit(solution)/shard_map/pallas_call | solution.py:125
  127.3 10.2 %all-to-all-start.7 = ((f32[32,32,128]{2,1,0:T(8,128)}), f32[32,32,128]{2,1,0:T(8,128)S(1)}, u32[]{:S(2)}, u32[]{:S(2)}) async-start(f32[32,32,128]{2,1,0:T(8,128)} %get-tuple-element.33), calls=%async_computation.7 | async-start | bytes 1048576 | tf_op jit(solution)/shard_map/all_to_all | solution.py:348
  137.5 1.7 %shard_map.69.refs_2_ = f32[32,32]{1,0:T(8,128)S(1)} custom-call(f32[32,32]{1,0:T(8,128)S(1)} %get-tuple-element.34.left_ref, f32[32,32]{1,0:T(8,128)S(1)} %get-tuple-element.35.right_ref), custom_call_target="tpu_custom_call" | custom-call | tf_op jit(solution)/shard_map/pallas_call | solution.py:125
  139.2 9.8 %all-to-all-done.7.refs_1_ = f32[32,32,128]{2,1,0:T(8,128)S(1)} async-done(((f32[32,32,128]{2,1,0:T(8,128)}), f32[32,32,128]{2,1,0:T(8,128)S(1)}, u32[]{:S(2)}, u32[]{:S(2)}) %all-to-all-start.7) | async-done | bytes 524320 | tf_op jit(solution)/shard_map/all_to_all | solution.py:348
  149.0 1.3 shard_map.70
  (1 shorter events, 0.0 us)
Async XLA Ops:
  0.6 0.7 copy-start.3
  1.3 1.0 copy-start
  2.4 0.9 copy-start.2
  3.3 10.7 %copy-start.1 = (bf16[2,128,1024]{2,1,0:T(8,128)(2,1)S(1)}, bf16[2,128,1024]{2,1,0:T(8,128)(2,1)}, u32[]{:S(2)}) copy-start(bf16[2,128,1024]{2,1,0:T(8,128)(2,1)} %tensor_ref.5) | copy-start | bytes 1572868
  4.2 9.7 %all-to-all-start = ((f32[4,72,128]{2,1,0:T(8,128)}), f32[4,72,128]{2,1,0:T(8,128)S(1)}, u32[]{:S(2)}, u32[]{:S(2)}) async-start(f32[4,72,128]{2,1,0:T(8,128)} %shard_map.58), calls=%async_computation | async-start | bytes 294912 | tf_op jit(solution)/shard_map/all_to_all | solution.py:324
  31.5 27.5 %all-to-all-start.2 = ((bf16[16,80,128]{2,1,0:T(8,128)(2,1)}), bf16[16,80,128]{2,1,0:T(8,128)(2,1)S(1)}, u32[]{:S(2)}, u32[]{:S(2)}) async-start(bf16[16,80,128]{2,1,0:T(8,128)(2,1)} %shard_map.61), calls=%async_computation.2 | async-start | bytes 655360 | tf_op jit(solution)/shard_map/all_to_all | solution.py:330
  62.1 21.8 %all-to-all-start.3 = ((f32[32,32,128]{2,1,0:T(8,128)}), f32[32,32,128]{2,1,0:T(8,128)S(1)}, u32[]{:S(2)}, u32[]{:S(2)}) async-start(f32[32,32,128]{2,1,0:T(8,128)} %get-tuple-element.22), calls=%async_computation.3 | async-start | bytes 1048576 | tf_op jit(solution)/shard_map/all_to_all | solution.py:348
  85.1 8.1 %all-to-all-start.4 = ((f32[4,64,128]{2,1,0:T(8,128)}), f32[4,64,128]{2,1,0:T(8,128)S(1)}, u32[]{:S(2)}, u32[]{:S(2)}) async-start(f32[4,64,128]{2,1,0:T(8,128)} %get-tuple-element.25), calls=%async_computation.4 | async-start | bytes 262144 | tf_op jit(solution)/shard_map/all_to_all | solution.py:369
  127.3 21.8 %all-to-all-start.7 = ((f32[32,32,128]{2,1,0:T(8,128)}), f32[32,32,128]{2,1,0:T(8,128)S(1)}, u32[]{:S(2)}, u32[]{:S(2)}) async-start(f32[32,32,128]{2,1,0:T(8,128)} %get-tuple-element.33), calls=%async_computation.7 | async-start | bytes 1048576 | tf_op jit(solution)/shard_map/all_to_all | solution.py:348

commit v5 on v4

--- a/solution.py
+++ b/solution.py
@@ -107,15 +107,11 @@
     return jnp.where(col_part >= row_part, upper, upper.T), jnp.concatenate(terms, axis=0)
 
 
-def call(body, outs, *args, smem=(), slow=()):
+def call(body, outs, *args, away=(), slow=()):
     single = not isinstance(outs, tuple)
     listed = (outs,) if single else outs
-    specs = [
-        pl.BlockSpec(memory_space=pltpu.SMEM if place in smem else pltpu.VMEM)
-        for place in range(len(args))
-    ]
     args = [
-        arg if place in smem else pltpu.with_memory_space_constraint(arg, pltpu.VMEM)
+        arg if place in away else pltpu.with_memory_space_constraint(arg, pltpu.VMEM)
         for place, arg in enumerate(args)
     ]
     shapes = tuple(
@@ -125,7 +121,7 @@
     result = pl.pallas_call(
         body,
         out_shape=shapes,
-        in_specs=specs,
+        in_specs=[pl.BlockSpec(memory_space=pltpu.VMEM) for _ in args],
         out_specs=tuple(pl.BlockSpec(memory_space=pltpu.VMEM) for _ in listed),
     )(*args)
     return result[0] if single else result
@@ -174,17 +170,19 @@
         one = jnp.sum(raw * projected[trial], axis=1, keepdims=True)
         terms = jnp.where(lane == trial, one, terms)
     small = split(pack_small(gram_of(raw), terms))
-    blocks, rows, width = sent_ref.shape
+    members, rows, width = sent_ref.shape
+    blocks = tensor_ref.shape[2] // width
     rounded = raw.astype(jnp.bfloat16)
     for trial in range(own_trials):
         partial = jnp.dot(rounded, tensor_ref[trial], preferred_element_type=jnp.float32)
         partial = partial.astype(WIRE)
-        for block in range(blocks):
-            sent_ref[block, trial * size : (trial + 1) * size, :] = partial[
-                :, block * width : (block + 1) * width
+        for member in range(members):
+            start = member % blocks * width
+            sent_ref[member, trial * size : (trial + 1) * size, :] = partial[
+                :, start : start + width
             ]
-    for block in range(blocks):
-        sent_ref[block, own_trials * size :, :] = small
+    for member in range(members):
+        sent_ref[member, own_trials * size :, :] = small
 
 
 def first_neuron_body(shared_ref, gram_ref, tensor_ref, raw_ref, sent_ref):
@@ -216,11 +214,12 @@
         sent_ref[member, main:, :] = halves
 
 
-def finish_body(neuron_count, plane_ref, got_ref, gram_ref, raw_ref, *outs):
+def finish_body(neuron_count, got_ref, gram_ref, raw_ref, *outs):
     neuron_ref, neuron_gram_ref, trial_ref, trial_gram_ref, own_ref, sent_ref = outs
     size = raw_ref.shape[0]
     trial_count = trial_ref.shape[1]
     own_trials = own_ref.shape[0]
+    plane = lax.axis_index("x")
     total = got_ref[0].astype(jnp.float32)
     for member in range(1, got_ref.shape[0]):
         total = total + got_ref[member].astype(jnp.float32)
@@ -239,11 +238,11 @@
     lane = lax.broadcasted_iota(jnp.int32, trial_now.shape, 1)
     row = lax.broadcasted_iota(jnp.int32, (own_trials, trial_count), 0)
     column = lax.broadcasted_iota(jnp.int32, (own_trials, trial_count), 1)
-    chosen = (column == plane_ref[0] * own_trials + row).astype(jnp.float32)
+    chosen = (column == plane * own_trials + row).astype(jnp.float32)
     own_ref[...] = rows_product(chosen, trial_now)
     weighted = None
     for trial in range(own_trials):
-        mine = lane == plane_ref[0] * own_trials + trial
+        mine = lane == plane * own_trials + trial
         column = jnp.sum(jnp.where(mine, trial_now, 0.0), axis=1, keepdims=True)
         part = column * total[trial * size : (trial + 1) * size]
         weighted = part if weighted is None else weighted + part
@@ -284,12 +283,12 @@
     inverse_ref[...] = damped_inverse(gram * trial_gram_ref[...])
 
 
-def last_body(planes, place_ref, got_ref, inverse_ref, time_ref):
+def last_body(planes, got_ref, inverse_ref, time_ref):
     time_now = time_of(planes, got_ref, inverse_ref)
     count = time_ref.shape[0]
     row = lax.broadcasted_iota(jnp.int32, (count, time_now.shape[1]), 0)
     column = lax.broadcasted_iota(jnp.int32, (count, time_now.shape[1]), 1)
-    chosen = (column == place_ref[0] * count + row).astype(jnp.float32)
+    chosen = (column == lax.axis_index(("z", "pair", "y", "core", "x")) * count + row).astype(jnp.float32)
     time_ref[...] = rows_product(chosen, time_now)
 
 
@@ -298,13 +297,13 @@
     components = time_init.shape[0]
     planes = lax.axis_size("x")
     short = ("y", "core")
-    blocks = lax.axis_size(short)
-    layers = lax.axis_size("z")
-    neuron_count = own_neurons * blocks * layers
+    near = ("pair",) + short
+    blocks, layers = lax.axis_size(short), lax.axis_size("z")
+    twins = lax.axis_size("pair")
+    neuron_count = own_neurons * blocks * twins * layers
     trial_count = own_trials * planes
     width = timepoints // blocks
     main = own_trials * components
-    plane = lax.axis_index("x").astype(jnp.int32).reshape(1)
 
     def shape(*dims, kind=jnp.float32):
         return jax.ShapeDtypeStruct(dims, kind)
@@ -312,7 +311,7 @@
     square = shape(components, components)
     neuron_outs = (
         shape(components, own_neurons),
-        shape(blocks, main + 2 * PART, width, kind=WIRE),
+        shape(twins * blocks, main + 2 * PART, width, kind=WIRE),
     )
     shared = call(
         project_body,
@@ -320,12 +319,13 @@
         time_init,
         trial_init.T,
         tensor,
+        away=(0, 1, 2),
     )
     shared = lax.all_to_all(shared, "x", 0, 0)
     time_gram = call(gram_body, square, time_init)
     raw, sent = call(first_neuron_body, neuron_outs, shared, time_gram, tensor)
     for sweep_index in range(SWEEPS):
-        got = lax.all_to_all(sent, short, 0, 0)
+        got = lax.all_to_all(sent, near, 0, 0)
         sent = call(reduce_body, shape(layers, main + 2 * PART, width, kind=WIRE), got)
         got = lax.all_to_all(sent, "z", 0, 0)
         neuron_now, neuron_gram, trial_now, trial_gram, own_trial, sent = call(
@@ -338,24 +338,19 @@
                 shape(own_trials, components),
                 shape(blocks * planes, components, width),
             ),
-            plane,
             got,
             time_gram,
             raw,
-            smem=(0,),
             slow=(0, 4) if sweep_index == SWEEPS - 1 else (),
         )
         got = lax.all_to_all(sent, short + ("x",), 0, 0)
         inverse = call(inverse_body, square, neuron_gram, trial_gram)
         if sweep_index == SWEEPS - 1:
-            place = lax.axis_index(("z", "y", "core", "x")).astype(jnp.int32).reshape(1)
             time_out = call(
                 lambda *refs: last_body(planes, *refs),
-                shape(timepoints // (layers * blocks * planes), components),
-                place,
+                shape(timepoints // (layers * twins * blocks * planes), components),
                 got,
                 inverse,
-                smem=(0,),
                 slow=(0,),
             )
             break
@@ -374,11 +369,11 @@
 
 def solution(mesh):
     neuron, trial = mesh.shape["neuron"], mesh.shape["trial"]
-    layers = max(neuron // 8, 1)
+    layers = neuron // 16
     fine = Mesh(
-        mesh.devices.reshape(layers, neuron // layers // 2, 2, trial), ("z", "y", "core", "x")
-    )
-    rows = ("z", "y", "core")
+        mesh.devices.reshape(layers, 2, 4, 2, trial), ("z", "pair", "y", "core", "x")
+    )
+    rows = ("z", "pair", "y", "core")
     return jax.shard_map(
         per_device,
         mesh=fine,

time: 151 us -> 144 us (0.954)
  blocking collectives: 44.9 us -> 71.6 us
  starting transfers between devices: 41 us -> 24.3 us
  waiting for transfers between devices: 42.2 us -> 27.2 us
  local copies, waits for them, and re-layouts: 2.62 us -> 0.01 us
    all_to_all x1 -> x2, blocking collectives: 20.8 us -> 43.1 us  [per_device(): got = lax.all_to_all(sent, 'z', 0, 0)]
    all_to_all x1 -> x0, waiting for transfers between devices: 15 us -> none  [per_device(): got = lax.all_to_all(sent, 'z', 0, 0)]
    all_to_all x1 -> x0, starting transfers between devices: 12.4 us -> none  [per_device(): got = lax.all_to_all(sent, 'z', 0, 0)]
    all_to_all x2, starting transfers between devices: 20.5 us -> 16 us  [per_device(): got = lax.all_to_all(sent, short + ('x',), 0, 0)]
    all_to_all x2, blocking collectives: 24.1 us -> 28.5 us  [per_device(): got = lax.all_to_all(sent, near, 0, 0)]
    unnamed x8 -> x4, local copies, waits for them, and re-layouts: 2.62 us -> 0.01 us
  transfers between devices with their start and end apart: 5 -> 4, of which waited for: 5 -> 4; matrix products, arithmetic and copies ran while one was open for 0% -> 0% of each run, Pallas kernels for 4% -> 4%
where the time goes in v5:
time: 144 us; the launch traced here: 143 us
  blocking collectives  71.6 us (50%)
  waiting for transfers between devices  27.2 us (19%)
  starting transfers between devices  24.3 us (17%)
  Pallas kernels  19.3 us (13%)
    all_to_all x2, blocking collectives, per_device(): got = lax.all_to_all(sent, 'z', 0, 0)  43.1 us
    all_to_all x2, blocking collectives, per_device(): got = lax.all_to_all(sent, near, 0, 0)  28.5 us
    all_to_all x2, waiting for transfers between devices, per_device(): got = lax.all_to_all(sent, short + ('x',), 0, 0)  19.7 us
    pallas_call x13, Pallas kernels, call(): pl.pallas_call(body, out_shape=shapes, in_specs=[pl.BlockSpec(memory_spac...  19.3 us
    all_to_all x2, starting transfers between devices, per_device(): got = lax.all_to_all(sent, short + ('x',), 0, 0)  16 us
    all_to_all x2, starting transfers between devices, per_device(): shared = lax.all_to_all(shared, 'x', 0, 0)  8.29 us
    all_to_all x2, waiting for transfers between devices, per_device(): shared = lax.all_to_all(shared, 'x', 0, 0)  7.54 us
  transfers between devices with their start and end apart: 4, of which 4 were waited for; matrix products, arithmetic and copies ran while one was open for 0% of the time, Pallas kernels for 4%

profile of v5, /device:TPU:1, one launch (start us, length us, event | category | flops | bytes accessed | tf_op | source)
XLA Modules:
  0.0 143.0 jit_solution(6531393591669936398)
XLA Ops:
  0.6 0.0 copy-start
  0.6 2.1 %shard_map.58 = f32[4,72,128]{2,1,0:T(8,128)} custom-call(f32[32,1024]{1,0:T(8,128)} %time_ref.3, f32[2,32]{1,0:T(2,128)} %bitcast.3, bf16[2,128,1024]{2,1,0:T(8,128)(2,1)} %tensor_ref.5), custom_call_target="tpu_custom_call" | custom-call | tf_op jit(solution)/shard_map/pallas_call | solution.py:121
  2.8 0.0 copy-start.1
  2.8 5.0 %all-to-all-start = ((f32[4,72,128]{2,1,0:T(8,128)}), f32[4,72,128]{2,1,0:T(8,128)S(1)}, u32[]{:S(2)}, u32[]{:S(2)}) async-start(f32[4,72,128]{2,1,0:T(8,128)} %shard_map.58), calls=%async_computation | async-start | bytes 294912 | tf_op jit(solution)/shard_map/all_to_all | solution.py:324
  7.7 0.0 copy-done.1
  7.7 0.2 shard_map.59.gram_ref.refs_1_
  8.0 4.7 %all-to-all-done.shared_ref = f32[4,72,128]{2,1,0:T(8,128)S(1)} async-done(((f32[4,72,128]{2,1,0:T(8,128)}), f32[4,72,128]{2,1,0:T(8,128)S(1)}, u32[]{:S(2)}, u32[]{:S(2)}) %all-to-all-start) | async-done | bytes 147488 | tf_op jit(solution)/shard_map/all_to_all | solution.py:324
  12.6 0.0 copy-done
  12.6 2.4 %shard_map.60 = (f32[32,128]{1,0:T(8,128)S(1)}, bf16[16,80,128]{2,1,0:T(8,128)(2,1)S(1)}) custom-call(f32[4,72,128]{2,1,0:T(8,128)S(1)} %all-to-all-done.shared_ref, f32[32,32]{1,0:T(8,128)S(1)} %shard_map.59.gram_ref.refs_1_, bf16[2,128,1024]{2,1,0:T(8,128)(2,1)S(1)} %copy-done), custom_call_target="tpu_custom_call" | custom-call | tf_op jit(solution)/shard_map/pallas_call | solution.py:121
  15.1 16.6 %all_to_all.40.got_ref = bf16[16,80,128]{2,1,0:T(8,128)(2,1)S(1)} all-to-all(bf16[16,80,128]{2,1,0:T(8,128)(2,1)S(1)} %get-tuple-element.20), channel_id=1, replica_groups=mesh['z'=8,'pair'=2,'y'=4,'core'=2,'x'=4] {'pair','y','core'}, dimensions={0} | all-to-all | bytes 655360 | tf_op jit(solution)/shard_map/all_to_all | solution.py:328
  31.7 0.1 shard_map.61
  31.7 26.5 %all_to_all.41.refs_0_ = bf16[8,80,128]{2,1,0:T(8,128)(2,1)S(1)} all-to-all(bf16[8,80,128]{2,1,0:T(8,128)(2,1)S(1)} %shard_map.61), channel_id=1, replica_groups=mesh['z'=8,'pair'=2,'y'=4,'core'=2,'x'=4] {'z'}, dimensions={0} | all-to-all | bytes 327680 | tf_op jit(solution)/shard_map/all_to_all | solution.py:330
  58.3 3.0 %shard_map.62 = (f32[32,128]{1,0:T(8,128)}, f32[32,32]{1,0:T(8,128)S(1)}, f32[32,8]{1,0:T(8,128)S(1)}, f32[32,32]{1,0:T(8,128)S(1)}, f32[2,32]{1,0:T(2,128)}, /*index=5*/f32[32,32,128]{2,1,0:T(8,128)}) custom-call(bf16[8,80,128]{2,1,0:T(8,128)(2,1)S(1)} %all_to_all.41.refs_0_, f32[32,32]{1,0:T(8,128)S(1)} %shard_map.59.gram_ref.refs_1_, ...), custom_call_target="tpu_custom_call" | custom-call | tf_op jit(solution)/shard_map/pallas_call | solution.py:121
  61.3 8.0 %all-to-all-start.3 = ((f32[32,32,128]{2,1,0:T(8,128)}), f32[32,32,128]{2,1,0:T(8,128)S(1)}, u32[]{:S(2)}, u32[]{:S(2)}) async-start(f32[32,32,128]{2,1,0:T(8,128)} %get-tuple-element.22), calls=%async_computation.3 | async-start | bytes 1048576 | tf_op jit(solution)/shard_map/all_to_all | solution.py:346
  69.3 1.7 %shard_map.63.refs_1_ = f32[32,32]{1,0:T(8,128)S(1)} custom-call(f32[32,32]{1,0:T(8,128)S(1)} %get-tuple-element.23.left_ref, f32[32,32]{1,0:T(8,128)S(1)} %get-tuple-element.24.right_ref.trial_gram_ref), custom_call_target="tpu_custom_call" | custom-call | tf_op jit(solution)/shard_map/pallas_call | solution.py:121
  71.0 9.8 %all-to-all-done.3.refs_0_ = f32[32,32,128]{2,1,0:T(8,128)S(1)} async-done(((f32[32,32,128]{2,1,0:T(8,128)}), f32[32,32,128]{2,1,0:T(8,128)S(1)}, u32[]{:S(2)}, u32[]{:S(2)}) %all-to-all-start.3) | async-done | bytes 524320 | tf_op jit(solution)/shard_map/all_to_all | solution.py:346
  80.8 1.3 shard_map.64
  82.1 3.3 %all-to-all-start.4 = ((f32[4,64,128]{2,1,0:T(8,128)}), f32[4,64,128]{2,1,0:T(8,128)S(1)}, u32[]{:S(2)}, u32[]{:S(2)}) async-start(f32[4,64,128]{2,1,0:T(8,128)} %get-tuple-element.25), calls=%async_computation.4 | async-start | bytes 262144 | tf_op jit(solution)/shard_map/all_to_all | solution.py:364
  85.4 1.9 %shard_map.65 = (f32[32,32]{1,0:T(8,128)S(1)}, f32[32,32]{1,0:T(8,128)S(1)}) custom-call(f32[32,1024]{1,0:T(8,128)S(1)} %get-tuple-element.27.time_ref, f32[32,32]{1,0:T(8,128)S(1)} %get-tuple-element.24.right_ref.trial_gram_ref), custom_call_target="tpu_custom_call" | custom-call | tf_op jit(solution)/shard_map/pallas_call | solution.py:121
  87.3 2.9 %all-to-all-done.4.shared_ref = f32[4,64,128]{2,1,0:T(8,128)S(1)} async-done(((f32[4,64,128]{2,1,0:T(8,128)}), f32[4,64,128]{2,1,0:T(8,128)S(1)}, u32[]{:S(2)}, u32[]{:S(2)}) %all-to-all-start.4) | async-done | bytes 131104 | tf_op jit(solution)/shard_map/all_to_all | solution.py:364
  90.2 0.5 shard_map.66
  90.7 11.9 %all_to_all.42.got_ref = bf16[16,80,128]{2,1,0:T(8,128)(2,1)S(1)} all-to-all(bf16[16,80,128]{2,1,0:T(8,128)(2,1)S(1)} %get-tuple-element.29), channel_id=1, replica_groups=mesh['z'=8,'pair'=2,'y'=4,'core'=2,'x'=4] {'pair','y','core'}, dimensions={0} | all-to-all | bytes 655360 | tf_op jit(solution)/shard_map/all_to_all | solution.py:328
  102.6 0.1 shard_map.67
  102.7 16.6 %all_to_all.43.refs_0_ = bf16[8,80,128]{2,1,0:T(8,128)(2,1)S(1)} all-to-all(bf16[8,80,128]{2,1,0:T(8,128)(2,1)S(1)} %shard_map.67), channel_id=1, replica_groups=mesh['z'=8,'pair'=2,'y'=4,'core'=2,'x'=4] {'z'}, dimensions={0} | all-to-all | bytes 327680 | tf_op jit(solution)/shard_map/all_to_all | solution.py:330
  119.2 3.0 %shard_map.68 = (f32[32,128]{1,0:T(8,128)}, f32[32,32]{1,0:T(8,128)S(1)}, f32[32,8]{1,0:T(8,128)}, f32[32,32]{1,0:T(8,128)S(1)}, f32[2,32]{1,0:T(2,128)}, /*index=5*/f32[32,32,128]{2,1,0:T(8,128)}) custom-call(bf16[8,80,128]{2,1,0:T(8,128)(2,1)S(1)} %all_to_all.43.refs_0_, f32[32,32]{1,0:T(8,128)S(1)} %get-tuple-element.30.refs_1_, ...), custom_call_target="tpu_custom_call" | custom-call | tf_op jit(solution)/shard_map/pallas_call | solution.py:121
  122.2 8.0 %all-to-all-start.7 = ((f32[32,32,128]{2,1,0:T(8,128)}), f32[32,32,128]{2,1,0:T(8,128)S(1)}, u32[]{:S(2)}, u32[]{:S(2)}) async-start(f32[32,32,128]{2,1,0:T(8,128)} %get-tuple-element.33), calls=%async_computation.7 | async-start | bytes 1048576 | tf_op jit(solution)/shard_map/all_to_all | solution.py:346
  130.2 1.7 %shard_map.69.refs_1_ = f32[32,32]{1,0:T(8,128)S(1)} custom-call(f32[32,32]{1,0:T(8,128)S(1)} %get-tuple-element.34.left_ref, f32[32,32]{1,0:T(8,128)S(1)} %get-tuple-element.35.right_ref), custom_call_target="tpu_custom_call" | custom-call | tf_op jit(solution)/shard_map/pallas_call | solution.py:121
  131.9 9.8 %all-to-all-done.7.refs_0_ = f32[32,32,128]{2,1,0:T(8,128)S(1)} async-done(((f32[32,32,128]{2,1,0:T(8,128)}), f32[32,32,128]{2,1,0:T(8,128)S(1)}, u32[]{:S(2)}, u32[]{:S(2)}) %all-to-all-start.7) | async-done | bytes 524320 | tf_op jit(solution)/shard_map/all_to_all | solution.py:346
  141.7 1.3 shard_map.70
Async XLA Ops:
  0.6 12.0 %copy-start = (bf16[2,128,1024]{2,1,0:T(8,128)(2,1)S(1)}, bf16[2,128,1024]{2,1,0:T(8,128)(2,1)}, u32[]{:S(2)}) copy-start(bf16[2,128,1024]{2,1,0:T(8,128)(2,1)} %tensor_ref.5) | copy-start | bytes 1572868
  2.8 5.0 %copy-start.1 = (f32[32,1024]{1,0:T(8,128)S(1)}, f32[32,1024]{1,0:T(8,128)}, u32[]{:S(2)}) copy-start(f32[32,1024]{1,0:T(8,128)} %time_ref.3) | copy-start | bytes 393220
  2.8 9.9 %all-to-all-start = ((f32[4,72,128]{2,1,0:T(8,128)}), f32[4,72,128]{2,1,0:T(8,128)S(1)}, u32[]{:S(2)}, u32[]{:S(2)}) async-start(f32[4,72,128]{2,1,0:T(8,128)} %shard_map.58), calls=%async_computation | async-start | bytes 294912 | tf_op jit(solution)/shard_map/all_to_all | solution.py:324
  61.3 19.5 %all-to-all-start.3 = ((f32[32,32,128]{2,1,0:T(8,128)}), f32[32,32,128]{2,1,0:T(8,128)S(1)}, u32[]{:S(2)}, u32[]{:S(2)}) async-start(f32[32,32,128]{2,1,0:T(8,128)} %get-tuple-element.22), calls=%async_computation.3 | async-start | bytes 1048576 | tf_op jit(solution)/shard_map/all_to_all | solution.py:346
  82.1 8.1 %all-to-all-start.4 = ((f32[4,64,128]{2,1,0:T(8,128)}), f32[4,64,128]{2,1,0:T(8,128)S(1)}, u32[]{:S(2)}, u32[]{:S(2)}) async-start(f32[4,64,128]{2,1,0:T(8,128)} %get-tuple-element.25), calls=%async_computation.4 | async-start | bytes 262144 | tf_op jit(solution)/shard_map/all_to_all | solution.py:364
  122.2 19.5 %all-to-all-start.7 = ((f32[32,32,128]{2,1,0:T(8,128)}), f32[32,32,128]{2,1,0:T(8,128)S(1)}, u32[]{:S(2)}, u32[]{:S(2)}) async-start(f32[32,32,128]{2,1,0:T(8,128)} %get-tuple-element.33), calls=%async_computation.7 | async-start | bytes 1048576 | tf_op jit(solution)/shard_map/all_to_all | solution.py:346

commit v6 on v5

--- a/solution.py
+++ b/solution.py
@@ -170,19 +170,20 @@
         one = jnp.sum(raw * projected[trial], axis=1, keepdims=True)
         terms = jnp.where(lane == trial, one, terms)
     small = split(pack_small(gram_of(raw), terms))
-    members, rows, width = sent_ref.shape
-    blocks = tensor_ref.shape[2] // width
+    members, _, lanes = sent_ref.shape
+    blocks = tensor_ref.shape[2] // lanes
+    low = lax.broadcasted_iota(jnp.int32, (size, lanes), 1) < lanes // 2
     rounded = raw.astype(jnp.bfloat16)
-    for trial in range(own_trials):
-        partial = jnp.dot(rounded, tensor_ref[trial], preferred_element_type=jnp.float32)
-        partial = partial.astype(WIRE)
-        for member in range(members):
-            start = member % blocks * width
-            sent_ref[member, trial * size : (trial + 1) * size, :] = partial[
-                :, start : start + width
-            ]
+    first = jnp.dot(rounded, tensor_ref[0], preferred_element_type=jnp.float32)
+    second = jnp.dot(rounded, tensor_ref[1], preferred_element_type=jnp.float32)
+    for block in range(blocks):
+        start = block * lanes
+        one = first[:, start : start + lanes]
+        two = pltpu.roll(second[:, start : start + lanes], lanes // 2, 1)
+        sent_ref[block, :size, :] = jnp.where(low, one, two).astype(WIRE)
+        sent_ref[blocks + block, :size, :] = jnp.where(low, two, one).astype(WIRE)
     for member in range(members):
-        sent_ref[member, own_trials * size :, :] = small
+        sent_ref[member, size:, :] = small
 
 
 def first_neuron_body(shared_ref, gram_ref, tensor_ref, raw_ref, sent_ref):
@@ -223,8 +224,7 @@
     total = got_ref[0].astype(jnp.float32)
     for member in range(1, got_ref.shape[0]):
         total = total + got_ref[member].astype(jnp.float32)
-    main = own_trials * size
-    small = total[main : main + PART] + total[main + PART :]
+    small = total[size : size + PART] + total[size + PART :]
     raw_gram, terms = unpack_small(small, size, trial_count)
     diagonal = raw_gram * eye_of(size)
     down = 1.0 / jnp.sqrt(jnp.sum(diagonal, axis=1, keepdims=True) / neuron_count + tiny_eps)
@@ -240,35 +240,49 @@
     column = lax.broadcasted_iota(jnp.int32, (own_trials, trial_count), 1)
     chosen = (column == plane * own_trials + row).astype(jnp.float32)
     own_ref[...] = rows_product(chosen, trial_now)
-    weighted = None
+    columns = []
     for trial in range(own_trials):
         mine = lane == plane * own_trials + trial
-        column = jnp.sum(jnp.where(mine, trial_now, 0.0), axis=1, keepdims=True)
-        part = column * total[trial * size : (trial + 1) * size]
-        weighted = part if weighted is None else weighted + part
-    weighted = weighted * down
+        columns.append(jnp.sum(jnp.where(mine, trial_now, 0.0), axis=1, keepdims=True))
+    lanes = total.shape[1]
+    low = lax.broadcasted_iota(jnp.int32, (size, lanes), 1) < lanes // 2
+    same = low == (lax.axis_index("pair") == 0)
+    weighted = jnp.where(same, columns[0], columns[1]) * down * total[:size]
+    weighted = weighted + pltpu.roll(weighted, lanes // 2, 1)
+    half = size // 2
+    weighted = jnp.where(low[:half], weighted[:half], weighted[half:])
     for member in range(sent_ref.shape[0]):
         sent_ref[member] = weighted
 
 
+def sum_body(got_ref, sent_ref):
+    total = got_ref[0]
+    for member in range(1, got_ref.shape[0]):
+        total = total + got_ref[member]
+    for member in range(sent_ref.shape[0]):
+        sent_ref[member] = total
+
+
 def inverse_body(left_ref, right_ref, out_ref):
     out_ref[...] = damped_inverse(left_ref[...] * right_ref[...])
 
 
-def time_of(planes, got_ref, inverse_ref):
+def time_of(got_ref, inverse_ref):
+    members, half, lanes = got_ref.shape
+    low = lax.broadcasted_iota(jnp.int32, (half, lanes), 1) < lanes // 2
     pieces = []
-    for block in range(got_ref.shape[0] // planes):
-        piece = got_ref[block * planes]
-        for plane in range(1, planes):
-            piece = piece + got_ref[block * planes + plane]
-        pieces.append(piece)
+    for block in range(members // 2):
+        one, two = got_ref[block], got_ref[members // 2 + block]
+        upper = jnp.where(low, one, pltpu.roll(two, lanes // 2, 1))
+        lower = jnp.where(low, pltpu.roll(one, lanes // 2, 1), two)
+        pieces.append(jnp.concatenate([upper, lower], axis=0))
     raw = product(inverse_ref[...], jnp.concatenate(pieces, axis=1))
     mean = jnp.sum(raw * raw, axis=1, keepdims=True) / raw.shape[1]
     return raw / jnp.sqrt(mean + tiny_eps)
 
 
-def next_body(planes, got_ref, inverse_ref, tensor_ref, time_ref, sent_ref):
-    time_now = time_of(planes, got_ref, inverse_ref)
+def next_body(got_ref, inverse_ref, tensor_ref, time_ref, sent_ref):
+    time_now = time_of(got_ref, inverse_ref)
     time_ref[...] = time_now
     put_projected(time_now, tensor_ref, sent_ref)
 
@@ -283,8 +297,8 @@
     inverse_ref[...] = damped_inverse(gram * trial_gram_ref[...])
 
 
-def last_body(planes, got_ref, inverse_ref, time_ref):
-    time_now = time_of(planes, got_ref, inverse_ref)
+def last_body(got_ref, inverse_ref, time_ref):
+    time_now = time_of(got_ref, inverse_ref)
     count = time_ref.shape[0]
     row = lax.broadcasted_iota(jnp.int32, (count, time_now.shape[1]), 0)
     column = lax.broadcasted_iota(jnp.int32, (count, time_now.shape[1]), 1)
@@ -302,7 +316,7 @@
     twins = lax.axis_size("pair")
     neuron_count = own_neurons * blocks * twins * layers
     trial_count = own_trials * planes
-    width = timepoints // blocks
+    lanes = timepoints // blocks
     main = own_trials * components
 
     def shape(*dims, kind=jnp.float32):
@@ -311,7 +325,7 @@
     square = shape(components, components)
     neuron_outs = (
         shape(components, own_neurons),
-        shape(twins * blocks, main + 2 * PART, width, kind=WIRE),
+        shape(twins * blocks, components + 2 * PART, lanes, kind=WIRE),
     )
     shared = call(
         project_body,
@@ -326,7 +340,7 @@
     raw, sent = call(first_neuron_body, neuron_outs, shared, time_gram, tensor)
     for sweep_index in range(SWEEPS):
         got = lax.all_to_all(sent, near, 0, 0)
-        sent = call(reduce_body, shape(layers, main + 2 * PART, width, kind=WIRE), got)
+        sent = call(reduce_body, shape(layers, components + 2 * PART, lanes, kind=WIRE), got)
         got = lax.all_to_all(sent, "z", 0, 0)
         neuron_now, neuron_gram, trial_now, trial_gram, own_trial, sent = call(
             lambda *refs: finish_body(neuron_count, *refs),
@@ -336,18 +350,20 @@
                 shape(components, trial_count),
                 square,
                 shape(own_trials, components),
-                shape(blocks * planes, components, width),
+                shape(planes, components // 2, lanes),
             ),
             got,
             time_gram,
             raw,
             slow=(0, 4) if sweep_index == SWEEPS - 1 else (),
         )
-        got = lax.all_to_all(sent, short + ("x",), 0, 0)
+        got = lax.all_to_all(sent, "x", 0, 0)
+        sent = call(sum_body, shape(twins * blocks, components // 2, lanes), got)
+        got = lax.all_to_all(sent, near, 0, 0)
         inverse = call(inverse_body, square, neuron_gram, trial_gram)
         if sweep_index == SWEEPS - 1:
             time_out = call(
-                lambda *refs: last_body(planes, *refs),
+                last_body,
                 shape(timepoints // (layers * twins * blocks * planes), components),
                 got,
                 inverse,
@@ -355,7 +371,7 @@
             )
             break
         time_now, shared = call(
-            lambda *refs: next_body(planes, *refs),
+            next_body,
             (shape(components, timepoints), shape(planes, main, own_neurons)),
             got,
             inverse,

time: 144 us -> 142 us (0.986)
  waiting for transfers between devices: 27.2 us -> 16.6 us
  blocking collectives: 71.6 us -> 80.2 us
    all_to_all x0 -> x2, blocking collectives: none -> 13.3 us  [per_device(): got = lax.all_to_all(sent, 'x', 0, 0)]
    all_to_all x2, waiting for transfers between devices: 19.7 us -> 9.03 us  [per_device(): got = lax.all_to_all(sent, near, 0, 0)]
    all_to_all x2, blocking collectives: 43.1 us -> 40.4 us  [per_device(): got = lax.all_to_all(sent, 'z', 0, 0)]
    all_to_all x2, blocking collectives: 28.5 us -> 26.5 us  [per_device(): got = lax.all_to_all(sent, near, 0, 0)]
    pallas_call x13 -> x15, Pallas kernels: 19.3 us -> 20.4 us  [call(): pl.pallas_call(body, out_shape=shapes, in_specs=[pl.BlockSpec(memory_spac...]
where the time goes in v6:
time: 142 us; the launch traced here: 141 us
  blocking collectives  80.2 us (56%)
  starting transfers between devices  23 us (16%)
  Pallas kernels  20.4 us (14%)
  waiting for transfers between devices  16.6 us (12%)
    all_to_all x2, blocking collectives, per_device(): got = lax.all_to_all(sent, 'z', 0, 0)  40.4 us
    all_to_all x2, blocking collectives, per_device(): got = lax.all_to_all(sent, near, 0, 0)  26.5 us
    pallas_call x15, Pallas kernels, call(): pl.pallas_call(body, out_shape=shapes, in_specs=[pl.BlockSpec(memory_spac...  20.4 us
    all_to_all x2, starting transfers between devices, per_device(): got = lax.all_to_all(sent, near, 0, 0)  14.7 us
    all_to_all x2, blocking collectives, per_device(): got = lax.all_to_all(sent, 'x', 0, 0)  13.3 us
    all_to_all x2, waiting for transfers between devices, per_device(): got = lax.all_to_all(sent, near, 0, 0)  9.03 us
    all_to_all x2, starting transfers between devices, per_device(): shared = lax.all_to_all(shared, 'x', 0, 0)  8.29 us
    all_to_all x2, waiting for transfers between devices, per_device(): shared = lax.all_to_all(shared, 'x', 0, 0)  7.54 us
  transfers between devices with their start and end apart: 4, of which 4 were waited for; matrix products, arithmetic and copies ran while one was open for 0% of the time, Pallas kernels for 4%

profile of v6, /device:TPU:1, one launch (start us, length us, event | category | flops | bytes accessed | tf_op | source)
XLA Modules:
  0.0 140.8 jit_solution(2418738735396283597)
XLA Ops:
  0.6 0.0 copy-start
  0.6 2.1 %shard_map.58 = f32[4,72,128]{2,1,0:T(8,128)} custom-call(f32[32,1024]{1,0:T(8,128)} %time_ref.3, f32[2,32]{1,0:T(2,128)} %bitcast.3, bf16[2,128,1024]{2,1,0:T(8,128)(2,1)} %tensor_ref.7), custom_call_target="tpu_custom_call" | custom-call | tf_op jit(solution)/shard_map/pallas_call | solution.py:121
  2.8 0.0 copy-start.1
  2.8 5.0 %all-to-all-start = ((f32[4,72,128]{2,1,0:T(8,128)}), f32[4,72,128]{2,1,0:T(8,128)S(1)}, u32[]{:S(2)}, u32[]{:S(2)}) async-start(f32[4,72,128]{2,1,0:T(8,128)} %shard_map.58), calls=%async_computation | async-start | bytes 294912 | tf_op jit(solution)/shard_map/all_to_all | solution.py:338
  7.7 0.0 copy-done.1
  7.7 0.2 shard_map.59.gram_ref.refs_1_
  8.0 4.7 %all-to-all-done.shared_ref = f32[4,72,128]{2,1,0:T(8,128)S(1)} async-done(((f32[4,72,128]{2,1,0:T(8,128)}), f32[4,72,128]{2,1,0:T(8,128)S(1)}, u32[]{:S(2)}, u32[]{:S(2)}) %all-to-all-start) | async-done | bytes 147488 | tf_op jit(solution)/shard_map/all_to_all | solution.py:338
  12.6 0.0 copy-done
  12.6 2.5 %shard_map.60 = (f32[32,128]{1,0:T(8,128)S(1)}, bf16[16,48,128]{2,1,0:T(8,128)(2,1)S(1)}) custom-call(f32[4,72,128]{2,1,0:T(8,128)S(1)} %all-to-all-done.shared_ref, f32[32,32]{1,0:T(8,128)S(1)} %shard_map.59.gram_ref.refs_1_, bf16[2,128,1024]{2,1,0:T(8,128)(2,1)S(1)} %copy-done), custom_call_target="tpu_custom_call" | custom-call | tf_op jit(solution)/shard_map/pallas_call | solution.py:121
  15.1 15.6 %all_to_all.50.got_ref = bf16[16,48,128]{2,1,0:T(8,128)(2,1)S(1)} all-to-all(bf16[16,48,128]{2,1,0:T(8,128)(2,1)S(1)} %get-tuple-element.20), channel_id=1, replica_groups=mesh['z'=8,'pair'=2,'y'=4,'core'=2,'x'=4] {'pair','y','core'}, dimensions={0} | all-to-all | bytes 393216 | tf_op jit(solution)/shard_map/all_to_all | solution.py:342
  30.7 25.3 %all_to_all.51.refs_0_ = bf16[8,48,128]{2,1,0:T(8,128)(2,1)S(1)} all-to-all(bf16[8,48,128]{2,1,0:T(8,128)(2,1)S(1)} %shard_map.61), channel_id=1, replica_groups=mesh['z'=8,'pair'=2,'y'=4,'core'=2,'x'=4] {'z'}, dimensions={0} | all-to-all | bytes 196608 | tf_op jit(solution)/shard_map/all_to_all | solution.py:344
  56.0 2.8 %shard_map.62 = (f32[32,128]{1,0:T(8,128)}, f32[32,32]{1,0:T(8,128)S(1)}, f32[32,8]{1,0:T(8,128)S(1)}, f32[32,32]{1,0:T(8,128)S(1)}, f32[2,32]{1,0:T(2,128)}, /*index=5*/f32[4,16,128]{2,1,0:T(8,128)S(1)}) custom-call(bf16[8,48,128]{2,1,0:T(8,128)(2,1)S(1)} %all_to_all.51.refs_0_, f32[32,32]{1,0:T(8,128)S(1)} %shard_map.59.gram_ref.refs_1_, ...), custom_call_target="tpu_custom_call" | custom-call | tf_op jit(solution)/shard_map/pallas_call | solution.py:121
  58.8 6.6 %all_to_all.52.got_ref = f32[4,16,128]{2,1,0:T(8,128)S(1)} all-to-all(f32[4,16,128]{2,1,0:T(8,128)S(1)} %get-tuple-element.22), channel_id=1, replica_groups=mesh['z'=8,'pair'=2,'y'=4,'core'=2,'x'=4] {'x'}, dimensions={0} | all-to-all | bytes 65536 | tf_op jit(solution)/shard_map/all_to_all | solution.py:360
  65.4 0.7 shard_map.63
  66.1 7.5 %all-to-all-start.4 = ((f32[16,16,128]{2,1,0:T(8,128)}), f32[16,16,128]{2,1,0:T(8,128)S(1)}, u32[]{:S(2)}, u32[]{:S(2)}) async-start(f32[16,16,128]{2,1,0:T(8,128)} %shard_map.63), calls=%async_computation.4 | async-start | bytes 262144 | tf_op jit(solution)/shard_map/all_to_all | solution.py:362
  73.6 1.7 %shard_map.64.inverse_ref = f32[32,32]{1,0:T(8,128)S(1)} custom-call(f32[32,32]{1,0:T(8,128)S(1)} %get-tuple-element.23.left_ref, f32[32,32]{1,0:T(8,128)S(1)} %get-tuple-element.24.right_ref.trial_gram_ref), custom_call_target="tpu_custom_call" | custom-call | tf_op jit(solution)/shard_map/pallas_call | solution.py:121
  75.3 4.5 %all-to-all-done.4.got_ref = f32[16,16,128]{2,1,0:T(8,128)S(1)} async-done(((f32[16,16,128]{2,1,0:T(8,128)}), f32[16,16,128]{2,1,0:T(8,128)S(1)}, u32[]{:S(2)}, u32[]{:S(2)}) %all-to-all-start.4) | async-done | bytes 131104 | tf_op jit(solution)/shard_map/all_to_all | solution.py:362
  79.8 1.3 shard_map.65
  81.1 3.3 %all-to-all-start.5 = ((f32[4,64,128]{2,1,0:T(8,128)}), f32[4,64,128]{2,1,0:T(8,128)S(1)}, u32[]{:S(2)}, u32[]{:S(2)}) async-start(f32[4,64,128]{2,1,0:T(8,128)} %get-tuple-element.25), calls=%async_computation.5 | async-start | bytes 262144 | tf_op jit(solution)/shard_map/all_to_all | solution.py:380
  84.4 1.9 %shard_map.66 = (f32[32,32]{1,0:T(8,128)S(1)}, f32[32,32]{1,0:T(8,128)S(1)}) custom-call(f32[32,1024]{1,0:T(8,128)S(1)} %get-tuple-element.27.time_ref, f32[32,32]{1,0:T(8,128)S(1)} %get-tuple-element.24.right_ref.trial_gram_ref), custom_call_target="tpu_custom_call" | custom-call | tf_op jit(solution)/shard_map/pallas_call | solution.py:121
  86.4 2.9 %all-to-all-done.5.shared_ref = f32[4,64,128]{2,1,0:T(8,128)S(1)} async-done(((f32[4,64,128]{2,1,0:T(8,128)}), f32[4,64,128]{2,1,0:T(8,128)S(1)}, u32[]{:S(2)}, u32[]{:S(2)}) %all-to-all-start.5) | async-done | bytes 131104 | tf_op jit(solution)/shard_map/all_to_all | solution.py:380
  89.2 0.6 shard_map.67
  89.8 10.9 %all_to_all.53.got_ref = bf16[16,48,128]{2,1,0:T(8,128)(2,1)S(1)} all-to-all(bf16[16,48,128]{2,1,0:T(8,128)(2,1)S(1)} %get-tuple-element.29), channel_id=1, replica_groups=mesh['z'=8,'pair'=2,'y'=4,'core'=2,'x'=4] {'pair','y','core'}, dimensions={0} | all-to-all | bytes 393216 | tf_op jit(solution)/shard_map/all_to_all | solution.py:342
  100.8 15.1 %all_to_all.54.refs_0_ = bf16[8,48,128]{2,1,0:T(8,128)(2,1)S(1)} all-to-all(bf16[8,48,128]{2,1,0:T(8,128)(2,1)S(1)} %shard_map.68), channel_id=1, replica_groups=mesh['z'=8,'pair'=2,'y'=4,'core'=2,'x'=4] {'z'}, dimensions={0} | all-to-all | bytes 196608 | tf_op jit(solution)/shard_map/all_to_all | solution.py:344
  115.9 2.8 %shard_map.69 = (f32[32,128]{1,0:T(8,128)}, f32[32,32]{1,0:T(8,128)S(1)}, f32[32,8]{1,0:T(8,128)}, f32[32,32]{1,0:T(8,128)S(1)}, f32[2,32]{1,0:T(2,128)}, /*index=5*/f32[4,16,128]{2,1,0:T(8,128)S(1)}) custom-call(bf16[8,48,128]{2,1,0:T(8,128)(2,1)S(1)} %all_to_all.54.refs_0_, f32[32,32]{1,0:T(8,128)S(1)} %get-tuple-element.30.refs_1_, ...), custom_call_target="tpu_custom_call" | custom-call | tf_op jit(solution)/shard_map/pallas_call | solution.py:121
  118.7 6.6 %all_to_all.55.got_ref = f32[4,16,128]{2,1,0:T(8,128)S(1)} all-to-all(f32[4,16,128]{2,1,0:T(8,128)S(1)} %get-tuple-element.33), channel_id=1, replica_groups=mesh['z'=8,'pair'=2,'y'=4,'core'=2,'x'=4] {'x'}, dimensions={0} | all-to-all | bytes 65536 | tf_op jit(solution)/shard_map/all_to_all | solution.py:360
  125.3 0.7 shard_map.70
  126.0 7.3 %all-to-all-start.9 = ((f32[16,16,128]{2,1,0:T(8,128)}), f32[16,16,128]{2,1,0:T(8,128)S(1)}, u32[]{:S(2)}, u32[]{:S(2)}) async-start(f32[16,16,128]{2,1,0:T(8,128)} %shard_map.70), calls=%async_computation.9 | async-start | bytes 262144 | tf_op jit(solution)/shard_map/all_to_all | solution.py:362
  133.3 1.7 %shard_map.71.inverse_ref = f32[32,32]{1,0:T(8,128)S(1)} custom-call(f32[32,32]{1,0:T(8,128)S(1)} %get-tuple-element.34.left_ref, f32[32,32]{1,0:T(8,128)S(1)} %get-tuple-element.35.right_ref), custom_call_target="tpu_custom_call" | custom-call | tf_op jit(solution)/shard_map/pallas_call | solution.py:121
  135.0 4.5 %all-to-all-done.9.got_ref = f32[16,16,128]{2,1,0:T(8,128)S(1)} async-done(((f32[16,16,128]{2,1,0:T(8,128)}), f32[16,16,128]{2,1,0:T(8,128)S(1)}, u32[]{:S(2)}, u32[]{:S(2)}) %all-to-all-start.9) | async-done | bytes 131104 | tf_op jit(solution)/shard_map/all_to_all | solution.py:362
  139.5 1.4 shard_map.72
  (2 shorter events, 0.1 us)
Async XLA Ops:
  0.6 12.0 %copy-start = (bf16[2,128,1024]{2,1,0:T(8,128)(2,1)S(1)}, bf16[2,128,1024]{2,1,0:T(8,128)(2,1)}, u32[]{:S(2)}) copy-start(bf16[2,128,1024]{2,1,0:T(8,128)(2,1)} %tensor_ref.7) | copy-start | bytes 1572868
  2.8 5.0 %copy-start.1 = (f32[32,1024]{1,0:T(8,128)S(1)}, f32[32,1024]{1,0:T(8,128)}, u32[]{:S(2)}) copy-start(f32[32,1024]{1,0:T(8,128)} %time_ref.3) | copy-start | bytes 393220
  2.8 9.9 %all-to-all-start = ((f32[4,72,128]{2,1,0:T(8,128)}), f32[4,72,128]{2,1,0:T(8,128)S(1)}, u32[]{:S(2)}, u32[]{:S(2)}) async-start(f32[4,72,128]{2,1,0:T(8,128)} %shard_map.58), calls=%async_computation | async-start | bytes 294912 | tf_op jit(solution)/shard_map/all_to_all | solution.py:338
  66.1 13.7 %all-to-all-start.4 = ((f32[16,16,128]{2,1,0:T(8,128)}), f32[16,16,128]{2,1,0:T(8,128)S(1)}, u32[]{:S(2)}, u32[]{:S(2)}) async-start(f32[16,16,128]{2,1,0:T(8,128)} %shard_map.63), calls=%async_computation.4 | async-start | bytes 262144 | tf_op jit(solution)/shard_map/all_to_all | solution.py:362
  81.1 8.1 %all-to-all-start.5 = ((f32[4,64,128]{2,1,0:T(8,128)}), f32[4,64,128]{2,1,0:T(8,128)S(1)}, u32[]{:S(2)}, u32[]{:S(2)}) async-start(f32[4,64,128]{2,1,0:T(8,128)} %get-tuple-element.25), calls=%async_computation.5 | async-start | bytes 262144 | tf_op jit(solution)/shard_map/all_to_all | solution.py:380
  126.0 13.5 %all-to-all-start.9 = ((f32[16,16,128]{2,1,0:T(8,128)}), f32[16,16,128]{2,1,0:T(8,128)S(1)}, u32[]{:S(2)}, u32[]{:S(2)}) async-start(f32[16,16,128]{2,1,0:T(8,128)} %shard_map.70), calls=%async_computation.9 | async-start | bytes 262144 | tf_op jit(solution)/shard_map/all_to_all | solution.py:362

commit v7 on v6

--- a/solution.py
+++ b/solution.py
@@ -63,17 +63,31 @@
     share = size / trace
     both = jnp.concatenate([system * share + ridge_share * eye, eye], axis=1)
     row = lax.broadcasted_iota(jnp.int32, both.shape, 0)
+
+    def pivots(step):
+        if step >= size:
+            return []
+        return [
+            jnp.broadcast_to(both[:, place : place + 1], both.shape) for place in (step, step + 1)
+        ]
+
+    ahead = [pivots(0), pivots(2)]
     for step in range(0, size, 2):
-        first = jnp.broadcast_to(both[:, step : step + 1], both.shape)
-        second = jnp.broadcast_to(both[:, step + 1 : step + 2], both.shape)
-        upper, lower = both[step : step + 1], both[step + 1 : step + 2]
+        first, second = ahead[0]
         p00, p01 = first[step : step + 1], second[step : step + 1]
         p10, p11 = first[step + 1 : step + 2], second[step + 1 : step + 2]
         over = 1.0 / (p00 * p11 - p01 * p10)
-        new_upper = (p11 * upper - p01 * lower) * over
-        new_lower = (p00 * lower - p10 * upper) * over
-        cleared = both - first * new_upper - second * new_lower
-        both = jnp.where(row == step, new_upper, jnp.where(row == step + 1, new_lower, cleared))
+        p00, p01, p10, p11 = p00 * over, p01 * over, p10 * over, p11 * over
+
+        def cleared(matrix):
+            upper, lower = matrix[step : step + 1], matrix[step + 1 : step + 2]
+            new_upper = p11 * upper - p01 * lower
+            new_lower = p00 * lower - p10 * upper
+            rest = matrix - first * new_upper - second * new_lower
+            return jnp.where(row == step, new_upper, jnp.where(row == step + 1, new_lower, rest))
+
+        ahead = [[cleared(one) for one in ahead[1]], [cleared(one) for one in pivots(step + 4)]]
+        both = cleared(both)
     return both[:, size:] * share
 
 
@@ -127,13 +141,13 @@
     return result[0] if single else result
 
 
-def put_projected(time_now, tensor_ref, sent_ref):
+def put_projected(time_now, tensor_of, sent_ref):
     rounded = time_now.astype(jnp.bfloat16)
     size = time_now.shape[0]
-    for trial in range(tensor_ref.shape[0]):
+    for trial in range(sent_ref.shape[1] // size):
         projected = lax.dot_general(
             rounded,
-            tensor_ref[trial],
+            tensor_of(trial),
             (((1,), (1,)), ((), ())),
             preferred_element_type=jnp.float32,
         )
@@ -141,14 +155,46 @@
             sent_ref[member, trial * size : (trial + 1) * size, :] = projected
 
 
-def project_body(time_ref, trial_ref, tensor_ref, sent_ref):
-    put_projected(time_ref[...], tensor_ref, sent_ref)
+def project_body(time_hbm, trial_hbm, tensor_hbm, sent_ref, time_ref, trial_ref, tensor_ref, arrived):
     count, size = trial_ref.shape
+    copies = [
+        pltpu.make_async_copy(time_hbm, time_ref, arrived.at[0]),
+        pltpu.make_async_copy(trial_hbm, trial_ref, arrived.at[1]),
+    ]
+    for trial in range(count):
+        copies.append(
+            pltpu.make_async_copy(tensor_hbm.at[trial], tensor_ref.at[trial], arrived.at[2 + trial])
+        )
+    for copy in copies:
+        copy.start()
+    copies[0].wait()
+
+    def tensor_of(trial):
+        copies[2 + trial].wait()
+        return tensor_ref[trial]
+
+    put_projected(time_ref[...], tensor_of, sent_ref)
+    copies[1].wait()
     lanes = sent_ref.shape[2]
     tile = jnp.concatenate([trial_ref[...], jnp.zeros((PART - count, size), jnp.float32)], axis=0)
     tile = jnp.concatenate([tile, jnp.zeros((PART, lanes - size), jnp.float32)], axis=1)
     for member in range(sent_ref.shape[0]):
         sent_ref[member, count * size :, :] = tile
+
+
+def project(out, time_init, trial_rows, tensor):
+    return pl.pallas_call(
+        project_body,
+        out_shape=out,
+        in_specs=[pl.BlockSpec(memory_space=pl.ANY) for _ in range(3)],
+        out_specs=pl.BlockSpec(memory_space=pltpu.VMEM),
+        scratch_shapes=[
+            pltpu.VMEM(time_init.shape, time_init.dtype),
+            pltpu.VMEM(trial_rows.shape, trial_rows.dtype),
+            pltpu.VMEM(tensor.shape, tensor.dtype),
+            pltpu.SemaphoreType.DMA((2 + tensor.shape[0],)),
+        ],
+    )(time_init, trial_rows, tensor)
 
 
 def put_neuron(trial_now, inverse, shared_ref, tensor_ref, raw_ref, sent_ref):
@@ -278,13 +324,14 @@
         pieces.append(jnp.concatenate([upper, lower], axis=0))
     raw = product(inverse_ref[...], jnp.concatenate(pieces, axis=1))
     mean = jnp.sum(raw * raw, axis=1, keepdims=True) / raw.shape[1]
-    return raw / jnp.sqrt(mean + tiny_eps)
+    return raw, jnp.sqrt(mean + tiny_eps)
 
 
 def next_body(got_ref, inverse_ref, tensor_ref, time_ref, sent_ref):
-    time_now = time_of(got_ref, inverse_ref)
+    raw, norm = time_of(got_ref, inverse_ref)
+    time_now = raw / norm
     time_ref[...] = time_now
-    put_projected(time_now, tensor_ref, sent_ref)
+    put_projected(time_now, lambda trial: tensor_ref[trial], sent_ref)
 
 
 def gram_body(time_ref, gram_ref):
@@ -298,12 +345,19 @@
 
 
 def last_body(got_ref, inverse_ref, time_ref):
-    time_now = time_of(got_ref, inverse_ref)
-    count = time_ref.shape[0]
-    row = lax.broadcasted_iota(jnp.int32, (count, time_now.shape[1]), 0)
-    column = lax.broadcasted_iota(jnp.int32, (count, time_now.shape[1]), 1)
-    chosen = (column == lax.axis_index(("z", "pair", "y", "core", "x")) * count + row).astype(jnp.float32)
-    time_ref[...] = rows_product(chosen, time_now)
+    raw, norm = time_of(got_ref, inverse_ref)
+    count, size = time_ref.shape
+    lanes = got_ref.shape[2]
+    position = lax.axis_index(("z", "pair", "y", "core", "x"))
+    column = lax.broadcasted_iota(jnp.int32, raw.shape, 1)
+    mine = jnp.where(column // count == position, raw, 0.0)
+    picked = mine[:, :lanes]
+    for start in range(lanes, raw.shape[1], lanes):
+        picked = picked + mine[:, start : start + lanes]
+    row = lax.broadcasted_iota(jnp.int32, (count, lanes), 0)
+    lane = lax.broadcasted_iota(jnp.int32, (count, lanes), 1)
+    chosen = (lane == position * count % lanes + row).astype(jnp.float32)
+    time_ref[...] = rows_product(chosen, picked / norm)
 
 
 def per_device(tensor, time_init, trial_init):
@@ -327,13 +381,8 @@
         shape(components, own_neurons),
         shape(twins * blocks, components + 2 * PART, lanes, kind=WIRE),
     )
-    shared = call(
-        project_body,
-        shape(planes, main + PART, own_neurons),
-        time_init,
-        trial_init.T,
-        tensor,
-        away=(0, 1, 2),
+    shared = project(
+        shape(planes, main + PART, own_neurons), time_init, trial_init.T, tensor
     )
     shared = lax.all_to_all(shared, "x", 0, 0)
     time_gram = call(gram_body, square, time_init)

time: 142 us -> 139 us (0.979)
  Pallas kernels: 20.4 us -> 15.9 us
  waiting for transfers between devices: 16.6 us -> 18.8 us
    pallas_call x15 -> x14, Pallas kernels: 20.4 us -> 13.6 us  [call(): pl.pallas_call(body, out_shape=shapes, in_specs=[pl.BlockSpec(memory_spac...]
    pallas_call x0 -> x1, Pallas kernels: none -> 2.3 us  [project(): pl.pallas_call(project_body, out_shape=out, in_specs=[pl.BlockSpec(memory...]
    all_to_all x2, waiting for transfers between devices: 9.03 us -> 10.5 us  [per_device(): got = lax.all_to_all(sent, near, 0, 0)]
  transfers between devices with their start and end apart: 4 -> 4, of which waited for: 4 -> 4; matrix products, arithmetic and copies ran while one was open for 0% -> 0% of each run, Pallas kernels for 4% -> 2%
where the time goes in v7:
time: 139 us
  blocking collectives  80.2 us (58%)
  starting transfers between devices  23 us (17%)
  waiting for transfers between devices  18.8 us (14%)
  Pallas kernels  15.9 us (11%)
    all_to_all x2, blocking collectives, per_device(): got = lax.all_to_all(sent, 'z', 0, 0)  40.4 us
    all_to_all x2, blocking collectives, per_device(): got = lax.all_to_all(sent, near, 0, 0)  26.5 us
    all_to_all x2, starting transfers between devices, per_device(): got = lax.all_to_all(sent, near, 0, 0)  14.7 us
    pallas_call x14, Pallas kernels, call(): pl.pallas_call(body, out_shape=shapes, in_specs=[pl.BlockSpec(memory_spac...  13.6 us
    all_to_all x2, blocking collectives, per_device(): got = lax.all_to_all(sent, 'x', 0, 0)  13.3 us
    all_to_all x2, waiting for transfers between devices, per_device(): got = lax.all_to_all(sent, near, 0, 0)  10.5 us
    all_to_all x2, starting transfers between devices, per_device(): shared = lax.all_to_all(shared, 'x', 0, 0)  8.3 us
    all_to_all x2, waiting for transfers between devices, per_device(): shared = lax.all_to_all(shared, 'x', 0, 0)  8.28 us
  transfers between devices with their start and end apart: 4, of which 4 were waited for; matrix products, arithmetic and copies ran while one was open for 0% of the time, Pallas kernels for 2%

profile of v7, /device:TPU:1, one launch (start us, length us, event | category | flops | bytes accessed | tf_op | source)
XLA Modules:
  0.0 138.5 jit_solution(17221708057681001052)
XLA Ops:
  0.6 0.0 copy-start
  0.6 2.3 %shard_map.58 = f32[4,72,128]{2,1,0:T(8,128)} custom-call(f32[32,1024]{1,0:T(8,128)} %time_ref.1, f32[2,32]{1,0:T(2,128)} %bitcast.3, bf16[2,128,1024]{2,1,0:T(8,128)(2,1)} %tensor_ref.5), custom_call_target="tpu_custom_call" | custom-call | tf_op jit(solution)/shard_map/pallas_call | solution.py:186
  2.9 0.0 copy-start.1
  3.0 5.0 %all-to-all-start = ((f32[4,72,128]{2,1,0:T(8,128)}), f32[4,72,128]{2,1,0:T(8,128)S(1)}, u32[]{:S(2)}, u32[]{:S(2)}) async-start(f32[4,72,128]{2,1,0:T(8,128)} %shard_map.58), calls=%async_computation | async-start | bytes 294912 | tf_op jit(solution)/shard_map/all_to_all | solution.py:387
  7.9 0.0 copy-done.1
  7.9 0.2 shard_map.59.gram_ref.refs_1_
  8.2 4.7 %all-to-all-done.shared_ref = f32[4,72,128]{2,1,0:T(8,128)S(1)} async-done(((f32[4,72,128]{2,1,0:T(8,128)}), f32[4,72,128]{2,1,0:T(8,128)S(1)}, u32[]{:S(2)}, u32[]{:S(2)}) %all-to-all-start) | async-done | bytes 147488 | tf_op jit(solution)/shard_map/all_to_all | solution.py:387
  12.8 0.0 copy-done
  12.8 1.7 %shard_map.60 = (f32[32,128]{1,0:T(8,128)S(1)}, bf16[16,48,128]{2,1,0:T(8,128)(2,1)S(1)}) custom-call(f32[4,72,128]{2,1,0:T(8,128)S(1)} %all-to-all-done.shared_ref, f32[32,32]{1,0:T(8,128)S(1)} %shard_map.59.gram_ref.refs_1_, bf16[2,128,1024]{2,1,0:T(8,128)(2,1)S(1)} %copy-done), custom_call_target="tpu_custom_call" | custom-call | tf_op jit(solution)/shard_map/pallas_call | solution.py:135
  14.6 15.6 %all_to_all.50.got_ref = bf16[16,48,128]{2,1,0:T(8,128)(2,1)S(1)} all-to-all(bf16[16,48,128]{2,1,0:T(8,128)(2,1)S(1)} %get-tuple-element.20), channel_id=1, replica_groups=mesh['z'=8,'pair'=2,'y'=4,'core'=2,'x'=4] {'pair','y','core'}, dimensions={0} | all-to-all | bytes 393216 | tf_op jit(solution)/shard_map/all_to_all | solution.py:391
  30.2 25.3 %all_to_all.51.refs_0_ = bf16[8,48,128]{2,1,0:T(8,128)(2,1)S(1)} all-to-all(bf16[8,48,128]{2,1,0:T(8,128)(2,1)S(1)} %shard_map.61), channel_id=1, replica_groups=mesh['z'=8,'pair'=2,'y'=4,'core'=2,'x'=4] {'z'}, dimensions={0} | all-to-all | bytes 196608 | tf_op jit(solution)/shard_map/all_to_all | solution.py:393
  55.4 2.0 %shard_map.62 = (f32[32,128]{1,0:T(8,128)}, f32[32,32]{1,0:T(8,128)S(1)}, f32[32,8]{1,0:T(8,128)S(1)}, f32[32,32]{1,0:T(8,128)S(1)}, f32[2,32]{1,0:T(2,128)}, /*index=5*/f32[4,16,128]{2,1,0:T(8,128)S(1)}) custom-call(bf16[8,48,128]{2,1,0:T(8,128)(2,1)S(1)} %all_to_all.51.refs_0_, f32[32,32]{1,0:T(8,128)S(1)} %shard_map.59.gram_ref.refs_1_, ...), custom_call_target="tpu_custom_call" | custom-call | tf_op jit(solution)/shard_map/pallas_call | solution.py:135
  57.5 6.6 %all_to_all.52.got_ref = f32[4,16,128]{2,1,0:T(8,128)S(1)} all-to-all(f32[4,16,128]{2,1,0:T(8,128)S(1)} %get-tuple-element.22), channel_id=1, replica_groups=mesh['z'=8,'pair'=2,'y'=4,'core'=2,'x'=4] {'x'}, dimensions={0} | all-to-all | bytes 65536 | tf_op jit(solution)/shard_map/all_to_all | solution.py:409
  64.1 0.7 shard_map.63
  64.8 7.5 %all-to-all-start.4 = ((f32[16,16,128]{2,1,0:T(8,128)}), f32[16,16,128]{2,1,0:T(8,128)S(1)}, u32[]{:S(2)}, u32[]{:S(2)}) async-start(f32[16,16,128]{2,1,0:T(8,128)} %shard_map.63), calls=%async_computation.4 | async-start | bytes 262144 | tf_op jit(solution)/shard_map/all_to_all | solution.py:411
  72.3 1.0 shard_map.64.inverse_ref
  73.2 5.2 %all-to-all-done.4.got_ref = f32[16,16,128]{2,1,0:T(8,128)S(1)} async-done(((f32[16,16,128]{2,1,0:T(8,128)}), f32[16,16,128]{2,1,0:T(8,128)S(1)}, u32[]{:S(2)}, u32[]{:S(2)}) %all-to-all-start.4) | async-done | bytes 131104 | tf_op jit(solution)/shard_map/all_to_all | solution.py:411
  78.5 1.3 shard_map.65
  79.8 3.3 %all-to-all-start.5 = ((f32[4,64,128]{2,1,0:T(8,128)}), f32[4,64,128]{2,1,0:T(8,128)S(1)}, u32[]{:S(2)}, u32[]{:S(2)}) async-start(f32[4,64,128]{2,1,0:T(8,128)} %get-tuple-element.25), calls=%async_computation.5 | async-start | bytes 262144 | tf_op jit(solution)/shard_map/all_to_all | solution.py:429
  83.1 1.2 shard_map.66
  84.3 3.6 %all-to-all-done.5.shared_ref = f32[4,64,128]{2,1,0:T(8,128)S(1)} async-done(((f32[4,64,128]{2,1,0:T(8,128)}), f32[4,64,128]{2,1,0:T(8,128)S(1)}, u32[]{:S(2)}, u32[]{:S(2)}) %all-to-all-start.5) | async-done | bytes 131104 | tf_op jit(solution)/shard_map/all_to_all | solution.py:429
  87.9 0.6 shard_map.67
  88.5 10.9 %all_to_all.53.got_ref = bf16[16,48,128]{2,1,0:T(8,128)(2,1)S(1)} all-to-all(bf16[16,48,128]{2,1,0:T(8,128)(2,1)S(1)} %get-tuple-element.29), channel_id=1, replica_groups=mesh['z'=8,'pair'=2,'y'=4,'core'=2,'x'=4] {'pair','y','core'}, dimensions={0} | all-to-all | bytes 393216 | tf_op jit(solution)/shard_map/all_to_all | solution.py:391
  99.5 15.1 %all_to_all.54.refs_0_ = bf16[8,48,128]{2,1,0:T(8,128)(2,1)S(1)} all-to-all(bf16[8,48,128]{2,1,0:T(8,128)(2,1)S(1)} %shard_map.68), channel_id=1, replica_groups=mesh['z'=8,'pair'=2,'y'=4,'core'=2,'x'=4] {'z'}, dimensions={0} | all-to-all | bytes 196608 | tf_op jit(solution)/shard_map/all_to_all | solution.py:393
  114.6 2.0 %shard_map.69 = (f32[32,128]{1,0:T(8,128)}, f32[32,32]{1,0:T(8,128)S(1)}, f32[32,8]{1,0:T(8,128)}, f32[32,32]{1,0:T(8,128)S(1)}, f32[2,32]{1,0:T(2,128)}, /*index=5*/f32[4,16,128]{2,1,0:T(8,128)S(1)}) custom-call(bf16[8,48,128]{2,1,0:T(8,128)(2,1)S(1)} %all_to_all.54.refs_0_, f32[32,32]{1,0:T(8,128)S(1)} %get-tuple-element.30.refs_1_, ...), custom_call_target="tpu_custom_call" | custom-call | tf_op jit(solution)/shard_map/pallas_call | solution.py:135
  116.6 6.6 %all_to_all.55.got_ref = f32[4,16,128]{2,1,0:T(8,128)S(1)} all-to-all(f32[4,16,128]{2,1,0:T(8,128)S(1)} %get-tuple-element.33), channel_id=1, replica_groups=mesh['z'=8,'pair'=2,'y'=4,'core'=2,'x'=4] {'x'}, dimensions={0} | all-to-all | bytes 65536 | tf_op jit(solution)/shard_map/all_to_all | solution.py:409
  123.3 0.7 shard_map.70
  123.9 7.3 %all-to-all-start.9 = ((f32[16,16,128]{2,1,0:T(8,128)}), f32[16,16,128]{2,1,0:T(8,128)S(1)}, u32[]{:S(2)}, u32[]{:S(2)}) async-start(f32[16,16,128]{2,1,0:T(8,128)} %shard_map.70), calls=%async_computation.9 | async-start | bytes 262144 | tf_op jit(solution)/shard_map/all_to_all | solution.py:411
  131.2 1.0 shard_map.71.inverse_ref
  132.2 5.2 %all-to-all-done.9.got_ref = f32[16,16,128]{2,1,0:T(8,128)S(1)} async-done(((f32[16,16,128]{2,1,0:T(8,128)}), f32[16,16,128]{2,1,0:T(8,128)S(1)}, u32[]{:S(2)}, u32[]{:S(2)}) %all-to-all-start.9) | async-done | bytes 131104 | tf_op jit(solution)/shard_map/all_to_all | solution.py:411
  137.4 1.1 shard_map.72
  (2 shorter events, 0.1 us)
Async XLA Ops:
  0.6 12.2 %copy-start = (bf16[2,128,1024]{2,1,0:T(8,128)(2,1)S(1)}, bf16[2,128,1024]{2,1,0:T(8,128)(2,1)}, u32[]{:S(2)}) copy-start(bf16[2,128,1024]{2,1,0:T(8,128)(2,1)} %tensor_ref.5) | copy-start | bytes 1572868
  2.9 5.0 %copy-start.1 = (f32[32,1024]{1,0:T(8,128)S(1)}, f32[32,1024]{1,0:T(8,128)}, u32[]{:S(2)}) copy-start(f32[32,1024]{1,0:T(8,128)} %time_ref.1) | copy-start | bytes 393220
  3.0 9.9 %all-to-all-start = ((f32[4,72,128]{2,1,0:T(8,128)}), f32[4,72,128]{2,1,0:T(8,128)S(1)}, u32[]{:S(2)}, u32[]{:S(2)}) async-start(f32[4,72,128]{2,1,0:T(8,128)} %shard_map.58), calls=%async_computation | async-start | bytes 294912 | tf_op jit(solution)/shard_map/all_to_all | solution.py:387
  64.8 13.7 %all-to-all-start.4 = ((f32[16,16,128]{2,1,0:T(8,128)}), f32[16,16,128]{2,1,0:T(8,128)S(1)}, u32[]{:S(2)}, u32[]{:S(2)}) async-start(f32[16,16,128]{2,1,0:T(8,128)} %shard_map.63), calls=%async_computation.4 | async-start | bytes 262144 | tf_op jit(solution)/shard_map/all_to_all | solution.py:411
  79.8 8.1 %all-to-all-start.5 = ((f32[4,64,128]{2,1,0:T(8,128)}), f32[4,64,128]{2,1,0:T(8,128)S(1)}, u32[]{:S(2)}, u32[]{:S(2)}) async-start(f32[4,64,128]{2,1,0:T(8,128)} %get-tuple-element.25), calls=%async_computation.5 | async-start | bytes 262144 | tf_op jit(solution)/shard_map/all_to_all | solution.py:429
  123.9 13.5 %all-to-all-start.9 = ((f32[16,16,128]{2,1,0:T(8,128)}), f32[16,16,128]{2,1,0:T(8,128)S(1)}, u32[]{:S(2)}, u32[]{:S(2)}) async-start(f32[16,16,128]{2,1,0:T(8,128)} %shard_map.70), calls=%async_computation.9 | async-start | bytes 262144 | tf_op jit(solution)/shard_map/all_to_all | solution.py:411

commit v8 on v7

--- a/solution.py
+++ b/solution.py
@@ -155,7 +155,8 @@
             sent_ref[member, trial * size : (trial + 1) * size, :] = projected
 
 
-def project_body(time_hbm, trial_hbm, tensor_hbm, sent_ref, time_ref, trial_ref, tensor_ref, arrived):
+def project_body(time_hbm, trial_hbm, tensor_hbm, *refs):
+    sent_ref, tensor_ref, gram_ref, time_ref, trial_ref, arrived = refs
     count, size = trial_ref.shape
     copies = [
         pltpu.make_async_copy(time_hbm, time_ref, arrived.at[0]),
@@ -168,6 +169,7 @@
     for copy in copies:
         copy.start()
     copies[0].wait()
+    gram_ref[...] = gram_of(time_ref[...])
 
     def tensor_of(trial):
         copies[2 + trial].wait()
@@ -182,16 +184,15 @@
         sent_ref[member, count * size :, :] = tile
 
 
-def project(out, time_init, trial_rows, tensor):
+def project(outs, time_init, trial_rows, tensor):
     return pl.pallas_call(
         project_body,
-        out_shape=out,
+        out_shape=tuple(pltpu.VMEM(out.shape, out.dtype) for out in outs),
         in_specs=[pl.BlockSpec(memory_space=pl.ANY) for _ in range(3)],
-        out_specs=pl.BlockSpec(memory_space=pltpu.VMEM),
+        out_specs=tuple(pl.BlockSpec(memory_space=pltpu.VMEM) for _ in outs),
         scratch_shapes=[
             pltpu.VMEM(time_init.shape, time_init.dtype),
             pltpu.VMEM(trial_rows.shape, trial_rows.dtype),
-            pltpu.VMEM(tensor.shape, tensor.dtype),
             pltpu.SemaphoreType.DMA((2 + tensor.shape[0],)),
         ],
     )(time_init, trial_rows, tensor)
@@ -261,11 +262,10 @@
         sent_ref[member, main:, :] = halves
 
 
-def finish_body(neuron_count, got_ref, gram_ref, raw_ref, *outs):
-    neuron_ref, neuron_gram_ref, trial_ref, trial_gram_ref, own_ref, sent_ref = outs
+def finish_body(neuron_count, own_trials, last, got_ref, gram_ref, raw_ref, *outs):
+    neuron_gram_ref, trial_gram_ref, sent_ref, *rest = outs
     size = raw_ref.shape[0]
-    trial_count = trial_ref.shape[1]
-    own_trials = own_ref.shape[0]
+    trial_count = own_trials * sent_ref.shape[0]
     plane = lax.axis_index("x")
     total = got_ref[0].astype(jnp.float32)
     for member in range(1, got_ref.shape[0]):
@@ -275,17 +275,21 @@
     diagonal = raw_gram * eye_of(size)
     down = 1.0 / jnp.sqrt(jnp.sum(diagonal, axis=1, keepdims=True) / neuron_count + tiny_eps)
     across = 1.0 / jnp.sqrt(jnp.sum(diagonal, axis=0, keepdims=True) / neuron_count + tiny_eps)
-    neuron_ref[...] = raw_ref[...] * down
     neuron_gram = down * raw_gram * across
     neuron_gram_ref[...] = neuron_gram
     trial_now = product(damped_inverse(neuron_gram * gram_ref[...]), terms * down)
-    trial_ref[...] = trial_now
     trial_gram_ref[...] = gram_of(trial_now)
     lane = lax.broadcasted_iota(jnp.int32, trial_now.shape, 1)
-    row = lax.broadcasted_iota(jnp.int32, (own_trials, trial_count), 0)
-    column = lax.broadcasted_iota(jnp.int32, (own_trials, trial_count), 1)
-    chosen = (column == plane * own_trials + row).astype(jnp.float32)
-    own_ref[...] = rows_product(chosen, trial_now)
+    if last:
+        neuron_ref, own_ref = rest
+        neuron_ref[...] = raw_ref[...] * down
+        row = lax.broadcasted_iota(jnp.int32, (own_trials, trial_count), 0)
+        column = lax.broadcasted_iota(jnp.int32, (own_trials, trial_count), 1)
+        chosen = (column == plane * own_trials + row).astype(jnp.float32)
+        own_ref[...] = rows_product(chosen, trial_now)
+    else:
+        (trial_ref,) = rest
+        trial_ref[...] = trial_now
     columns = []
     for trial in range(own_trials):
         mine = lane == plane * own_trials + trial
@@ -309,11 +313,8 @@
         sent_ref[member] = total
 
 
-def inverse_body(left_ref, right_ref, out_ref):
-    out_ref[...] = damped_inverse(left_ref[...] * right_ref[...])
-
-
-def time_of(got_ref, inverse_ref):
+def time_of(got_ref, left_ref, right_ref):
+    inverse = damped_inverse(left_ref[...] * right_ref[...])
     members, half, lanes = got_ref.shape
     low = lax.broadcasted_iota(jnp.int32, (half, lanes), 1) < lanes // 2
     pieces = []
@@ -322,30 +323,26 @@
         upper = jnp.where(low, one, pltpu.roll(two, lanes // 2, 1))
         lower = jnp.where(low, pltpu.roll(one, lanes // 2, 1), two)
         pieces.append(jnp.concatenate([upper, lower], axis=0))
-    raw = product(inverse_ref[...], jnp.concatenate(pieces, axis=1))
+    raw = product(inverse, jnp.concatenate(pieces, axis=1))
     mean = jnp.sum(raw * raw, axis=1, keepdims=True) / raw.shape[1]
     return raw, jnp.sqrt(mean + tiny_eps)
 
 
-def next_body(got_ref, inverse_ref, tensor_ref, time_ref, sent_ref):
-    raw, norm = time_of(got_ref, inverse_ref)
+def next_body(got_ref, neuron_gram_ref, trial_gram_ref, tensor_ref, *outs):
+    sent_ref, gram_ref, inverse_ref = outs
+    raw, norm = time_of(got_ref, neuron_gram_ref, trial_gram_ref)
     time_now = raw / norm
-    time_ref[...] = time_now
     put_projected(time_now, lambda trial: tensor_ref[trial], sent_ref)
-
-
-def gram_body(time_ref, gram_ref):
-    gram_ref[...] = gram_of(time_ref[...])
-
-
-def next_inverse_body(time_ref, trial_gram_ref, gram_ref, inverse_ref):
-    gram = gram_of(time_ref[...])
+    gram = gram_of(time_now)
     gram_ref[...] = gram
     inverse_ref[...] = damped_inverse(gram * trial_gram_ref[...])
 
 
-def last_body(got_ref, inverse_ref, time_ref):
-    raw, norm = time_of(got_ref, inverse_ref)
+def last_body(got_ref, neuron_gram_ref, trial_gram_ref, *refs):
+    held_neuron_ref, held_own_ref, neuron_ref, time_ref, own_ref = refs
+    neuron_ref[...] = held_neuron_ref[...]
+    own_ref[...] = held_own_ref[...]
+    raw, norm = time_of(got_ref, neuron_gram_ref, trial_gram_ref)
     count, size = time_ref.shape
     lanes = got_ref.shape[2]
     position = lax.axis_index(("z", "pair", "y", "core", "x"))
@@ -381,54 +378,58 @@
         shape(components, own_neurons),
         shape(twins * blocks, components + 2 * PART, lanes, kind=WIRE),
     )
-    shared = project(
-        shape(planes, main + PART, own_neurons), time_init, trial_init.T, tensor
+    shared, tensor, time_gram = project(
+        (
+            shape(planes, main + PART, own_neurons),
+            shape(own_trials, own_neurons, timepoints, kind=tensor.dtype),
+            square,
+        ),
+        time_init,
+        trial_init.T,
+        tensor,
     )
     shared = lax.all_to_all(shared, "x", 0, 0)
-    time_gram = call(gram_body, square, time_init)
     raw, sent = call(first_neuron_body, neuron_outs, shared, time_gram, tensor)
     for sweep_index in range(SWEEPS):
         got = lax.all_to_all(sent, near, 0, 0)
         sent = call(reduce_body, shape(layers, components + 2 * PART, lanes, kind=WIRE), got)
         got = lax.all_to_all(sent, "z", 0, 0)
-        neuron_now, neuron_gram, trial_now, trial_gram, own_trial, sent = call(
-            lambda *refs: finish_body(neuron_count, *refs),
-            (
-                shape(components, own_neurons),
-                square,
-                shape(components, trial_count),
-                square,
-                shape(own_trials, components),
-                shape(planes, components // 2, lanes),
-            ),
+        last = sweep_index == SWEEPS - 1
+        neuron_shape = shape(components, own_neurons)
+        own_shape = shape(own_trials, components)
+        extra = (neuron_shape, own_shape) if last else (shape(components, trial_count),)
+        neuron_gram, trial_gram, sent, *rest = call(
+            lambda *refs: finish_body(neuron_count, own_trials, last, *refs),
+            (square, square, shape(planes, components // 2, lanes)) + extra,
             got,
             time_gram,
             raw,
-            slow=(0, 4) if sweep_index == SWEEPS - 1 else (),
         )
         got = lax.all_to_all(sent, "x", 0, 0)
         sent = call(sum_body, shape(twins * blocks, components // 2, lanes), got)
         got = lax.all_to_all(sent, near, 0, 0)
-        inverse = call(inverse_body, square, neuron_gram, trial_gram)
-        if sweep_index == SWEEPS - 1:
-            time_out = call(
+        if last:
+            share_width = timepoints // (layers * twins * blocks * planes)
+            neuron_now, time_out, own_trial = call(
                 last_body,
-                shape(timepoints // (layers * twins * blocks * planes), components),
+                (neuron_shape, shape(share_width, components), own_shape),
                 got,
-                inverse,
-                slow=(0,),
+                neuron_gram,
+                trial_gram,
+                *rest,
+                slow=(0, 1, 2),
             )
             break
-        time_now, shared = call(
+        shared, time_gram, inverse = call(
             next_body,
-            (shape(components, timepoints), shape(planes, main, own_neurons)),
+            (shape(planes, main, own_neurons), square, square),
             got,
-            inverse,
+            neuron_gram,
+            trial_gram,
             tensor,
         )
         shared = lax.all_to_all(shared, "x", 0, 0)
-        time_gram, inverse = call(next_inverse_body, (square, square), time_now, trial_gram)
-        raw, sent = call(neuron_body, neuron_outs, shared, trial_now, inverse, tensor)
+        raw, sent = call(neuron_body, neuron_outs, shared, rest[0], inverse, tensor)
     return (neuron_now, time_out.T, own_trial.T)
 
 

time: 139 us -> 136 us (0.978)
  blocking collectives: 80.2 us -> 123 us
  starting transfers between devices: 23 us -> 0 us
  waiting for transfers between devices: 18.8 us -> 0 us
  Pallas kernels: 15.9 us -> 11.6 us
    all_to_all x2 -> x4, blocking collectives: 26.5 us -> 51.9 us  [per_device(): got = lax.all_to_all(sent, near, 0, 0)]
    all_to_all x4 -> x0, starting transfers between devices: 23 us -> none  [the longest x2 14.7 us: per_device(): got = lax.all_to_all(sent, near, 0, 0)]
    all_to_all x4 -> x0, waiting for transfers between devices: 18.8 us -> none  [the longest x2 10.5 us: per_device(): got = lax.all_to_all(sent, near, 0, 0)]
    all_to_all x0 -> x2, blocking collectives: none -> 16.8 us  [per_device(): shared = lax.all_to_all(shared, 'x', 0, 0)]
    pallas_call x14 -> x10, Pallas kernels: 13.6 us -> 9.82 us  [call(): pl.pallas_call(body, out_shape=shapes, in_specs=[pl.BlockSpec(memory_spac...]
  transfers between devices with their start and end apart: 4 -> 0, of which waited for: 4 -> 0; matrix products, arithmetic and copies ran while one was open for 0% -> 0% of each run, Pallas kernels for 2% -> 0%
where the time goes in v8:
time: 136 us; the launch traced here: 135 us
  blocking collectives  123 us (90%)
  Pallas kernels  11.6 us (9%)
    all_to_all x4, blocking collectives, per_device(): got = lax.all_to_all(sent, near, 0, 0)  51.9 us
    all_to_all x2, blocking collectives, per_device(): got = lax.all_to_all(sent, 'z', 0, 0)  41.1 us
    all_to_all x2, blocking collectives, per_device(): shared = lax.all_to_all(shared, 'x', 0, 0)  16.8 us
    all_to_all x2, blocking collectives, per_device(): got = lax.all_to_all(sent, 'x', 0, 0)  13.3 us
    pallas_call x10, Pallas kernels, call(): pl.pallas_call(body, out_shape=shapes, in_specs=[pl.BlockSpec(memory_spac...  9.82 us

profile of v8, /device:TPU:1, one launch (start us, length us, event | category | flops | bytes accessed | tf_op | source)
XLA Modules:
  0.0 135.4 jit_solution(10881381840042114622)
XLA Ops:
  0.6 1.8 %shard_map.58 = (f32[4,72,128]{2,1,0:T(8,128)S(1)}, bf16[2,128,1024]{2,1,0:T(8,128)(2,1)S(1)}, f32[32,32]{1,0:T(8,128)S(1)}) custom-call(f32[32,1024]{1,0:T(8,128)} %time_hbm.1, f32[2,32]{1,0:T(2,128)} %bitcast.3, bf16[2,128,1024]{2,1,0:T(8,128)(2,1)} %tensor_hbm.1), custom_call_target="tpu_custom_call" | custom-call | tf_op jit(solution)/shard_map/pallas_call | solution.py:188
  2.4 9.5 %all_to_all.50.shared_ref = f32[4,72,128]{2,1,0:T(8,128)S(1)} all-to-all(f32[4,72,128]{2,1,0:T(8,128)S(1)} %get-tuple-element.25), channel_id=1, replica_groups=mesh['z'=8,'pair'=2,'y'=4,'core'=2,'x'=4] {'x'}, dimensions={0} | all-to-all | bytes 294912 | tf_op jit(solution)/shard_map/all_to_all | solution.py:391
  11.9 1.7 %shard_map.59 = (f32[32,128]{1,0:T(8,128)S(1)}, bf16[16,48,128]{2,1,0:T(8,128)(2,1)S(1)}) custom-call(f32[4,72,128]{2,1,0:T(8,128)S(1)} %all_to_all.50.shared_ref, f32[32,32]{1,0:T(8,128)S(1)} %get-tuple-element.26.gram_ref.refs_1_, bf16[2,128,1024]{2,1,0:T(8,128)(2,1)S(1)} %get-tuple-element.27.tensor_ref), custom_call_target="tpu_custom_call" | custom-call | tf_op jit(solution)/shard_map/pallas_call | solution.py:135
  13.7 14.8 %all_to_all.51.got_ref = bf16[16,48,128]{2,1,0:T(8,128)(2,1)S(1)} all-to-all(bf16[16,48,128]{2,1,0:T(8,128)(2,1)S(1)} %get-tuple-element.28), channel_id=1, replica_groups=mesh['z'=8,'pair'=2,'y'=4,'core'=2,'x'=4] {'pair','y','core'}, dimensions={0} | all-to-all | bytes 393216 | tf_op jit(solution)/shard_map/all_to_all | solution.py:394
  28.5 26.0 %all_to_all.52.refs_0_ = bf16[8,48,128]{2,1,0:T(8,128)(2,1)S(1)} all-to-all(bf16[8,48,128]{2,1,0:T(8,128)(2,1)S(1)} %shard_map.60), channel_id=1, replica_groups=mesh['z'=8,'pair'=2,'y'=4,'core'=2,'x'=4] {'z'}, dimensions={0} | all-to-all | bytes 196608 | tf_op jit(solution)/shard_map/all_to_all | solution.py:396
  54.5 1.4 %shard_map.61 = (f32[32,32]{1,0:T(8,128)S(1)}, f32[32,32]{1,0:T(8,128)S(1)}, f32[4,16,128]{2,1,0:T(8,128)S(1)}, f32[32,8]{1,0:T(8,128)S(1)}) custom-call(bf16[8,48,128]{2,1,0:T(8,128)(2,1)S(1)} %all_to_all.52.refs_0_, f32[32,32]{1,0:T(8,128)S(1)} %get-tuple-element.26.gram_ref.refs_1_, f32[32,128]{1,0:T(8,128)S(1)} %get-tuple-element.29.refs_2_), custom_call_target="tpu_custom_call" | custom-call | tf_op jit(solution)/shard_map/pallas_call | solution.py:135
  56.0 6.7 %all_to_all.53.got_ref = f32[4,16,128]{2,1,0:T(8,128)S(1)} all-to-all(f32[4,16,128]{2,1,0:T(8,128)S(1)} %get-tuple-element.30), channel_id=1, replica_groups=mesh['z'=8,'pair'=2,'y'=4,'core'=2,'x'=4] {'x'}, dimensions={0} | all-to-all | bytes 65536 | tf_op jit(solution)/shard_map/all_to_all | solution.py:408
  62.7 13.1 %all_to_all.54.got_ref = f32[16,16,128]{2,1,0:T(8,128)S(1)} all-to-all(f32[16,16,128]{2,1,0:T(8,128)S(1)} %shard_map.62), channel_id=1, replica_groups=mesh['z'=8,'pair'=2,'y'=4,'core'=2,'x'=4] {'pair','y','core'}, dimensions={0} | all-to-all | bytes 262144 | tf_op jit(solution)/shard_map/all_to_all | solution.py:410
  75.8 2.5 %shard_map.63 = (f32[4,64,128]{2,1,0:T(8,128)S(1)}, f32[32,32]{1,0:T(8,128)S(1)}, f32[32,32]{1,0:T(8,128)S(1)}) custom-call(f32[16,16,128]{2,1,0:T(8,128)S(1)} %all_to_all.54.got_ref, f32[32,32]{1,0:T(8,128)S(1)} %get-tuple-element.31.neuron_gram_ref, f32[32,32]{1,0:T(8,128)S(1)} %get-tuple-element.32.trial_gram_ref, ...), custom_call_target="tpu_custom_call" | custom-call | tf_op jit(solution)/shard_map/pallas_call | solution.py:135
  78.3 7.2 %all_to_all.55.shared_ref = f32[4,64,128]{2,1,0:T(8,128)S(1)} all-to-all(f32[4,64,128]{2,1,0:T(8,128)S(1)} %get-tuple-element.33), channel_id=1, replica_groups=mesh['z'=8,'pair'=2,'y'=4,'core'=2,'x'=4] {'x'}, dimensions={0} | all-to-all | bytes 262144 | tf_op jit(solution)/shard_map/all_to_all | solution.py:431
  85.5 0.6 shard_map.64
  86.1 10.9 %all_to_all.56.got_ref = bf16[16,48,128]{2,1,0:T(8,128)(2,1)S(1)} all-to-all(bf16[16,48,128]{2,1,0:T(8,128)(2,1)S(1)} %get-tuple-element.36), channel_id=1, replica_groups=mesh['z'=8,'pair'=2,'y'=4,'core'=2,'x'=4] {'pair','y','core'}, dimensions={0} | all-to-all | bytes 393216 | tf_op jit(solution)/shard_map/all_to_all | solution.py:394
  97.0 15.1 %all_to_all.57.refs_0_ = bf16[8,48,128]{2,1,0:T(8,128)(2,1)S(1)} all-to-all(bf16[8,48,128]{2,1,0:T(8,128)(2,1)S(1)} %shard_map.65), channel_id=1, replica_groups=mesh['z'=8,'pair'=2,'y'=4,'core'=2,'x'=4] {'z'}, dimensions={0} | all-to-all | bytes 196608 | tf_op jit(solution)/shard_map/all_to_all | solution.py:396
  112.1 1.5 %shard_map.66 = (f32[32,32]{1,0:T(8,128)S(1)}, f32[32,32]{1,0:T(8,128)S(1)}, f32[4,16,128]{2,1,0:T(8,128)S(1)}, f32[32,128]{1,0:T(8,128)S(1)}, f32[2,32]{1,0:T(2,128)S(1)}) custom-call(bf16[8,48,128]{2,1,0:T(8,128)(2,1)S(1)} %all_to_all.57.refs_0_, f32[32,32]{1,0:T(8,128)S(1)} %get-tuple-element.37.refs_1_, f32[32,128]{1,0:T(8,128)S(1)} %get-tuple-element.38.refs_2_), custom_call_target="tpu_custom_call" | custom-call | tf_op jit(solution)/shard_map/pallas_call | solution.py:135
  113.6 6.7 %all_to_all.58.got_ref = f32[4,16,128]{2,1,0:T(8,128)S(1)} all-to-all(f32[4,16,128]{2,1,0:T(8,128)S(1)} %get-tuple-element.39), channel_id=1, replica_groups=mesh['z'=8,'pair'=2,'y'=4,'core'=2,'x'=4] {'x'}, dimensions={0} | all-to-all | bytes 65536 | tf_op jit(solution)/shard_map/all_to_all | solution.py:408
  120.3 13.1 %all_to_all.59.got_ref = f32[16,16,128]{2,1,0:T(8,128)S(1)} all-to-all(f32[16,16,128]{2,1,0:T(8,128)S(1)} %shard_map.67), channel_id=1, replica_groups=mesh['z'=8,'pair'=2,'y'=4,'core'=2,'x'=4] {'pair','y','core'}, dimensions={0} | all-to-all | bytes 262144 | tf_op jit(solution)/shard_map/all_to_all | solution.py:410
  133.3 2.0 %shard_map.68 = (f32[32,128]{1,0:T(8,128)}, f32[2,32]{1,0:T(2,128)}, f32[2,32]{1,0:T(2,128)}) custom-call(f32[16,16,128]{2,1,0:T(8,128)S(1)} %all_to_all.59.got_ref, f32[32,32]{1,0:T(8,128)S(1)} %get-tuple-element.40.neuron_gram_ref, f32[32,32]{1,0:T(8,128)S(1)} %get-tuple-element.41.trial_gram_ref, f32[32,128]{1,0:T(8,128)S(1)} %get-tuple-element.42.refs_0_, ...), custom_call_target="tpu_custom_call" | custom-call | tf_op jit(solution)/shard_map/pallas_call | solution.py:135
  (4 shorter events, 0.1 us)

commit v9 on v8

--- a/solution.py
+++ b/solution.py
@@ -12,6 +12,7 @@
 tiny_eps = 1e-06
 EXACT = lax.Precision.HIGHEST
 PART = 8
+AHEAD = 3
 WIRE = jnp.bfloat16
 
 
@@ -61,8 +62,9 @@
     eye = eye_of(size)
     trace = jnp.sum(jnp.sum(system * eye, axis=1, keepdims=True), axis=0, keepdims=True)
     share = size / trace
-    both = jnp.concatenate([system * share + ridge_share * eye, eye], axis=1)
+    both = system * share + ridge_share * eye
     row = lax.broadcasted_iota(jnp.int32, both.shape, 0)
+    lane = lax.broadcasted_iota(jnp.int32, both.shape, 1)
 
     def pivots(step):
         if step >= size:
@@ -71,7 +73,7 @@
             jnp.broadcast_to(both[:, place : place + 1], both.shape) for place in (step, step + 1)
         ]
 
-    ahead = [pivots(0), pivots(2)]
+    ahead = [pivots(2 * place) for place in range(AHEAD)]
     for step in range(0, size, 2):
         first, second = ahead[0]
         p00, p01 = first[step : step + 1], second[step : step + 1]
@@ -86,9 +88,10 @@
             rest = matrix - first * new_upper - second * new_lower
             return jnp.where(row == step, new_upper, jnp.where(row == step + 1, new_lower, rest))
 
-        ahead = [[cleared(one) for one in ahead[1]], [cleared(one) for one in pivots(step + 4)]]
-        both = cleared(both)
-    return both[:, size:] * share
+        ahead = [[cleared(one) for one in pair] for pair in ahead[1:] + [pivots(step + 2 * AHEAD)]]
+        inner = jnp.logical_or(lane == step, lane == step + 1)
+        both = cleared(jnp.where(inner, eye, both))
+    return both * share
 
 
 def pack_small(gram, terms):
@@ -323,17 +326,19 @@
         upper = jnp.where(low, one, pltpu.roll(two, lanes // 2, 1))
         lower = jnp.where(low, pltpu.roll(one, lanes // 2, 1), two)
         pieces.append(jnp.concatenate([upper, lower], axis=0))
-    raw = product(inverse, jnp.concatenate(pieces, axis=1))
-    mean = jnp.sum(raw * raw, axis=1, keepdims=True) / raw.shape[1]
-    return raw, jnp.sqrt(mean + tiny_eps)
+    return product(inverse, jnp.concatenate(pieces, axis=1))
 
 
 def next_body(got_ref, neuron_gram_ref, trial_gram_ref, tensor_ref, *outs):
     sent_ref, gram_ref, inverse_ref = outs
-    raw, norm = time_of(got_ref, neuron_gram_ref, trial_gram_ref)
-    time_now = raw / norm
-    put_projected(time_now, lambda trial: tensor_ref[trial], sent_ref)
-    gram = gram_of(time_now)
+    raw = time_of(got_ref, neuron_gram_ref, trial_gram_ref)
+    raw_gram = gram_of(raw)
+    diagonal = raw_gram * eye_of(raw.shape[0])
+    count = raw.shape[1]
+    down = 1.0 / jnp.sqrt(jnp.sum(diagonal, axis=1, keepdims=True) / count + tiny_eps)
+    across = 1.0 / jnp.sqrt(jnp.sum(diagonal, axis=0, keepdims=True) / count + tiny_eps)
+    put_projected(raw * down, lambda trial: tensor_ref[trial], sent_ref)
+    gram = down * raw_gram * across
     gram_ref[...] = gram
     inverse_ref[...] = damped_inverse(gram * trial_gram_ref[...])
 
@@ -342,7 +347,9 @@
     held_neuron_ref, held_own_ref, neuron_ref, time_ref, own_ref = refs
     neuron_ref[...] = held_neuron_ref[...]
     own_ref[...] = held_own_ref[...]
-    raw, norm = time_of(got_ref, neuron_gram_ref, trial_gram_ref)
+    raw = time_of(got_ref, neuron_gram_ref, trial_gram_ref)
+    mean = jnp.sum(raw * raw, axis=1, keepdims=True) / raw.shape[1]
+    down = 1.0 / jnp.sqrt(mean + tiny_eps)
     count, size = time_ref.shape
     lanes = got_ref.shape[2]
     position = lax.axis_index(("z", "pair", "y", "core", "x"))
@@ -354,7 +361,7 @@
     row = lax.broadcasted_iota(jnp.int32, (count, lanes), 0)
     lane = lax.broadcasted_iota(jnp.int32, (count, lanes), 1)
     chosen = (lane == position * count % lanes + row).astype(jnp.float32)
-    time_ref[...] = rows_product(chosen, picked / norm)
+    time_ref[...] = rows_product(chosen, picked * down)
 
 
 def per_device(tensor, time_init, trial_init):

time: 136 us -> 135 us (level)
  no operation moved by 1% of the time
where the time goes in v9:
time: 135 us; the launch traced here: 134 us
  blocking collectives  123 us (91%)
  Pallas kernels  10.6 us (8%)
    all_to_all x4, blocking collectives, per_device(): got = lax.all_to_all(sent, near, 0, 0)  51.9 us
    all_to_all x2, blocking collectives, per_device(): got = lax.all_to_all(sent, 'z', 0, 0)  41.1 us
    all_to_all x2, blocking collectives, per_device(): shared = lax.all_to_all(shared, 'x', 0, 0)  16.8 us
    all_to_all x2, blocking collectives, per_device(): got = lax.all_to_all(sent, 'x', 0, 0)  13.3 us
    pallas_call x10, Pallas kernels, call(): pl.pallas_call(body, out_shape=shapes, in_specs=[pl.BlockSpec(memory_spac...  8.84 us

profile of v9, /device:TPU:1, one launch (start us, length us, event | category | flops | bytes accessed | tf_op | source)
XLA Modules:
  0.0 134.4 jit_solution(6945287671157239037)
XLA Ops:
  0.6 1.8 %shard_map.58 = (f32[4,72,128]{2,1,0:T(8,128)S(1)}, bf16[2,128,1024]{2,1,0:T(8,128)(2,1)S(1)}, f32[32,32]{1,0:T(8,128)S(1)}) custom-call(f32[32,1024]{1,0:T(8,128)} %time_hbm.1, f32[2,32]{1,0:T(2,128)} %bitcast.3, bf16[2,128,1024]{2,1,0:T(8,128)(2,1)} %tensor_hbm.1), custom_call_target="tpu_custom_call" | custom-call | tf_op jit(solution)/shard_map/pallas_call | solution.py:191
  2.4 9.5 %all_to_all.50.shared_ref = f32[4,72,128]{2,1,0:T(8,128)S(1)} all-to-all(f32[4,72,128]{2,1,0:T(8,128)S(1)} %get-tuple-element.25), channel_id=1, replica_groups=mesh['z'=8,'pair'=2,'y'=4,'core'=2,'x'=4] {'x'}, dimensions={0} | all-to-all | bytes 294912 | tf_op jit(solution)/shard_map/all_to_all | solution.py:398
  11.9 1.6 %shard_map.59 = (f32[32,128]{1,0:T(8,128)S(1)}, bf16[16,48,128]{2,1,0:T(8,128)(2,1)S(1)}) custom-call(f32[4,72,128]{2,1,0:T(8,128)S(1)} %all_to_all.50.shared_ref, f32[32,32]{1,0:T(8,128)S(1)} %get-tuple-element.26.gram_ref.refs_1_, bf16[2,128,1024]{2,1,0:T(8,128)(2,1)S(1)} %get-tuple-element.27.tensor_ref), custom_call_target="tpu_custom_call" | custom-call | tf_op jit(solution)/shard_map/pallas_call | solution.py:138
  13.5 14.8 %all_to_all.51.got_ref = bf16[16,48,128]{2,1,0:T(8,128)(2,1)S(1)} all-to-all(bf16[16,48,128]{2,1,0:T(8,128)(2,1)S(1)} %get-tuple-element.28), channel_id=1, replica_groups=mesh['z'=8,'pair'=2,'y'=4,'core'=2,'x'=4] {'pair','y','core'}, dimensions={0} | all-to-all | bytes 393216 | tf_op jit(solution)/shard_map/all_to_all | solution.py:401
  28.4 26.0 %all_to_all.52.refs_0_ = bf16[8,48,128]{2,1,0:T(8,128)(2,1)S(1)} all-to-all(bf16[8,48,128]{2,1,0:T(8,128)(2,1)S(1)} %shard_map.60), channel_id=1, replica_groups=mesh['z'=8,'pair'=2,'y'=4,'core'=2,'x'=4] {'z'}, dimensions={0} | all-to-all | bytes 196608 | tf_op jit(solution)/shard_map/all_to_all | solution.py:403
  54.4 1.3 shard_map.61
  55.7 6.7 %all_to_all.53.got_ref = f32[4,16,128]{2,1,0:T(8,128)S(1)} all-to-all(f32[4,16,128]{2,1,0:T(8,128)S(1)} %get-tuple-element.30), channel_id=1, replica_groups=mesh['z'=8,'pair'=2,'y'=4,'core'=2,'x'=4] {'x'}, dimensions={0} | all-to-all | bytes 65536 | tf_op jit(solution)/shard_map/all_to_all | solution.py:415
  62.4 13.1 %all_to_all.54.got_ref = f32[16,16,128]{2,1,0:T(8,128)S(1)} all-to-all(f32[16,16,128]{2,1,0:T(8,128)S(1)} %shard_map.62), channel_id=1, replica_groups=mesh['z'=8,'pair'=2,'y'=4,'core'=2,'x'=4] {'pair','y','core'}, dimensions={0} | all-to-all | bytes 262144 | tf_op jit(solution)/shard_map/all_to_all | solution.py:417
  75.5 2.1 %shard_map.63 = (f32[4,64,128]{2,1,0:T(8,128)S(1)}, f32[32,32]{1,0:T(8,128)S(1)}, f32[32,32]{1,0:T(8,128)S(1)}) custom-call(f32[16,16,128]{2,1,0:T(8,128)S(1)} %all_to_all.54.got_ref, f32[32,32]{1,0:T(8,128)S(1)} %get-tuple-element.31.neuron_gram_ref, f32[32,32]{1,0:T(8,128)S(1)} %get-tuple-element.32.trial_gram_ref, ...), custom_call_target="tpu_custom_call" | custom-call | tf_op jit(solution)/shard_map/pallas_call | solution.py:138
  77.6 7.2 %all_to_all.55.shared_ref = f32[4,64,128]{2,1,0:T(8,128)S(1)} all-to-all(f32[4,64,128]{2,1,0:T(8,128)S(1)} %get-tuple-element.33), channel_id=1, replica_groups=mesh['z'=8,'pair'=2,'y'=4,'core'=2,'x'=4] {'x'}, dimensions={0} | all-to-all | bytes 262144 | tf_op jit(solution)/shard_map/all_to_all | solution.py:438
  84.8 0.6 shard_map.64
  85.4 10.9 %all_to_all.56.got_ref = bf16[16,48,128]{2,1,0:T(8,128)(2,1)S(1)} all-to-all(bf16[16,48,128]{2,1,0:T(8,128)(2,1)S(1)} %get-tuple-element.36), channel_id=1, replica_groups=mesh['z'=8,'pair'=2,'y'=4,'core'=2,'x'=4] {'pair','y','core'}, dimensions={0} | all-to-all | bytes 393216 | tf_op jit(solution)/shard_map/all_to_all | solution.py:401
  96.4 15.1 %all_to_all.57.refs_0_ = bf16[8,48,128]{2,1,0:T(8,128)(2,1)S(1)} all-to-all(bf16[8,48,128]{2,1,0:T(8,128)(2,1)S(1)} %shard_map.65), channel_id=1, replica_groups=mesh['z'=8,'pair'=2,'y'=4,'core'=2,'x'=4] {'z'}, dimensions={0} | all-to-all | bytes 196608 | tf_op jit(solution)/shard_map/all_to_all | solution.py:403
  111.5 1.3 shard_map.66
  112.8 6.7 %all_to_all.58.got_ref = f32[4,16,128]{2,1,0:T(8,128)S(1)} all-to-all(f32[4,16,128]{2,1,0:T(8,128)S(1)} %get-tuple-element.39), channel_id=1, replica_groups=mesh['z'=8,'pair'=2,'y'=4,'core'=2,'x'=4] {'x'}, dimensions={0} | all-to-all | bytes 65536 | tf_op jit(solution)/shard_map/all_to_all | solution.py:415
  119.5 13.1 %all_to_all.59.got_ref = f32[16,16,128]{2,1,0:T(8,128)S(1)} all-to-all(f32[16,16,128]{2,1,0:T(8,128)S(1)} %shard_map.67), channel_id=1, replica_groups=mesh['z'=8,'pair'=2,'y'=4,'core'=2,'x'=4] {'pair','y','core'}, dimensions={0} | all-to-all | bytes 262144 | tf_op jit(solution)/shard_map/all_to_all | solution.py:417
  132.5 1.8 %shard_map.68 = (f32[32,128]{1,0:T(8,128)}, f32[2,32]{1,0:T(2,128)}, f32[2,32]{1,0:T(2,128)}) custom-call(f32[16,16,128]{2,1,0:T(8,128)S(1)} %all_to_all.59.got_ref, f32[32,32]{1,0:T(8,128)S(1)} %get-tuple-element.40.neuron_gram_ref, f32[32,32]{1,0:T(8,128)S(1)} %get-tuple-element.41.trial_gram_ref, f32[32,128]{1,0:T(8,128)S(1)} %get-tuple-element.42.refs_0_, ...), custom_call_target="tpu_custom_call" | custom-call | tf_op jit(solution)/shard_map/pallas_call | solution.py:138
  (4 shorter events, 0.1 us)

commit v10 on v9

--- a/solution.py
+++ b/solution.py
@@ -144,22 +144,37 @@
     return result[0] if single else result
 
 
-def put_projected(time_now, tensor_of, sent_ref):
+def put_projected(time_now, trial_own, tensor_of, projected_ref, sent_ref):
     rounded = time_now.astype(jnp.bfloat16)
     size = time_now.shape[0]
-    for trial in range(sent_ref.shape[1] // size):
+    part = None
+    for trial in range(trial_own.shape[1]):
         projected = lax.dot_general(
             rounded,
             tensor_of(trial),
             (((1,), (1,)), ((), ())),
             preferred_element_type=jnp.float32,
         )
-        for member in range(sent_ref.shape[0]):
-            sent_ref[member, trial * size : (trial + 1) * size, :] = projected
+        projected_ref[trial] = projected
+        scaled = trial_own[:, trial : trial + 1] * projected
+        part = scaled if part is None else part + scaled
+    for member in range(sent_ref.shape[0]):
+        sent_ref[member, :size, :] = part
+
+
+def tile_of(rows, lanes):
+    count, size = rows.shape
+    tile = jnp.concatenate([rows, jnp.zeros((PART - count, size), jnp.float32)], axis=0)
+    return jnp.concatenate([tile, jnp.zeros((PART, lanes - size), jnp.float32)], axis=1)
+
+
+def trial_of(got_ref, start, count, size):
+    lines = [got_ref[member, start : start + count, :size] for member in range(got_ref.shape[0])]
+    return rows_product(eye_of(size), jnp.concatenate(lines, axis=0))
 
 
 def project_body(time_hbm, trial_hbm, tensor_hbm, *refs):
-    sent_ref, tensor_ref, gram_ref, time_ref, trial_ref, arrived = refs
+    sent_ref, projected_ref, tensor_ref, gram_ref, time_ref, trial_ref, arrived = refs
     count, size = trial_ref.shape
     copies = [
         pltpu.make_async_copy(time_hbm, time_ref, arrived.at[0]),
@@ -178,13 +193,12 @@
         copies[2 + trial].wait()
         return tensor_ref[trial]
 
-    put_projected(time_ref[...], tensor_of, sent_ref)
     copies[1].wait()
-    lanes = sent_ref.shape[2]
-    tile = jnp.concatenate([trial_ref[...], jnp.zeros((PART - count, size), jnp.float32)], axis=0)
-    tile = jnp.concatenate([tile, jnp.zeros((PART, lanes - size), jnp.float32)], axis=1)
+    trial_own = rows_product(eye_of(size), trial_ref[...])
+    put_projected(time_ref[...], trial_own, tensor_of, projected_ref, sent_ref)
+    tile = tile_of(trial_ref[...], sent_ref.shape[2])
     for member in range(sent_ref.shape[0]):
-        sent_ref[member, count * size :, :] = tile
+        sent_ref[member, size:, :] = tile
 
 
 def project(outs, time_init, trial_rows, tensor):
@@ -201,24 +215,17 @@
     )(time_init, trial_rows, tensor)
 
 
-def put_neuron(trial_now, inverse, shared_ref, tensor_ref, raw_ref, sent_ref):
-    size, trial_count = trial_now.shape
-    own_trials = tensor_ref.shape[0]
-    terms = []
-    projected = []
-    for trial in range(trial_count):
-        start = trial % own_trials * size
-        projected.append(shared_ref[trial // own_trials, start : start + size, :])
-    neuron_terms = trial_now[:, 0:1] * projected[0]
-    for trial in range(1, trial_count):
-        neuron_terms = neuron_terms + trial_now[:, trial : trial + 1] * projected[trial]
+def put_neuron(inverse, shared_ref, projected_ref, tensor_ref, raw_ref, sent_ref):
+    own_trials, size, _ = projected_ref.shape
+    neuron_terms = shared_ref[0, :size, :]
+    for member in range(1, shared_ref.shape[0]):
+        neuron_terms = neuron_terms + shared_ref[member, :size, :]
     raw = product(inverse, neuron_terms)
     raw_ref[...] = raw
-    lane = lax.broadcasted_iota(jnp.int32, (size, trial_count), 1)
-    terms = jnp.zeros((size, trial_count), jnp.float32)
-    for trial in range(trial_count):
-        one = jnp.sum(raw * projected[trial], axis=1, keepdims=True)
-        terms = jnp.where(lane == trial, one, terms)
+    terms = [
+        jnp.sum(raw * projected_ref[trial], axis=1, keepdims=True) for trial in range(own_trials)
+    ]
+    terms = jnp.concatenate(terms, axis=1)
     small = split(pack_small(gram_of(raw), terms))
     members, _, lanes = sent_ref.shape
     blocks = tensor_ref.shape[2] // lanes
@@ -236,21 +243,15 @@
         sent_ref[member, size:, :] = small
 
 
-def first_neuron_body(shared_ref, gram_ref, tensor_ref, raw_ref, sent_ref):
-    own_trials = tensor_ref.shape[0]
-    size = raw_ref.shape[0]
-    main = own_trials * size
-    lines = [
-        shared_ref[member, main : main + own_trials, :size]
-        for member in range(shared_ref.shape[0])
-    ]
-    trial_now = rows_product(eye_of(size), jnp.concatenate(lines, axis=0))
+def first_neuron_body(shared_ref, projected_ref, gram_ref, tensor_ref, raw_ref, sent_ref):
+    own_trials, size, _ = projected_ref.shape
+    trial_now = trial_of(shared_ref, size, own_trials, size)
     inverse = damped_inverse(gram_of(trial_now) * gram_ref[...])
-    put_neuron(trial_now, inverse, shared_ref, tensor_ref, raw_ref, sent_ref)
-
-
-def neuron_body(shared_ref, trial_ref, inverse_ref, tensor_ref, raw_ref, sent_ref):
-    put_neuron(trial_ref[...], inverse_ref[...], shared_ref, tensor_ref, raw_ref, sent_ref)
+    put_neuron(inverse, shared_ref, projected_ref, tensor_ref, raw_ref, sent_ref)
+
+
+def neuron_body(shared_ref, projected_ref, inverse_ref, tensor_ref, raw_ref, sent_ref):
+    put_neuron(inverse_ref[...], shared_ref, projected_ref, tensor_ref, raw_ref, sent_ref)
 
 
 def reduce_body(got_ref, sent_ref):
@@ -266,37 +267,28 @@
 
 
 def finish_body(neuron_count, own_trials, last, got_ref, gram_ref, raw_ref, *outs):
-    neuron_gram_ref, trial_gram_ref, sent_ref, *rest = outs
+    neuron_gram_ref, sent_ref, *rest = outs
     size = raw_ref.shape[0]
-    trial_count = own_trials * sent_ref.shape[0]
-    plane = lax.axis_index("x")
     total = got_ref[0].astype(jnp.float32)
     for member in range(1, got_ref.shape[0]):
         total = total + got_ref[member].astype(jnp.float32)
     small = total[size : size + PART] + total[size + PART :]
-    raw_gram, terms = unpack_small(small, size, trial_count)
+    raw_gram, terms = unpack_small(small, size, own_trials)
     diagonal = raw_gram * eye_of(size)
     down = 1.0 / jnp.sqrt(jnp.sum(diagonal, axis=1, keepdims=True) / neuron_count + tiny_eps)
     across = 1.0 / jnp.sqrt(jnp.sum(diagonal, axis=0, keepdims=True) / neuron_count + tiny_eps)
     neuron_gram = down * raw_gram * across
     neuron_gram_ref[...] = neuron_gram
-    trial_now = product(damped_inverse(neuron_gram * gram_ref[...]), terms * down)
-    trial_gram_ref[...] = gram_of(trial_now)
-    lane = lax.broadcasted_iota(jnp.int32, trial_now.shape, 1)
+    trial_own = product(damped_inverse(neuron_gram * gram_ref[...]), terms * down)
+    trial_rows = rows_product(eye_of(own_trials), trial_own)
     if last:
         neuron_ref, own_ref = rest
         neuron_ref[...] = raw_ref[...] * down
-        row = lax.broadcasted_iota(jnp.int32, (own_trials, trial_count), 0)
-        column = lax.broadcasted_iota(jnp.int32, (own_trials, trial_count), 1)
-        chosen = (column == plane * own_trials + row).astype(jnp.float32)
-        own_ref[...] = rows_product(chosen, trial_now)
+        own_ref[...] = trial_rows
     else:
-        (trial_ref,) = rest
-        trial_ref[...] = trial_now
-    columns = []
-    for trial in range(own_trials):
-        mine = lane == plane * own_trials + trial
-        columns.append(jnp.sum(jnp.where(mine, trial_now, 0.0), axis=1, keepdims=True))
+        (own_ref,) = rest
+        own_ref[...] = trial_own
+    columns = [trial_own[:, trial : trial + 1] for trial in range(own_trials)]
     lanes = total.shape[1]
     low = lax.broadcasted_iota(jnp.int32, (size, lanes), 1) < lanes // 2
     same = low == (lax.axis_index("pair") == 0)
@@ -304,16 +296,20 @@
     weighted = weighted + pltpu.roll(weighted, lanes // 2, 1)
     half = size // 2
     weighted = jnp.where(low[:half], weighted[:half], weighted[half:])
+    tile = tile_of(trial_rows, lanes)
     for member in range(sent_ref.shape[0]):
-        sent_ref[member] = weighted
-
-
-def sum_body(got_ref, sent_ref):
-    total = got_ref[0]
+        sent_ref[member, :half, :] = weighted
+        sent_ref[member, half:, :] = tile
+
+
+def sum_body(own_trials, got_ref, sent_ref, trial_gram_ref):
+    _, half, lanes = sent_ref.shape
+    total = got_ref[0, :half, :]
     for member in range(1, got_ref.shape[0]):
-        total = total + got_ref[member]
+        total = total + got_ref[member, :half, :]
     for member in range(sent_ref.shape[0]):
         sent_ref[member] = total
+    trial_gram_ref[...] = gram_of(trial_of(got_ref, half, own_trials, 2 * half))
 
 
 def time_of(got_ref, left_ref, right_ref):
@@ -329,15 +325,16 @@
     return product(inverse, jnp.concatenate(pieces, axis=1))
 
 
-def next_body(got_ref, neuron_gram_ref, trial_gram_ref, tensor_ref, *outs):
-    sent_ref, gram_ref, inverse_ref = outs
+def next_body(got_ref, neuron_gram_ref, trial_gram_ref, own_ref, tensor_ref, *outs):
+    sent_ref, projected_ref, gram_ref, inverse_ref = outs
     raw = time_of(got_ref, neuron_gram_ref, trial_gram_ref)
     raw_gram = gram_of(raw)
     diagonal = raw_gram * eye_of(raw.shape[0])
     count = raw.shape[1]
     down = 1.0 / jnp.sqrt(jnp.sum(diagonal, axis=1, keepdims=True) / count + tiny_eps)
     across = 1.0 / jnp.sqrt(jnp.sum(diagonal, axis=0, keepdims=True) / count + tiny_eps)
-    put_projected(raw * down, lambda trial: tensor_ref[trial], sent_ref)
+    tensor_of = lambda trial: tensor_ref[trial]
+    put_projected(raw * down, own_ref[...], tensor_of, projected_ref, sent_ref)
     gram = down * raw_gram * across
     gram_ref[...] = gram
     inverse_ref[...] = damped_inverse(gram * trial_gram_ref[...])
@@ -373,9 +370,7 @@
     blocks, layers = lax.axis_size(short), lax.axis_size("z")
     twins = lax.axis_size("pair")
     neuron_count = own_neurons * blocks * twins * layers
-    trial_count = own_trials * planes
     lanes = timepoints // blocks
-    main = own_trials * components
 
     def shape(*dims, kind=jnp.float32):
         return jax.ShapeDtypeStruct(dims, kind)
@@ -385,9 +380,11 @@
         shape(components, own_neurons),
         shape(twins * blocks, components + 2 * PART, lanes, kind=WIRE),
     )
-    shared, tensor, time_gram = project(
+    projected_shape = shape(own_trials, components, own_neurons)
+    shared, projected, tensor, time_gram = project(
         (
-            shape(planes, main + PART, own_neurons),
+            shape(planes, components + PART, own_neurons),
+            projected_shape,
             shape(own_trials, own_neurons, timepoints, kind=tensor.dtype),
             square,
         ),
@@ -396,7 +393,7 @@
         tensor,
     )
     shared = lax.all_to_all(shared, "x", 0, 0)
-    raw, sent = call(first_neuron_body, neuron_outs, shared, time_gram, tensor)
+    raw, sent = call(first_neuron_body, neuron_outs, shared, projected, time_gram, tensor)
     for sweep_index in range(SWEEPS):
         got = lax.all_to_all(sent, near, 0, 0)
         sent = call(reduce_body, shape(layers, components + 2 * PART, lanes, kind=WIRE), got)
@@ -404,16 +401,20 @@
         last = sweep_index == SWEEPS - 1
         neuron_shape = shape(components, own_neurons)
         own_shape = shape(own_trials, components)
-        extra = (neuron_shape, own_shape) if last else (shape(components, trial_count),)
-        neuron_gram, trial_gram, sent, *rest = call(
+        extra = (neuron_shape, own_shape) if last else (shape(components, own_trials),)
+        neuron_gram, sent, *rest = call(
             lambda *refs: finish_body(neuron_count, own_trials, last, *refs),
-            (square, square, shape(planes, components // 2, lanes)) + extra,
+            (square, shape(planes, components // 2 + PART, lanes)) + extra,
             got,
             time_gram,
             raw,
         )
         got = lax.all_to_all(sent, "x", 0, 0)
-        sent = call(sum_body, shape(twins * blocks, components // 2, lanes), got)
+        sent, trial_gram = call(
+            lambda *refs: sum_body(own_trials, *refs),
+            (shape(twins * blocks, components // 2, lanes), square),
+            got,
+        )
         got = lax.all_to_all(sent, near, 0, 0)
         if last:
             share_width = timepoints // (layers * twins * blocks * planes)
@@ -427,16 +428,17 @@
                 slow=(0, 1, 2),
             )
             break
-        shared, time_gram, inverse = call(
+        shared, projected, time_gram, inverse = call(
             next_body,
-            (shape(planes, main, own_neurons), square, square),
+            (shape(planes, components, own_neurons), projected_shape, square, square),
             got,
             neuron_gram,
             trial_gram,
+            *rest,
             tensor,
         )
         shared = lax.all_to_all(shared, "x", 0, 0)
-        raw, sent = call(neuron_body, neuron_outs, shared, rest[0], inverse, tensor)
+        raw, sent = call(neuron_body, neuron_outs, shared, projected, inverse, tensor)
     return (neuron_now, time_out.T, own_trial.T)
 
 

time: 135 us -> 135 us (level)
  no operation moved by 1% of the time
where the time goes in v10:
time: 135 us; the launch traced here: 134 us
  blocking collectives  123 us (91%)
  Pallas kernels  11.1 us (8%)
    all_to_all x4, blocking collectives, per_device(): got = lax.all_to_all(sent, near, 0, 0)  52 us
    all_to_all x2, blocking collectives, per_device(): got = lax.all_to_all(sent, 'z', 0, 0)  41.1 us
    all_to_all x2, blocking collectives, per_device(): shared = lax.all_to_all(shared, 'x', 0, 0)  16 us
    all_to_all x2, blocking collectives, per_device(): got = lax.all_to_all(sent, 'x', 0, 0)  13.5 us
    pallas_call x10, Pallas kernels, call(): pl.pallas_call(body, out_shape=shapes, in_specs=[pl.BlockSpec(memory_spac...  9.18 us

profile of v10, /device:TPU:1, one launch (start us, length us, event | category | flops | bytes accessed | tf_op | source)
XLA Modules:
  0.0 134.4 jit_solution(11336387690676146586)
XLA Ops:
  0.6 1.9 %shard_map.58 = (f32[4,40,128]{2,1,0:T(8,128)S(1)}, f32[2,32,128]{2,1,0:T(8,128)S(1)}, bf16[2,128,1024]{2,1,0:T(8,128)(2,1)S(1)}, f32[32,32]{1,0:T(8,128)S(1)}) custom-call(f32[32,1024]{1,0:T(8,128)} %time_hbm.1, f32[2,32]{1,0:T(2,128)} %bitcast.3, bf16[2,128,1024]{2,1,0:T(8,128)(2,1)} %tensor_hbm.1), custom_call_target="tpu_custom_call" | custom-call | tf_op jit(solution)/shard_map/pallas_call | solution.py:205
  2.5 9.2 %all_to_all.50.shared_ref = f32[4,40,128]{2,1,0:T(8,128)S(1)} all-to-all(f32[4,40,128]{2,1,0:T(8,128)S(1)} %get-tuple-element.29), channel_id=1, replica_groups=mesh['z'=8,'pair'=2,'y'=4,'core'=2,'x'=4] {'x'}, dimensions={0} | all-to-all | bytes 163840 | tf_op jit(solution)/shard_map/all_to_all | solution.py:395
  11.7 1.5 %shard_map.59 = (f32[32,128]{1,0:T(8,128)S(1)}, bf16[16,48,128]{2,1,0:T(8,128)(2,1)S(1)}) custom-call(f32[4,40,128]{2,1,0:T(8,128)S(1)} %all_to_all.50.shared_ref, f32[2,32,128]{2,1,0:T(8,128)S(1)} %get-tuple-element.30.projected_ref, f32[32,32]{1,0:T(8,128)S(1)} %get-tuple-element.31.gram_ref.refs_1_, bf16[2,128,1024]{2,1,0:T(8,128)(2,1)S(1)} %get-tuple-element.32.tensor_ref), custom_call_target="tpu_custom_call" | custom-call | tf_op jit(solution)/shard_map/pallas_call | solution.py:138
  13.3 14.9 %all_to_all.51.got_ref = bf16[16,48,128]{2,1,0:T(8,128)(2,1)S(1)} all-to-all(bf16[16,48,128]{2,1,0:T(8,128)(2,1)S(1)} %get-tuple-element.33), channel_id=1, replica_groups=mesh['z'=8,'pair'=2,'y'=4,'core'=2,'x'=4] {'pair','y','core'}, dimensions={0} | all-to-all | bytes 393216 | tf_op jit(solution)/shard_map/all_to_all | solution.py:398
  28.2 26.0 %all_to_all.52.refs_0_ = bf16[8,48,128]{2,1,0:T(8,128)(2,1)S(1)} all-to-all(bf16[8,48,128]{2,1,0:T(8,128)(2,1)S(1)} %shard_map.60), channel_id=1, replica_groups=mesh['z'=8,'pair'=2,'y'=4,'core'=2,'x'=4] {'z'}, dimensions={0} | all-to-all | bytes 196608 | tf_op jit(solution)/shard_map/all_to_all | solution.py:400
  54.2 1.3 shard_map.61
  55.5 6.8 %all_to_all.53.refs_0_ = f32[4,24,128]{2,1,0:T(8,128)S(1)} all-to-all(f32[4,24,128]{2,1,0:T(8,128)S(1)} %get-tuple-element.35), channel_id=1, replica_groups=mesh['z'=8,'pair'=2,'y'=4,'core'=2,'x'=4] {'x'}, dimensions={0} | all-to-all | bytes 98304 | tf_op jit(solution)/shard_map/all_to_all | solution.py:412
  62.2 0.3 shard_map.62
  62.5 13.1 %all_to_all.54.got_ref = f32[16,16,128]{2,1,0:T(8,128)S(1)} all-to-all(f32[16,16,128]{2,1,0:T(8,128)S(1)} %get-tuple-element.36), channel_id=1, replica_groups=mesh['z'=8,'pair'=2,'y'=4,'core'=2,'x'=4] {'pair','y','core'}, dimensions={0} | all-to-all | bytes 262144 | tf_op jit(solution)/shard_map/all_to_all | solution.py:418
  75.6 2.1 %shard_map.63 = (f32[4,32,128]{2,1,0:T(8,128)S(1)}, f32[2,32,128]{2,1,0:T(8,128)S(1)}, f32[32,32]{1,0:T(8,128)S(1)}, f32[32,32]{1,0:T(8,128)S(1)}) custom-call(f32[16,16,128]{2,1,0:T(8,128)S(1)} %all_to_all.54.got_ref, f32[32,32]{1,0:T(8,128)S(1)} %get-tuple-element.37.neuron_gram_ref, f32[32,32]{1,0:T(8,128)S(1)} %get-tuple-element.38.trial_gram_ref, ...), custom_call_target="tpu_custom_call" | custom-call | tf_op jit(solution)/shard_map/pallas_call | solution.py:138
  77.8 6.8 %all_to_all.55.shared_ref = f32[4,32,128]{2,1,0:T(8,128)S(1)} all-to-all(f32[4,32,128]{2,1,0:T(8,128)S(1)} %get-tuple-element.40), channel_id=1, replica_groups=mesh['z'=8,'pair'=2,'y'=4,'core'=2,'x'=4] {'x'}, dimensions={0} | all-to-all | bytes 131072 | tf_op jit(solution)/shard_map/all_to_all | solution.py:440
  84.6 0.5 shard_map.64
  85.1 10.9 %all_to_all.56.got_ref = bf16[16,48,128]{2,1,0:T(8,128)(2,1)S(1)} all-to-all(bf16[16,48,128]{2,1,0:T(8,128)(2,1)S(1)} %get-tuple-element.43), channel_id=1, replica_groups=mesh['z'=8,'pair'=2,'y'=4,'core'=2,'x'=4] {'pair','y','core'}, dimensions={0} | all-to-all | bytes 393216 | tf_op jit(solution)/shard_map/all_to_all | solution.py:398
  96.0 15.1 %all_to_all.57.refs_0_ = bf16[8,48,128]{2,1,0:T(8,128)(2,1)S(1)} all-to-all(bf16[8,48,128]{2,1,0:T(8,128)(2,1)S(1)} %shard_map.65), channel_id=1, replica_groups=mesh['z'=8,'pair'=2,'y'=4,'core'=2,'x'=4] {'z'}, dimensions={0} | all-to-all | bytes 196608 | tf_op jit(solution)/shard_map/all_to_all | solution.py:400
  111.1 1.3 shard_map.66
  112.5 6.8 %all_to_all.58.refs_0_ = f32[4,24,128]{2,1,0:T(8,128)S(1)} all-to-all(f32[4,24,128]{2,1,0:T(8,128)S(1)} %get-tuple-element.46), channel_id=1, replica_groups=mesh['z'=8,'pair'=2,'y'=4,'core'=2,'x'=4] {'x'}, dimensions={0} | all-to-all | bytes 98304 | tf_op jit(solution)/shard_map/all_to_all | solution.py:412
  119.2 0.3 shard_map.67
  119.5 13.1 %all_to_all.59.got_ref = f32[16,16,128]{2,1,0:T(8,128)S(1)} all-to-all(f32[16,16,128]{2,1,0:T(8,128)S(1)} %get-tuple-element.47), channel_id=1, replica_groups=mesh['z'=8,'pair'=2,'y'=4,'core'=2,'x'=4] {'pair','y','core'}, dimensions={0} | all-to-all | bytes 262144 | tf_op jit(solution)/shard_map/all_to_all | solution.py:418
  132.6 1.8 %shard_map.68 = (f32[32,128]{1,0:T(8,128)}, f32[2,32]{1,0:T(2,128)}, f32[2,32]{1,0:T(2,128)}) custom-call(f32[16,16,128]{2,1,0:T(8,128)S(1)} %all_to_all.59.got_ref, f32[32,32]{1,0:T(8,128)S(1)} %get-tuple-element.48.neuron_gram_ref, f32[32,32]{1,0:T(8,128)S(1)} %get-tuple-element.49.trial_gram_ref, f32[32,128]{1,0:T(8,128)S(1)} %get-tuple-element.50.refs_0_, ...), custom_call_target="tpu_custom_call" | custom-call | tf_op jit(solution)/shard_map/pallas_call | solution.py:138
  (2 shorter events, 0.1 us)

commit v11 on v10

--- a/solution.py
+++ b/solution.py
@@ -13,6 +13,7 @@
 EXACT = lax.Precision.HIGHEST
 PART = 8
 AHEAD = 3
+PIECES = 4
 WIRE = jnp.bfloat16
 
 
@@ -180,17 +181,25 @@
         pltpu.make_async_copy(time_hbm, time_ref, arrived.at[0]),
         pltpu.make_async_copy(trial_hbm, trial_ref, arrived.at[1]),
     ]
+    step = tensor_ref.shape[1] // PIECES
     for trial in range(count):
-        copies.append(
-            pltpu.make_async_copy(tensor_hbm.at[trial], tensor_ref.at[trial], arrived.at[2 + trial])
-        )
+        for piece in range(PIECES):
+            rows = pl.ds(piece * step, step)
+            copies.append(
+                pltpu.make_async_copy(
+                    tensor_hbm.at[trial, rows],
+                    tensor_ref.at[trial, rows],
+                    arrived.at[2 + trial * PIECES + piece],
+                )
+            )
     for copy in copies:
         copy.start()
     copies[0].wait()
     gram_ref[...] = gram_of(time_ref[...])
 
     def tensor_of(trial):
-        copies[2 + trial].wait()
+        for copy in copies[2 + trial * PIECES : 2 + (trial + 1) * PIECES]:
+            copy.wait()
         return tensor_ref[trial]
 
     copies[1].wait()
@@ -210,7 +219,7 @@
         scratch_shapes=[
             pltpu.VMEM(time_init.shape, time_init.dtype),
             pltpu.VMEM(trial_rows.shape, trial_rows.dtype),
-            pltpu.SemaphoreType.DMA((2 + tensor.shape[0],)),
+            pltpu.SemaphoreType.DMA((2 + tensor.shape[0] * PIECES,)),
         ],
     )(time_init, trial_rows, tensor)
 
@@ -302,18 +311,21 @@
         sent_ref[member, half:, :] = tile
 
 
-def sum_body(own_trials, got_ref, sent_ref, trial_gram_ref):
+def sum_body(own_trials, got_ref, sent_ref, trial_rows_ref):
     _, half, lanes = sent_ref.shape
     total = got_ref[0, :half, :]
     for member in range(1, got_ref.shape[0]):
         total = total + got_ref[member, :half, :]
     for member in range(sent_ref.shape[0]):
         sent_ref[member] = total
-    trial_gram_ref[...] = gram_of(trial_of(got_ref, half, own_trials, 2 * half))
-
-
-def time_of(got_ref, left_ref, right_ref):
-    inverse = damped_inverse(left_ref[...] * right_ref[...])
+    for member in range(got_ref.shape[0]):
+        trial_rows_ref[member * own_trials : (member + 1) * own_trials, :] = got_ref[
+            member, half : half + own_trials, : 2 * half
+        ]
+
+
+def time_of(got_ref, neuron_gram_ref, trial_gram):
+    inverse = damped_inverse(neuron_gram_ref[...] * trial_gram)
     members, half, lanes = got_ref.shape
     low = lax.broadcasted_iota(jnp.int32, (half, lanes), 1) < lanes // 2
     pieces = []
@@ -325,9 +337,10 @@
     return product(inverse, jnp.concatenate(pieces, axis=1))
 
 
-def next_body(got_ref, neuron_gram_ref, trial_gram_ref, own_ref, tensor_ref, *outs):
+def next_body(got_ref, neuron_gram_ref, trial_rows_ref, own_ref, tensor_ref, *outs):
     sent_ref, projected_ref, gram_ref, inverse_ref = outs
-    raw = time_of(got_ref, neuron_gram_ref, trial_gram_ref)
+    trial_gram = gram_of(rows_product(eye_of(trial_rows_ref.shape[1]), trial_rows_ref[...]))
+    raw = time_of(got_ref, neuron_gram_ref, trial_gram)
     raw_gram = gram_of(raw)
     diagonal = raw_gram * eye_of(raw.shape[0])
     count = raw.shape[1]
@@ -337,14 +350,15 @@
     put_projected(raw * down, own_ref[...], tensor_of, projected_ref, sent_ref)
     gram = down * raw_gram * across
     gram_ref[...] = gram
-    inverse_ref[...] = damped_inverse(gram * trial_gram_ref[...])
-
-
-def last_body(got_ref, neuron_gram_ref, trial_gram_ref, *refs):
+    inverse_ref[...] = damped_inverse(gram * trial_gram)
+
+
+def last_body(got_ref, neuron_gram_ref, trial_rows_ref, *refs):
     held_neuron_ref, held_own_ref, neuron_ref, time_ref, own_ref = refs
     neuron_ref[...] = held_neuron_ref[...]
     own_ref[...] = held_own_ref[...]
-    raw = time_of(got_ref, neuron_gram_ref, trial_gram_ref)
+    trial_gram = gram_of(rows_product(eye_of(trial_rows_ref.shape[1]), trial_rows_ref[...]))
+    raw = time_of(got_ref, neuron_gram_ref, trial_gram)
     mean = jnp.sum(raw * raw, axis=1, keepdims=True) / raw.shape[1]
     down = 1.0 / jnp.sqrt(mean + tiny_eps)
     count, size = time_ref.shape
@@ -410,9 +424,12 @@
             raw,
         )
         got = lax.all_to_all(sent, "x", 0, 0)
-        sent, trial_gram = call(
+        sent, trial_rows = call(
             lambda *refs: sum_body(own_trials, *refs),
-            (shape(twins * blocks, components // 2, lanes), square),
+            (
+                shape(twins * blocks, components // 2, lanes),
+                shape(planes * own_trials, components),
+            ),
             got,
         )
         got = lax.all_to_all(sent, near, 0, 0)
@@ -423,7 +440,7 @@
                 (neuron_shape, shape(share_width, components), own_shape),
                 got,
                 neuron_gram,
-                trial_gram,
+                trial_rows,
                 *rest,
                 slow=(0, 1, 2),
             )
@@ -433,7 +450,7 @@
             (shape(planes, components, own_neurons), projected_shape, square, square),
             got,
             neuron_gram,
-            trial_gram,
+            trial_rows,
             *rest,
             tensor,
         )

time: 135 us -> 135 us (level)
  no operation moved by 1% of the time
where the time goes in v11:
time: 135 us
  blocking collectives  123 us (91%)
  Pallas kernels  11.2 us (8%)
    all_to_all x4, blocking collectives, per_device(): got = lax.all_to_all(sent, near, 0, 0)  51.9 us
    all_to_all x2, blocking collectives, per_device(): got = lax.all_to_all(sent, 'z', 0, 0)  41.1 us
    all_to_all x2, blocking collectives, per_device(): shared = lax.all_to_all(shared, 'x', 0, 0)  16 us
    all_to_all x2, blocking collectives, per_device(): got = lax.all_to_all(sent, 'x', 0, 0)  13.5 us
    pallas_call x10, Pallas kernels, call(): pl.pallas_call(body, out_shape=shapes, in_specs=[pl.BlockSpec(memory_spac...  9.27 us

profile of v11, /device:TPU:1, one launch (start us, length us, event | category | flops | bytes accessed | tf_op | source)
XLA Modules:
  0.0 134.5 jit_solution(13109450760736342140)
XLA Ops:
  0.6 2.0 %shard_map.58 = (f32[4,40,128]{2,1,0:T(8,128)S(1)}, f32[2,32,128]{2,1,0:T(8,128)S(1)}, bf16[2,128,1024]{2,1,0:T(8,128)(2,1)S(1)}, f32[32,32]{1,0:T(8,128)S(1)}) custom-call(f32[32,1024]{1,0:T(8,128)} %time_hbm.1, f32[2,32]{1,0:T(2,128)} %bitcast.3, bf16[2,128,1024]{2,1,0:T(8,128)(2,1)} %tensor_hbm.1), custom_call_target="tpu_custom_call" | custom-call | tf_op jit(solution)/shard_map/pallas_call | solution.py:214
  2.6 9.2 %all_to_all.50.shared_ref = f32[4,40,128]{2,1,0:T(8,128)S(1)} all-to-all(f32[4,40,128]{2,1,0:T(8,128)S(1)} %get-tuple-element.29), channel_id=1, replica_groups=mesh['z'=8,'pair'=2,'y'=4,'core'=2,'x'=4] {'x'}, dimensions={0} | all-to-all | bytes 163840 | tf_op jit(solution)/shard_map/all_to_all | solution.py:409
  11.8 1.5 %shard_map.59 = (f32[32,128]{1,0:T(8,128)S(1)}, bf16[16,48,128]{2,1,0:T(8,128)(2,1)S(1)}) custom-call(f32[4,40,128]{2,1,0:T(8,128)S(1)} %all_to_all.50.shared_ref, f32[2,32,128]{2,1,0:T(8,128)S(1)} %get-tuple-element.30.projected_ref, f32[32,32]{1,0:T(8,128)S(1)} %get-tuple-element.31.gram_ref.refs_1_, bf16[2,128,1024]{2,1,0:T(8,128)(2,1)S(1)} %get-tuple-element.32.tensor_ref), custom_call_target="tpu_custom_call" | custom-call | tf_op jit(solution)/shard_map/pallas_call | solution.py:139
  13.3 14.9 %all_to_all.51.got_ref = bf16[16,48,128]{2,1,0:T(8,128)(2,1)S(1)} all-to-all(bf16[16,48,128]{2,1,0:T(8,128)(2,1)S(1)} %get-tuple-element.33), channel_id=1, replica_groups=mesh['z'=8,'pair'=2,'y'=4,'core'=2,'x'=4] {'pair','y','core'}, dimensions={0} | all-to-all | bytes 393216 | tf_op jit(solution)/shard_map/all_to_all | solution.py:412
  28.2 26.0 %all_to_all.52.refs_0_ = bf16[8,48,128]{2,1,0:T(8,128)(2,1)S(1)} all-to-all(bf16[8,48,128]{2,1,0:T(8,128)(2,1)S(1)} %shard_map.60), channel_id=1, replica_groups=mesh['z'=8,'pair'=2,'y'=4,'core'=2,'x'=4] {'z'}, dimensions={0} | all-to-all | bytes 196608 | tf_op jit(solution)/shard_map/all_to_all | solution.py:414
  54.2 1.3 shard_map.61
  55.5 6.8 %all_to_all.53.refs_0_ = f32[4,24,128]{2,1,0:T(8,128)S(1)} all-to-all(f32[4,24,128]{2,1,0:T(8,128)S(1)} %get-tuple-element.35), channel_id=1, replica_groups=mesh['z'=8,'pair'=2,'y'=4,'core'=2,'x'=4] {'x'}, dimensions={0} | all-to-all | bytes 98304 | tf_op jit(solution)/shard_map/all_to_all | solution.py:426
  62.3 13.1 %all_to_all.54.got_ref = f32[16,16,128]{2,1,0:T(8,128)S(1)} all-to-all(f32[16,16,128]{2,1,0:T(8,128)S(1)} %get-tuple-element.36), channel_id=1, replica_groups=mesh['z'=8,'pair'=2,'y'=4,'core'=2,'x'=4] {'pair','y','core'}, dimensions={0} | all-to-all | bytes 262144 | tf_op jit(solution)/shard_map/all_to_all | solution.py:435
  75.4 2.5 %shard_map.63 = (f32[4,32,128]{2,1,0:T(8,128)S(1)}, f32[2,32,128]{2,1,0:T(8,128)S(1)}, f32[32,32]{1,0:T(8,128)S(1)}, f32[32,32]{1,0:T(8,128)S(1)}) custom-call(f32[16,16,128]{2,1,0:T(8,128)S(1)} %all_to_all.54.got_ref, f32[32,32]{1,0:T(8,128)S(1)} %get-tuple-element.37.neuron_gram_ref, f32[8,32]{1,0:T(8,128)S(1)} %get-tuple-element.38.trial_rows_ref, ...), custom_call_target="tpu_custom_call" | custom-call | tf_op jit(solution)/shard_map/pallas_call | solution.py:139
  77.8 6.8 %all_to_all.55.shared_ref = f32[4,32,128]{2,1,0:T(8,128)S(1)} all-to-all(f32[4,32,128]{2,1,0:T(8,128)S(1)} %get-tuple-element.40), channel_id=1, replica_groups=mesh['z'=8,'pair'=2,'y'=4,'core'=2,'x'=4] {'x'}, dimensions={0} | all-to-all | bytes 131072 | tf_op jit(solution)/shard_map/all_to_all | solution.py:457
  84.7 0.5 shard_map.64
  85.1 10.9 %all_to_all.56.got_ref = bf16[16,48,128]{2,1,0:T(8,128)(2,1)S(1)} all-to-all(bf16[16,48,128]{2,1,0:T(8,128)(2,1)S(1)} %get-tuple-element.43), channel_id=1, replica_groups=mesh['z'=8,'pair'=2,'y'=4,'core'=2,'x'=4] {'pair','y','core'}, dimensions={0} | all-to-all | bytes 393216 | tf_op jit(solution)/shard_map/all_to_all | solution.py:412
  96.1 15.1 %all_to_all.57.refs_0_ = bf16[8,48,128]{2,1,0:T(8,128)(2,1)S(1)} all-to-all(bf16[8,48,128]{2,1,0:T(8,128)(2,1)S(1)} %shard_map.65), channel_id=1, replica_groups=mesh['z'=8,'pair'=2,'y'=4,'core'=2,'x'=4] {'z'}, dimensions={0} | all-to-all | bytes 196608 | tf_op jit(solution)/shard_map/all_to_all | solution.py:414
  111.2 1.3 shard_map.66
  112.5 6.8 %all_to_all.58.refs_0_ = f32[4,24,128]{2,1,0:T(8,128)S(1)} all-to-all(f32[4,24,128]{2,1,0:T(8,128)S(1)} %get-tuple-element.46), channel_id=1, replica_groups=mesh['z'=8,'pair'=2,'y'=4,'core'=2,'x'=4] {'x'}, dimensions={0} | all-to-all | bytes 98304 | tf_op jit(solution)/shard_map/all_to_all | solution.py:426
  119.3 13.1 %all_to_all.59.got_ref = f32[16,16,128]{2,1,0:T(8,128)S(1)} all-to-all(f32[16,16,128]{2,1,0:T(8,128)S(1)} %get-tuple-element.47), channel_id=1, replica_groups=mesh['z'=8,'pair'=2,'y'=4,'core'=2,'x'=4] {'pair','y','core'}, dimensions={0} | all-to-all | bytes 262144 | tf_op jit(solution)/shard_map/all_to_all | solution.py:435
  132.4 2.2 %shard_map.68 = (f32[32,128]{1,0:T(8,128)}, f32[2,32]{1,0:T(2,128)}, f32[2,32]{1,0:T(2,128)}) custom-call(f32[16,16,128]{2,1,0:T(8,128)S(1)} %all_to_all.59.got_ref, f32[32,32]{1,0:T(8,128)S(1)} %get-tuple-element.48.neuron_gram_ref, f32[8,32]{1,0:T(8,128)S(1)} %get-tuple-element.49.trial_rows_ref, f32[32,128]{1,0:T(8,128)S(1)} %get-tuple-element.50.refs_0_, ...), custom_call_target="tpu_custom_call" | custom-call | tf_op jit(solution)/shard_map/pallas_call | solution.py:139
  (4 shorter events, 0.1 us)
